TPU v7x, 32 devices: a whole 2x2x4 slice. The times are simulated.
32 devices in a mesh: gx: 8 (over y, x, core), gy: 4 (over z).
Axes of the slice: x: 2, y: 2, z: 4, core: 2. Of those that a mesh axis runs over, the one named last changes fastest.
Arguments:
- initial_thermal_state: float32 [64, 32, 16, 256], P('gx', 'gy'), may hold values from -4 to 4
- logarithmic_diffusivity: float32 [64, 32, 16, 256], P('gx', 'gy'), may hold values from -2 to 2
- rock_class_code: int32 [64, 32, 16], P('gx', 'gy'), may hold values from 0 to 7
- rock_class_diffusivity: float32 [8], replicated, may hold values from 0.004 to 0.016
- advection_courant: float32 [16], replicated, may hold values from 0 to 0.25
- probe_locations: int32 [1024], P(('gx', 'gy')), may hold values from 0 to 1023
- observed_readings: float32 [1024], P(('gx', 'gy')), may hold values from -4 to 4
- probe_noise_deviation: float32 [1024], P(('gx', 'gy')), may hold values from 0.1 to 1
- random_starters: int32 [256], replicated, may hold values from 0 to 65520
Outputs:
- temperature_final: float32 [64, 32, 16, 256], P('gx', 'gy')
- cond_updated: float32 [64, 32, 16, 256], P('gx', 'gy')
Inputs may be any that keep to these rules, and one draw needn't show every extreme that they name: probe_locations[j] is a cell (x' 8 + y') * 16 + z of the tile of device j // 32, devices ordered with gy fastest.
All inputs are finite; a program needn't handle non-finite values.
Results may differ from a plain program's by a relative error of at most 0.00017.
Values sent between devices are 32-bit elements; how exact they have to be, the bound alone decides.
No kernel may reach another device: no remote copies, remote signals or barrier semaphores. Data moves between devices by JAX's collectives and lax.ppermute only.
A program may use at most 64 MiB of HBM per device.

v0:
```python
import jax
import jax.numpy as jnp
from jax import lax
from jax.sharding import PartitionSpec as P

inflation = 4.0


def with_halo(cells, sides, width):
    for axis, dim in sides:
        count = lax.axis_size(axis)
        ends = count - 1
        head = lax.slice_in_dim(cells, 0, width, axis=dim)
        tail = lax.slice_in_dim(cells, cells.shape[dim] - width, cells.shape[dim], axis=dim)
        cells = jnp.concatenate(
            [
                lax.ppermute(tail, axis, [(i, (i + 1) % count) for i in range(ends)]),
                cells,
                lax.ppermute(head, axis, [((i + 1) % count, i) for i in range(ends)]),
            ],
            axis=dim,
        )
    return cells


def window(field, shift_x, shift_y, shift_z):
    return field[
        1 + shift_x : field.shape[0] - 1 + shift_x,
        1 + shift_y : field.shape[1] - 1 + shift_y,
        1 + shift_z : field.shape[2] - 1 + shift_z,
    ]


def advance_in_time(padded_temp, padded_diffusivity, advection_courant):
    temp_z = jnp.pad(padded_temp, ((0, 0), (0, 0), (1, 1), (0, 0)))
    cond_z = jnp.pad(padded_diffusivity, ((0, 0), (0, 0), (1, 1), (0, 0)))
    center = window(temp_z, 0, 0, 0)
    cond_center = window(cond_z, 0, 0, 0)
    change = jnp.zeros_like(center)
    for shift_x, shift_y, shift_z in (
        (1, 0, 0),
        (-1, 0, 0),
        (0, 1, 0),
        (0, -1, 0),
        (0, 0, 1),
        (0, 0, -1),
    ):
        change = change + 0.5 * (cond_center + window(cond_z, shift_x, shift_y, shift_z)) * (
            window(temp_z, shift_x, shift_y, shift_z) - center
        )
    upwind = center - window(temp_z, -1, 0, 0)
    return center + change - advection_courant[:, None] * upwind


def perturbation(obs_index, random_starters):
    first = random_starters * 7919 % 65521
    second = obs_index * 331 % 65521
    hashed = (first[None, :] * (second[:, None] % 32749) + first[None, :] + second[:, None]) % 65521
    uniform_value = (hashed.astype(jnp.float32) + 0.5) / 65521.0
    return jnp.sqrt(3.0) * (2.0 * uniform_value - 1.0)


def shards(
    initial_thermal_state,
    logarithmic_diffusivity,
    rock_class_code,
    rock_class_diffusivity,
    advection_courant,
    probe_locations,
    observed_readings,
    probe_noise_deviation,
    random_starters,
):
    tile_span_east, tile_span_north, stratum_indices, ensemble_roster = initial_thermal_state.shape
    levels = jnp.arange(rock_class_diffusivity.shape[0], dtype=jnp.int32)
    base_cond = jnp.sum(
        (rock_class_code[..., None] == levels).astype(jnp.float32) * rock_class_diffusivity, axis=-1
    )
    thermal_spreading_step = base_cond[..., None] * jnp.exp(logarithmic_diffusivity)
    ensemble_matrix = jnp.stack([initial_thermal_state, thermal_spreading_step])
    extended = with_halo(ensemble_matrix, (("gx", 1), ("gy", 2)), 1)
    interior_slice = advance_in_time(extended[0], extended[1], advection_courant)
    padded_middle = with_halo(interior_slice, (("gx", 0), ("gy", 1)), 1)
    final = advance_in_time(padded_middle, extended[1], advection_courant)
    flattened = final.reshape(-1, ensemble_roster)
    predicted = jnp.take(flattened, probe_locations, axis=0)
    scale = jnp.sqrt(jnp.float32(ensemble_roster - 1))
    spread = (predicted - jnp.mean(predicted, axis=1, keepdims=True)) / (
        probe_noise_deviation[:, None] * scale
    )
    obs_count = probe_locations.shape[0]
    obs_index = lax.axis_index(("gx", "gy")) * obs_count + jnp.arange(obs_count, dtype=jnp.int32)
    noise = perturbation(obs_index, random_starters)
    misfit = (
        observed_readings[:, None]
        + jnp.sqrt(inflation) * probe_noise_deviation[:, None] * noise
        - predicted
    ) / probe_noise_deviation[:, None]
    local_gram = jnp.dot(spread.T, spread, precision=lax.Precision.HIGHEST)
    local_cross = jnp.dot(spread.T, misfit, precision=lax.Precision.HIGHEST)
    gram, cross = lax.psum((local_gram, local_cross), ("gx", "gy"))
    system = gram + inflation * jnp.eye(ensemble_roster, dtype=jnp.float32)
    lower_factor = jnp.linalg.cholesky(system)
    halfway = lax.linalg.triangular_solve(lower_factor, cross, left_side=True, lower=True)
    weights = lax.linalg.triangular_solve(
        lower_factor, halfway, left_side=True, lower=True, transpose_a=True
    )
    anomalies = (
        (logarithmic_diffusivity - jnp.mean(logarithmic_diffusivity, axis=-1, keepdims=True))
        / scale
    ).reshape(-1, ensemble_roster)
    updated = logarithmic_diffusivity.reshape(-1, ensemble_roster) + jnp.dot(
        anomalies, weights, precision=lax.Precision.HIGHEST
    )
    return (final, updated.reshape(logarithmic_diffusivity.shape))


def solution(mesh):
    placed = (
        P("gx", "gy", None, None),
        P("gx", "gy", None, None),
        P("gx", "gy", None),
        P(),
        P(),
        P(("gx", "gy")),
        P(("gx", "gy")),
        P(("gx", "gy")),
        P(),
    )
    return jax.shard_map(
        shards,
        mesh=mesh,
        in_specs=placed,
        out_specs=(P("gx", "gy", None, None), P("gx", "gy", None, None)),
        check_vma=False,
    )
```

profile of v0, /device:TPU:0, one launch (start us, length us, event | category | flops | bytes accessed | tf_op | source)
XLA Modules:
  0.0 271.9 jit_solution(12888231429412441590)
XLA Ops:
  7.2 1.5 reduce_sum.28
  9.7 1.6 subtract_multiply_fusion
  11.4 2.4 collective-permute-start
  13.7 1.3 collective-permute-start.1
  15.1 4.2 %collective-permute-done.1 = f32[2,1,8,16,256]{4,3,2,1,0:T(8,128)S(1)} collective-permute-done((f32[2,1,8,16,256]{4,3,2,1,0:T(8,128)S(1)}, f32[2,1,8,16,256]{4,3,2,1,0:T(8,128)S(1)}, u32[]{:S(2)}, u32[]{:S(2)}) %collective-permute-start.1) | collective-permute-done | bytes 262176 | tf_op jit(solution)/shard_map/ppermute | solution.py:19
  20.8 4.2 %collective-permute-start.2 = (f32[2,10,1,16,256]{4,3,2,1,0:T(8,128)}, f32[2,10,1,16,256]{4,3,2,1,0:T(8,128)}, u32[]{:S(2)}, u32[]{:S(2)}) collective-permute-start(f32[2,10,1,16,256]{4,3,2,1,0:T(8,128)} %get-tuple-element.32), channel_id=1, source_target_pairs={{0,1},{1,2},{2,3},{4,5},{5,6},{6,7},{8,9},{9,10},{10,11},{12,13},{... | collective-permute-start | bytes 983048 | tf_op jit(solution)/shard_map/ppermute | solution.py:17
  25.0 1.3 collective-permute-start.3
  26.4 2.8 %collective-permute-done.2 = f32[2,10,1,16,256]{4,3,2,1,0:T(8,128)} collective-permute-done((f32[2,10,1,16,256]{4,3,2,1,0:T(8,128)}, f32[2,10,1,16,256]{4,3,2,1,0:T(8,128)}, u32[]{:S(2)}, u32[]{:S(2)}) %collective-permute-start.2) | collective-permute-done | bytes 327712 | tf_op jit(solution)/shard_map/ppermute | solution.py:17
  29.2 5.1 %collective-permute-done.3 = f32[2,10,1,16,256]{4,3,2,1,0:T(8,128)} collective-permute-done((f32[2,10,1,16,256]{4,3,2,1,0:T(8,128)}, f32[2,10,1,16,256]{4,3,2,1,0:T(8,128)}, u32[]{:S(2)}, u32[]{:S(2)}) %collective-permute-start.3) | collective-permute-done | bytes 327712 | tf_op jit(solution)/shard_map/ppermute | solution.py:19
  34.3 1.6 pad_maximum_fusion
  36.6 1.9 fusion.10
  38.5 1.3 collective-permute-start.4
  39.8 5.9 %collective-permute-start.5 = (f32[1,8,16,256]{3,2,1,0:T(8,128)S(1)}, f32[1,8,16,256]{3,2,1,0:T(8,128)S(1)}, u32[]{:S(2)}, u32[]{:S(2)}) collective-permute-start(f32[1,8,16,256]{3,2,1,0:T(8,128)S(1)} %get-tuple-element.40), channel_id=1, source_target_pairs={{0,4},{4,8},{8,12},{12,16},{16,20},{20,24},{24,28},{1,5},{5,9},{9,... | collective-permute-start | bytes 393224 | tf_op jit(solution)/shard_map/ppermute | solution.py:17
  45.8 0.9 collective-permute-done.5
  46.8 1.3 collective-permute-start.6
  48.1 4.6 %collective-permute-start.7 = (f32[10,1,16,256]{3,2,1,0:T(8,128)S(1)}, f32[10,1,16,256]{3,2,1,0:T(8,128)S(1)}, u32[]{:S(2)}, u32[]{:S(2)}) collective-permute-start(f32[10,1,16,256]{3,2,1,0:T(8,128)S(1)} %get-tuple-element.36), channel_id=1, source_target_pairs={{0,1},{1,2},{2,3},{4,5},{5,6},{6,7},{8,9},{9,10},{10,11},{12,13},{... | collective-permute-start | bytes 491528 | tf_op jit(solution)/shard_map/ppermute | solution.py:17
  52.7 1.3 collective-permute-done.6
  54.0 1.5 collective-permute-done.7
  55.9 2.1 fusion.16
  58.9 1.2 fusion.71
  60.1 1.2 fusion.64
  61.3 137.1 %all-reduce.7.cloned.1.call-done = (f32[256,256]{1,0:T(8,128)}, f32[256,256]{0,1:T(8,128)}) async-done(((f32[256,256]{1,0:T(8,128)}, f32[256,256]{0,1:T(8,128)}), (f32[256,256]{1,0:T(8,128)}, f32[256,256]{0,1:T(8,128)})) %all-reduce.7.cloned.1.call-update) | async-done | bytes 524304 | tf_op jit(solution)/shard_map/psum | solution.py:101
  198.4 1.0 select_add_fusion
  199.5 1.0 fusion.45
  200.6 11.7 %cholesky.49 = f32[128,128]{1,0:T(8,128)S(1)} custom-call(f32[128,128]{1,0:T(8,128)S(1)} %cholesky.115), custom_call_target="Cholesky" | custom-call | tf_op jit(solution)/shard_map/jit(cholesky)/cholesky | solution.py:103
  212.3 9.8 %custom-call.16 = f32[1,128,128]{1,2,0:T(8,128)S(1)} custom-call(f32[1,128,128]{2,1,0:T(8,128)S(1)} %get-tuple-element.43), custom_call_target="InvertDiagBlocksLowerTriangular" | custom-call | tf_op jit(solution)/shard_map/jit(cholesky)/cholesky | solution.py:103
  222.6 11.7 %cholesky.103 = f32[128,128]{1,0:T(8,128)S(1)} custom-call(f32[128,128]{1,0:T(8,128)S(1)} %convolution_subtract_fusion.2), custom_call_target="Cholesky" | custom-call | tf_op jit(solution)/shard_map/jit(cholesky)/cholesky | solution.py:103
  237.3 4.1 %while.1 = (s32[]{:T(128)}, f32[256,256]{0,1:T(8,128)S(1)}, s32[2,2]{1,0:T(2,128)S(1)}, f32[2,128,128]{2,1,0:T(8,128)S(1)}, s32[]{:T(128)}) while((s32[]{:T(128)}, f32[256,256]{0,1:T(8,128)S(1)}, s32[2,2]{1,0:T(2,128)S(1)}, f32[2,128,128]{2,1,0:T(8,128)S(1)}, s32[]{:T(128)}) %tuple.34), condition=%wide.while_cond, body=%wide.while_body.sunk | while | flops 2 | bytes 393321 | solution.py:105
  237.9 1.3 dynamic-slice.7
  240.0 1.3 dynamic-slice.7
  241.4 19.9 %custom-call.17 = f32[2,128,128]{1,2,0:T(8,128)S(1)} custom-call(f32[2,128,128]{2,1,0:T(8,128)S(1)} %get-tuple-element.9), custom_call_target="InvertDiagBlocksLowerTriangular" | custom-call | tf_op jit(solution)/shard_map/triangular_solve | solution.py:105
  263.1 2.0 convolution_add_fusion
  (73 shorter events, 10.1 us)
Async XLA Ops:
  7.2 4.1 %copy-start = (f32[8,8,16,256]{3,2,1,0:T(8,128)S(1)}, f32[8,8,16,256]{3,2,1,0:T(8,128)}, u32[]{:S(2)}) copy-start(f32[8,8,16,256]{3,2,1,0:T(8,128)} %param.9) | copy-start | bytes 3145732
  7.2 191.2 %all-reduce.7.cloned.1.call-start = ((), (), s32[]{:S(2)}) async-start(), calls=%async_computation | async-start | bytes 1048576 | tf_op jit(solution)/shard_map/psum | solution.py:101
  9.7 5.4 %copy-start.8 = (f32[32]{0:T(128)S(1)}, f32[32]{0:T(128)}, u32[]{:S(2)}) copy-start(f32[32]{0:T(128)} %param.16) | copy-start | bytes 388
  11.3 15.1 %copy-start.7 = (s32[32]{0:T(128)S(1)}, s32[32]{0:T(128)}, u32[]{:S(2)}) copy-start(s32[32]{0:T(128)} %param.14) | copy-start | bytes 388
  11.3 15.1 %copy-start.6 = (s32[256]{0:T(256)S(1)}, s32[256]{0:T(256)}, u32[]{:S(2)}) copy-start(s32[256]{0:T(256)} %param.17) | copy-start | bytes 3076
  11.4 3.7 %collective-permute-start = (f32[2,1,8,16,256]{4,3,2,1,0:T(8,128)S(1)}, f32[2,1,8,16,256]{4,3,2,1,0:T(8,128)S(1)}, u32[]{:S(2)}, u32[]{:S(2)}) collective-permute-start(f32[2,1,8,16,256]{4,3,2,1,0:T(8,128)S(1)} %get-tuple-element.34), channel_id=1, source_target_pairs={{0,4},{4,8},{8,12},{12,16},{16,20},{20,24},{24,28},{1,5},{5,9},{9,... | collective-permute-start | bytes 786440 | tf_op jit(solution)/shard_map/ppermute | solution.py:17
  13.7 5.5 %collective-permute-start.1 = (f32[2,1,8,16,256]{4,3,2,1,0:T(8,128)S(1)}, f32[2,1,8,16,256]{4,3,2,1,0:T(8,128)S(1)}, u32[]{:S(2)}, u32[]{:S(2)}) collective-permute-start(f32[2,1,8,16,256]{4,3,2,1,0:T(8,128)S(1)} %get-tuple-element.35), channel_id=1, source_target_pairs={{4,0},{8,4},{12,8},{16,12},{20,16},{24,20},{28,24},{5,1},{9,5},{13... | collective-permute-start | bytes 786440 | tf_op jit(solution)/shard_map/ppermute | solution.py:19
  19.3 0.7 copy-start.3
  20.8 8.4 %collective-permute-start.2 = (f32[2,10,1,16,256]{4,3,2,1,0:T(8,128)}, f32[2,10,1,16,256]{4,3,2,1,0:T(8,128)}, u32[]{:S(2)}, u32[]{:S(2)}) collective-permute-start(f32[2,10,1,16,256]{4,3,2,1,0:T(8,128)} %get-tuple-element.32), channel_id=1, source_target_pairs={{0,1},{1,2},{2,3},{4,5},{5,6},{6,7},{8,9},{9,10},{10,11},{12,13},{... | collective-permute-start | bytes 983048 | tf_op jit(solution)/shard_map/ppermute | solution.py:17
  25.0 9.3 %collective-permute-start.3 = (f32[2,10,1,16,256]{4,3,2,1,0:T(8,128)}, f32[2,10,1,16,256]{4,3,2,1,0:T(8,128)}, u32[]{:S(2)}, u32[]{:S(2)}) collective-permute-start(f32[2,10,1,16,256]{4,3,2,1,0:T(8,128)} %get-tuple-element.33), channel_id=1, source_target_pairs={{1,0},{2,1},{3,2},{5,4},{6,5},{7,6},{9,8},{10,9},{11,10},{13,12},{... | collective-permute-start | bytes 983048 | tf_op jit(solution)/shard_map/ppermute | solution.py:19
  36.0 0.7 copy-start.5
  38.5 7.3 %collective-permute-start.4 = (f32[1,8,16,256]{3,2,1,0:T(8,128)S(1)}, f32[1,8,16,256]{3,2,1,0:T(8,128)S(1)}, u32[]{:S(2)}, u32[]{:S(2)}) collective-permute-start(f32[1,8,16,256]{3,2,1,0:T(8,128)S(1)} %get-tuple-element.41), channel_id=1, source_target_pairs={{4,0},{8,4},{12,8},{16,12},{20,16},{24,20},{28,24},{5,1},{9,5},{13... | collective-permute-start | bytes 393224 | tf_op jit(solution)/shard_map/ppermute | solution.py:19
  39.8 6.9 %collective-permute-start.5 = (f32[1,8,16,256]{3,2,1,0:T(8,128)S(1)}, f32[1,8,16,256]{3,2,1,0:T(8,128)S(1)}, u32[]{:S(2)}, u32[]{:S(2)}) collective-permute-start(f32[1,8,16,256]{3,2,1,0:T(8,128)S(1)} %get-tuple-element.40), channel_id=1, source_target_pairs={{0,4},{4,8},{8,12},{12,16},{16,20},{20,24},{24,28},{1,5},{5,9},{9,... | collective-permute-start | bytes 393224 | tf_op jit(solution)/shard_map/ppermute | solution.py:17
  46.8 7.2 %collective-permute-start.6 = (f32[10,1,16,256]{3,2,1,0:T(8,128)S(1)}, f32[10,1,16,256]{3,2,1,0:T(8,128)S(1)}, u32[]{:S(2)}, u32[]{:S(2)}) collective-permute-start(f32[10,1,16,256]{3,2,1,0:T(8,128)S(1)} %get-tuple-element.37), channel_id=1, source_target_pairs={{1,0},{2,1},{3,2},{5,4},{6,5},{7,6},{9,8},{10,9},{11,10},{13,12},{... | collective-permute-start | bytes 491528 | tf_op jit(solution)/shard_map/ppermute | solution.py:19
  48.1 7.4 %collective-permute-start.7 = (f32[10,1,16,256]{3,2,1,0:T(8,128)S(1)}, f32[10,1,16,256]{3,2,1,0:T(8,128)S(1)}, u32[]{:S(2)}, u32[]{:S(2)}) collective-permute-start(f32[10,1,16,256]{3,2,1,0:T(8,128)S(1)} %get-tuple-element.36), channel_id=1, source_target_pairs={{0,1},{1,2},{2,3},{4,5},{5,6},{6,7},{8,9},{9,10},{10,11},{12,13},{... | collective-permute-start | bytes 491528 | tf_op jit(solution)/shard_map/ppermute | solution.py:17
  55.9 4.2 %copy-start.9 = (f32[32]{0:T(128)S(1)}, f32[32]{0:T(128)}, u32[]{:S(2)}) copy-start(f32[32]{0:T(128)} %param.15) | copy-start | bytes 388
  58.1 177.9 %copy-start.2 = (f32[8,8,16,256]{3,2,1,0:T(8,128)}, f32[8,8,16,256]{3,2,1,0:T(8,128)S(1)}, u32[]{:S(2)}) copy-start(f32[8,8,16,256]{3,2,1,0:T(8,128)S(1)} %fusion.16) | copy-start | bytes 3145732
  199.5 61.8 %copy-start.4 = (f32[256,256]{1,0:T(8,128)S(1)}, f32[256,256]{1,0:T(8,128)}, u32[]{:S(2)}) copy-start(f32[256,256]{1,0:T(8,128)} %get-tuple-element.26) | copy-start | bytes 786436
  237.2 25.9 %copy-start.1 = (f32[8,8,16,256]{3,2,1,0:T(8,128)S(1)}, f32[8,8,16,256]{3,2,1,0:T(8,128)}, u32[]{:S(2)}) copy-start(f32[8,8,16,256]{3,2,1,0:T(8,128)} %param.10) | copy-start | bytes 3145732
Sparse Core Ops, SparseCore 0:
  61.4 136.9 all-reduce.6
where the time goes:
time: 272 us
  waiting for transfers between devices  153 us (56%)
  other arithmetic  67.8 us (25%)
  starting transfers between devices  22.3 us (8%)
  between operations  15.7 us (6%)
  local copies, waits for them, and re-layouts  6.53 us (2%)
  matrix products  6.52 us (2%)
    psum x1, waiting for transfers between devices, shards(): gram, cross = lax.psum((local_gram, local_cross), ('gx', 'gy'))  137 us
    another operation x7, other arithmetic, shards(): lower_factor = jnp.linalg.cholesky(system)  34.6 us
    another operation x3, other arithmetic, shards(): lax.linalg.triangular_solve(lower_factor, halfway, left_side=True, lower=...  19.9 us
    ppermute x4, starting transfers between devices, with_halo(): lax.ppermute(tail, axis, [(i, (i + 1) % count) for i in range(ends)])  17.1 us
    ppermute x4, waiting for transfers between devices, with_halo(): lax.ppermute(head, axis, [((i + 1) % count, i) for i in range(ends)])  10.6 us
  transfers between devices with their start and end apart: 9, of which 7 were waited for; matrix products, arithmetic and copies ran while one was open for 0% of the time, Pallas kernels for 0%

commit v1 on v0

v1 whole, which is shorter than its diff:
```python
import jax
import jax.numpy as jnp
from jax import lax
from jax.experimental import pallas as pl
from jax.experimental.pallas import tpu as pltpu
from jax.sharding import PartitionSpec as P

inflation = 4.0
HIGHEST = lax.Precision.HIGHEST


def swap_pairs(count, first):
    pairs = []
    for i in range(first, count - 1, 2):
        pairs += [(i, i + 1), (i + 1, i)]
    return pairs


def outer_layers(cells, axis, dim):
    count = lax.axis_size(axis)
    even = lax.axis_index(axis) % 2 == 0
    head = lax.slice_in_dim(cells, 0, 1, axis=dim)
    tail = lax.slice_in_dim(cells, cells.shape[dim] - 1, cells.shape[dim], axis=dim)
    first = lax.ppermute(jnp.where(even, tail, head), axis, swap_pairs(count, 0))
    second = lax.ppermute(jnp.where(even, head, tail), axis, swap_pairs(count, 1))
    return jnp.where(even, second, first), jnp.where(even, first, second)


def with_layers(cells, layers_x, layers_y, dim):
    wide = jnp.concatenate([layers_x[0], cells, layers_x[1]], axis=dim)
    pads = [(0, 0)] * cells.ndim
    pads[dim] = (1, 1)
    south, north = (jnp.pad(layer, pads) for layer in layers_y)
    return jnp.concatenate([south, wide, north], axis=dim + 1)


def window(field, shift_x, shift_y, shift_z):
    return field[
        1 + shift_x : field.shape[0] - 1 + shift_x,
        1 + shift_y : field.shape[1] - 1 + shift_y,
        1 + shift_z : field.shape[2] - 1 + shift_z,
    ]


def advance_in_time(padded_temp, padded_diffusivity, advection_courant):
    temp_z = jnp.pad(padded_temp, ((0, 0), (0, 0), (1, 1), (0, 0)))
    cond_z = jnp.pad(padded_diffusivity, ((0, 0), (0, 0), (1, 1), (0, 0)))
    center = window(temp_z, 0, 0, 0)
    cond_center = window(cond_z, 0, 0, 0)
    change = jnp.zeros_like(center)
    for shift_x, shift_y, shift_z in (
        (1, 0, 0),
        (-1, 0, 0),
        (0, 1, 0),
        (0, -1, 0),
        (0, 0, 1),
        (0, 0, -1),
    ):
        change = change + 0.5 * (cond_center + window(cond_z, shift_x, shift_y, shift_z)) * (
            window(temp_z, shift_x, shift_y, shift_z) - center
        )
    upwind = center - window(temp_z, -1, 0, 0)
    return center + change - advection_courant[:, None] * upwind


def modulo(value, divisor):
    quotient = (value.astype(jnp.float32) * (1.0 / divisor)).astype(jnp.int32)
    rest = value - quotient * divisor
    rest = jnp.where(rest < 0, rest + divisor, rest)
    return jnp.where(rest >= divisor, rest - divisor, rest)


def perturbation(obs_index, random_starters):
    first = random_starters * 7919 % 65521
    second = obs_index * 331 % 65521
    hashed = modulo(
        first[None, :] * (second[:, None] % 32749) + first[None, :] + second[:, None], 65521
    )
    uniform_value = (hashed.astype(jnp.float32) + 0.5) / 65521.0
    return jnp.sqrt(3.0) * (2.0 * uniform_value - 1.0)


def plan_exchange(axes, rows, limit):
    gathers, sums, stride = [], [], 1
    for axis in axes:
        count = lax.axis_size(axis)
        bits = [1 << b for b in range(count.bit_length() - 1)]
        while bits:
            if len(bits) > 1 and rows * 4 <= limit:
                low, high = bits[-2], bits[-1]
                gathers.append((axis, stride, (low, high, low | high)))
                rows, bits = rows * 4, bits[:-2]
            elif rows * 2 <= limit:
                gathers.append((axis, stride, (bits.pop(),)))
                rows *= 2
            else:
                sums.append((axis, bits.pop()))
        stride *= count
    return gathers, sums


def swap(block, axis, step):
    return lax.ppermute(block, axis, [(i, i ^ step) for i in range(lax.axis_size(axis))])


def gather_blocks(block, owner, gathers):
    owners = owner[None]
    for axis, stride, steps in gathers:
        block = jnp.concatenate([block] + [swap(block, axis, step) for step in steps])
        owners = jnp.concatenate([owners] + [owners ^ (step * stride) for step in steps])
    return block, owners


def product(a, b, over_a=1, over_b=0):
    return lax.dot_general(
        a, b, (((over_a,), (over_b,)), ((), ())), precision=HIGHEST,
        preferred_element_type=jnp.float32,
    )


def inverse(block):
    size = block.shape[0]
    lane = lax.broadcasted_iota(jnp.int32, (size, size), 1)
    row_index = lax.broadcasted_iota(jnp.int32, (size, size), 0)

    def eight(_, held):
        for p in range(8):
            row = held[p : p + 1, :]
            column = jnp.broadcast_to(held[:, p : p + 1], (size, size))
            pivot = 1.0 / column[p : p + 1, :]
            scaled = jnp.where(lane[:1] == p, pivot, row * pivot)
            column = jnp.where(row_index == p, -1.0, column)
            held = jnp.where((lane == p) | (row_index == p), 0.0, held) - column * scaled
        held = jnp.concatenate([held[8:], held[:8]], 0)
        return pltpu.roll(held, size - 8, 1)

    return lax.fori_loop(0, size // 8, eight, block)


def products(scale, scaled_ref, noise_ref, out_ref):
    scaled = scaled_ref[...]
    members = scaled.shape[1]
    spread = scaled - jnp.sum(scaled, axis=1, keepdims=True) * (1.0 / members)
    misfit = noise_ref[...] - scale * scaled
    out_ref[:, :members] = product(spread, spread, 0, 0)
    out_ref[:, members:] = product(spread, misfit, 0, 0)


def solve(sums_ref, weights_ref):
    members = weights_ref.shape[0]
    half = members // 2
    diagonal = lax.broadcasted_iota(jnp.int32, (half, half), 0) == lax.broadcasted_iota(
        jnp.int32, (half, half), 1
    )
    shift = jnp.where(diagonal, inflation, 0.0)
    upper = product(inverse(sums_ref[:half, :half] + shift), sums_ref[:half, half:])
    lower = sums_ref[half:, half:] - product(sums_ref[half:, :half], upper)
    second = product(inverse(lower[:, :half] + shift), lower[:, half:])
    weights_ref[:half] = upper[:, half:] - product(upper[:, :half], second)
    weights_ref[half:] = second


def smoother(scale, scaled_ref, noise_ref, weights_ref, sums_ref):
    products(scale, scaled_ref, noise_ref, sums_ref)
    solve(sums_ref, weights_ref)


def ensemble_weights(scale, scaled, noise, sums):
    members = scaled.shape[1]
    pair = (members, 2 * members)
    weights = jax.ShapeDtypeStruct((members, members), jnp.float32)
    if not sums:
        return pl.pallas_call(
            lambda *refs: smoother(scale, *refs),
            out_shape=weights,
            scratch_shapes=[pltpu.VMEM(pair, jnp.float32)],
            name="smoother",
        )(scaled, noise)
    total = pl.pallas_call(
        lambda *refs: products(scale, *refs),
        out_shape=jax.ShapeDtypeStruct(pair, jnp.float32),
        name="products",
    )(scaled, noise)
    for axis, step in sums:
        total = total + swap(total, axis, step)
    return pl.pallas_call(solve, out_shape=weights, name="solve")(total)


def shards(
    initial_thermal_state,
    logarithmic_diffusivity,
    rock_class_code,
    rock_class_diffusivity,
    advection_courant,
    probe_locations,
    observed_readings,
    probe_noise_deviation,
    random_starters,
):
    members = initial_thermal_state.shape[-1]
    levels = jnp.arange(rock_class_diffusivity.shape[0], dtype=jnp.int32)
    base_cond = jnp.sum(
        (rock_class_code[..., None] == levels).astype(jnp.float32) * rock_class_diffusivity, axis=-1
    )
    cond = base_cond[..., None] * jnp.exp(logarithmic_diffusivity)
    both = jnp.stack([initial_thermal_state, cond])
    extended = with_layers(both, outer_layers(both, "gx", 1), outer_layers(both, "gy", 2), 1)
    middle = advance_in_time(extended[0], extended[1], advection_courant)
    padded_middle = with_layers(
        middle, outer_layers(middle, "gx", 0), outer_layers(middle, "gy", 1), 0
    )
    final = advance_in_time(padded_middle, extended[1], advection_courant)
    predicted = jnp.take(final.reshape(-1, members), probe_locations, axis=0)
    scale = (members - 1) ** 0.5
    scaled = (predicted - observed_readings[:, None]) / (probe_noise_deviation[:, None] * scale)
    obs_count = probe_locations.shape[0]
    gathers, sums = plan_exchange(("gy", "gx"), obs_count, 4 * members)
    everyone, owners = gather_blocks(scaled, lax.axis_index(("gx", "gy")), gathers)
    obs_index = (
        owners[:, None] * obs_count + jnp.arange(obs_count, dtype=jnp.int32)[None, :]
    ).reshape(-1)
    noise = inflation**0.5 * perturbation(obs_index, random_starters)
    weights = ensemble_weights(scale, everyone, noise, sums)
    anomalies = (
        (logarithmic_diffusivity - jnp.mean(logarithmic_diffusivity, axis=-1, keepdims=True))
        / scale
    ).reshape(-1, members)
    updated = logarithmic_diffusivity.reshape(-1, members) + product(anomalies, weights)
    return (final, updated.reshape(logarithmic_diffusivity.shape))


def solution(mesh):
    placed = (
        P("gx", "gy", None, None),
        P("gx", "gy", None, None),
        P("gx", "gy", None),
        P(),
        P(),
        P(("gx", "gy")),
        P(("gx", "gy")),
        P(("gx", "gy")),
        P(),
    )
    return jax.shard_map(
        shards,
        mesh=mesh,
        in_specs=placed,
        out_specs=(P("gx", "gy", None, None), P("gx", "gy", None, None)),
        check_vma=False,
    )
```

time: 272 us -> 95.8 us (0.35)
  waiting for transfers between devices: 153 us -> 12.4 us
  other arithmetic: 67.8 us -> 16 us
  Pallas kernels: 0 us -> 28.9 us
  between operations: 15.7 us -> 0.98 us
  starting transfers between devices: 22.3 us -> 26.1 us
  matrix products: 6.52 us -> 2.91 us
    psum x1 -> x0, waiting for transfers between devices: 137 us -> none  [shards(): gram, cross = lax.psum((local_gram, local_cross), ('gx', 'gy'))]
    another operation x10 -> x0, other arithmetic: 54.5 us -> none  [the longest x7 34.6 us: shards(): lower_factor = jnp.linalg.cholesky(system)]
    pallas_call x0 -> x1, Pallas kernels: none -> 28.9 us  [ensemble_weights(): pl.pallas_call(lambda *refs: smoother(scale, *refs), out_shape=weights, s...]
    select_n x1 -> x11, other arithmetic: 0.01 us -> 4.53 us  [the longest x4 2.18 us: outer_layers(): return (jnp.where(even, second, first), jnp.where(even, first, second))]
    another operation x18 -> x0, local copies, waits for them, and re-layouts: 4.39 us -> none
    ppermute x8 -> x15, starting transfers between devices: 22.2 us -> 26.1 us  [the longest x7 12.7 us: swap(): lax.ppermute(block, axis, [(i, i ^ step) for i in range(lax.axis_size(axi...]
    ppermute x8 -> x15, waiting for transfers between devices: 15.8 us -> 12.4 us  [the longest x7 7.58 us: swap(): lax.ppermute(block, axis, [(i, i ^ step) for i in range(lax.axis_size(axi...]
    unnamed x20 -> x22, local copies, waits for them, and re-layouts: 0.94 us -> 4.29 us
  transfers between devices with their start and end apart: 9 -> 15, of which waited for: 7 -> 6; matrix products, arithmetic and copies ran while one was open for 0% -> 9% of each run, Pallas kernels for 0% -> 0%
where the time goes in v1:
time: 95.8 us; the launch traced here: 95.4 us
  Pallas kernels  28.9 us (30%)
  starting transfers between devices  26.1 us (27%)
  other arithmetic  16 us (17%)
  waiting for transfers between devices  12.4 us (13%)
  local copies, waits for them, and re-layouts  8.06 us (8%)
  matrix products  2.91 us (3%)
  between operations  0.98 us (1%)
    pallas_call x1, Pallas kernels, ensemble_weights(): pl.pallas_call(lambda *refs: smoother(scale, *refs), out_shape=weights, s...  28.9 us
    ppermute x7, starting transfers between devices, swap(): lax.ppermute(block, axis, [(i, i ^ step) for i in range(lax.axis_size(axi...  12.7 us
    ppermute x4, starting transfers between devices, outer_layers(): lax.ppermute(jnp.where(even, tail, head), axis, swap_pairs(count, 0))  9.43 us
    ppermute x7, waiting for transfers between devices, swap(): lax.ppermute(block, axis, [(i, i ^ step) for i in range(lax.axis_size(axi...  7.58 us
    ppermute x4, waiting for transfers between devices, outer_layers(): lax.ppermute(jnp.where(even, tail, head), axis, swap_pairs(count, 0))  4.79 us
    unnamed x22, local copies, waits for them, and re-layouts  4.29 us
    ppermute x4, starting transfers between devices, outer_layers(): lax.ppermute(jnp.where(even, head, tail), axis, swap_pairs(count, 1))  4.01 us
    sub x2, other arithmetic, advance_in_time(): return center + change - advection_courant[:, None] * upwind  3.86 us
  transfers between devices with their start and end apart: 15, of which 6 were waited for; matrix products, arithmetic and copies ran while one was open for 9% of the time, Pallas kernels for 0%

profile of v1, /device:TPU:0, one launch (start us, length us, event | category | flops | bytes accessed | tf_op | source)
XLA Modules:
  0.0 95.4 jit_solution(14779867145553117045)
XLA Ops:
  0.7 1.5 %reduce_sum.19 = f32[8,8,16]{2,1,0:T(8,128)S(1)} reduce(f32[8,8,16,256]{3,2,1,0:T(8,128)} %param.10, f32[]{:T(128)} %constant.100.clone.1), dimensions={3}, to_apply=%region_1.2 | reduce | flops 261120 | bytes 1052676 | tf_op jit(solution)/shard_map/reduce_sum | solution.py:225
  2.2 0.9 select_reduce_fusion
  3.1 1.6 %subtract_multiply_fusion = (f32[8,8,16,256]{3,2,1,0:T(8,128)S(1)}, f32[1,8,8,16,256]{4,3,2,1,0:T(8,128)S(1)}) fusion(f32[8,8,16,256]{3,2,1,0:T(8,128)} %param.10, f32[8,8,16]{2,1,0:T(8,128)S(1)} %broadcast_multiply_fusion, f32[8,8,16]{2,1,0:T(8,128)S(1)} %select_reduce_fusion), kind=kLoop, calls=%fused_computation.84 | loop fusion | flops 786432 | bytes 3153920 | tf_op jit(solution)/shard_map/div | solution.py:225
  4.8 0.7 broadcast_select_fusion.2
  6.0 1.3 %collective-permute-start.2 = (f32[2,1,8,16,256]{4,3,2,1,0:T(8,128)S(1)}, f32[2,1,8,16,256]{4,3,2,1,0:T(8,128)}, u32[]{:S(2)}, u32[]{:S(2)}) collective-permute-start(f32[2,1,8,16,256]{4,3,2,1,0:T(8,128)S(1)} %get-tuple-element.6), channel_id=1, source_target_pairs={{4,8},{8,4},{12,16},{16,12},{20,24},{24,20},{5,9},{9,5},{13,17},{1... | collective-permute-start | bytes 786440 | tf_op jit(solution)/shard_map/ppermute | solution.py:25
  7.3 0.8 broadcast_select_fusion.7
  8.1 0.7 broadcast_select_fusion.6
  8.9 2.6 %collective-permute-start.1 = (f32[2,8,1,16,256]{4,3,2,1,0:T(8,128)}, f32[2,8,1,16,256]{4,3,2,1,0:T(8,128)}, u32[]{:S(2)}, u32[]{:S(2)}) collective-permute-start(f32[2,8,1,16,256]{4,3,2,1,0:T(8,128)} %broadcast_select_fusion.6), channel_id=1, source_target_pairs={{0,1},{1,0},{2,3},{3,2},{4,5},{5,4},{6,7},{7,6},{8,9},{9,8},{10,11... | collective-permute-start | bytes 786440 | tf_op jit(solution)/shard_map/ppermute | solution.py:24
  11.4 1.3 %collective-permute-start = (f32[2,8,1,16,256]{4,3,2,1,0:T(8,128)}, f32[2,8,1,16,256]{4,3,2,1,0:T(8,128)}, u32[]{:S(2)}, u32[]{:S(2)}) collective-permute-start(f32[2,8,1,16,256]{4,3,2,1,0:T(8,128)} %get-tuple-element.9), channel_id=1, source_target_pairs={{1,2},{2,1},{5,6},{6,5},{9,10},{10,9},{13,14},{14,13},{17,18},{18,... | collective-permute-start | bytes 786440 | tf_op jit(solution)/shard_map/ppermute | solution.py:25
  13.2 1.1 %broadcast_select_fusion.1 = (f32[2,1,8,16,256]{4,3,2,1,0:T(8,128)S(1)}, f32[2,1,8,16,256]{4,3,2,1,0:T(8,128)S(1)}) fusion(f32[2,1,8,16,256]{4,3,2,1,0:T(8,128)} %collective-permute-done.2, f32[2,1,8,16,256]{4,3,2,1,0:T(8,128)} %collective-permute-done.3, pred[]{:T(512)S(6)} %eq.36), kind=kLoop, calls=%fused_computation.94 | loop fusion | flops 131072 | bytes 1048577 | tf_op jit(solution)/shard_map/jit(_where)/select_n | solution.py:26
  14.3 2.9 %collective-permute-done.1 = f32[2,8,1,16,256]{4,3,2,1,0:T(8,128)} collective-permute-done((f32[2,8,1,16,256]{4,3,2,1,0:T(8,128)}, f32[2,8,1,16,256]{4,3,2,1,0:T(8,128)}, u32[]{:S(2)}, u32[]{:S(2)}) %collective-permute-start.1) | collective-permute-done | bytes 262176 | tf_op jit(solution)/shard_map/ppermute | solution.py:24
  17.2 1.1 %broadcast_select_fusion.5 = (f32[2,8,1,16,256]{4,3,2,1,0:T(8,128)S(1)}, f32[2,8,1,16,256]{4,3,2,1,0:T(8,128)S(1)}) fusion(f32[2,8,1,16,256]{4,3,2,1,0:T(8,128)} %collective-permute-done, f32[2,8,1,16,256]{4,3,2,1,0:T(8,128)} %collective-permute-done.1, pred[]{:T(512)S(6)} %eq.32), kind=kLoop, calls=%fused_computation.98 | loop fusion | flops 131072 | bytes 1048577 | tf_op jit(solution)/shard_map/jit(_where)/select_n | solution.py:26
  19.4 1.9 %fusion.10 = f32[8,8,16,256]{3,2,1,0:T(8,128)S(1)} fusion(f32[10,10,16,256]{3,2,1,0:T(8,128)S(1)} %get-tuple-element.13, f32[16]{0:T(128)S(1)} %copy-done.3, f32[10,10,16,256]{3,2,1,0:T(8,128)S(1)} %get-tuple-element.12), kind=kLoop, calls=%fused_computation.30 | loop fusion | flops 8650752 | bytes 14811648 | tf_op jit(solution)/shard_map/sub | solution.py:63
  21.3 5.6 %collective-permute-start.6 = (f32[8,1,16,256]{3,2,1,0:T(8,128)S(1)}, f32[8,1,16,256]{3,2,1,0:T(8,128)S(1)}, u32[]{:S(2)}, u32[]{:S(2)}) collective-permute-start(f32[8,1,16,256]{3,2,1,0:T(8,128)S(1)} %get-tuple-element.19), channel_id=1, source_target_pairs={{0,1},{1,0},{2,3},{3,2},{4,5},{5,4},{6,7},{7,6},{8,9},{9,8},{10,11... | collective-permute-start | bytes 393224 | tf_op jit(solution)/shard_map/ppermute | solution.py:24
  27.6 0.8 collective-permute-start.4
  29.1 1.9 %collective-permute-done.6 = f32[8,1,16,256]{3,2,1,0:T(8,128)S(1)} collective-permute-done((f32[8,1,16,256]{3,2,1,0:T(8,128)S(1)}, f32[8,1,16,256]{3,2,1,0:T(8,128)S(1)}, u32[]{:S(2)}, u32[]{:S(2)}) %collective-permute-start.6) | collective-permute-done | bytes 131104 | tf_op jit(solution)/shard_map/ppermute | solution.py:24
  31.6 2.0 %fusion.21 = f32[8,8,16,256]{3,2,1,0:T(8,128)S(1)} fusion(f32[8,8,16,256]{3,2,1,0:T(8,128)S(1)} %fusion.10, f32[10,10,18,256]{3,2,1,0:T(8,128)S(1)} %select_maximum_fusion.2, f32[10,1,16,256]{3,2,1,0:T(8,128)S(1)} %pad.30, f32[1,8,16,256]{3,2,1,0:T(8,128)S(1)} %get-tuple-element.25, f32[1,8,16,256]{3,2,1,0:T(8,128)S(1)} %get-tuple-element.24, ...), kind=kLoop, calls=%fused_computation.42 | loop fusion | flops 10747904 | bytes 11665920 | tf_op jit(solution)/shard_map/sub | solution.py:63
  34.8 3.5 %collective-permute-start.10 = (f32[32,256]{1,0:T(8,128)S(1)}, f32[32,256]{1,0:T(8,128)S(1)}, u32[]{:S(2)}, u32[]{:S(2)}) collective-permute-start(f32[32,256]{1,0:T(8,128)S(1)} %get-tuple-element.5), channel_id=1, source_target_pairs={{0,3},{1,2},{2,1},{3,0},{4,7},{5,6},{6,5},{7,4},{8,11},{9,10},{10,... | collective-permute-start | bytes 98312 | tf_op jit(solution)/shard_map/ppermute | solution.py:103
  38.3 2.8 %collective-permute-start.8 = (f32[32,256]{1,0:T(8,128)S(1)}, f32[32,256]{1,0:T(8,128)S(1)}, u32[]{:S(2)}, u32[]{:S(2)}) collective-permute-start(f32[32,256]{1,0:T(8,128)S(1)} %get-tuple-element.5), channel_id=1, source_target_pairs={{0,1},{1,0},{2,3},{3,2},{4,5},{5,4},{6,7},{7,6},{8,9},{9,8},{10,11... | collective-permute-start | bytes 98312 | tf_op jit(solution)/shard_map/ppermute | solution.py:103
  41.8 1.3 %collective-permute-done.8 = f32[32,256]{1,0:T(8,128)S(1)} collective-permute-done((f32[32,256]{1,0:T(8,128)S(1)}, f32[32,256]{1,0:T(8,128)S(1)}, u32[]{:S(2)}, u32[]{:S(2)}) %collective-permute-start.8) | collective-permute-done | bytes 32800 | tf_op jit(solution)/shard_map/ppermute | solution.py:103
  43.0 3.3 %collective-permute-done.9 = f32[32,256]{1,0:T(8,128)S(1)} collective-permute-done((f32[32,256]{1,0:T(8,128)S(1)}, f32[32,256]{1,0:T(8,128)S(1)}, u32[]{:S(2)}, u32[]{:S(2)}) %collective-permute-start.9) | collective-permute-done | bytes 32800 | tf_op jit(solution)/shard_map/ppermute | solution.py:103
  46.4 3.7 %collective-permute-start.11 = (f32[128,256]{1,0:T(8,128)S(1)}, f32[128,256]{1,0:T(8,128)S(1)}, u32[]{:S(2)}, u32[]{:S(2)}) collective-permute-start(f32[128,256]{1,0:T(8,128)S(1)} %pad_maximum_fusion.12), channel_id=1, source_target_pairs={{0,8},{4,12},{8,0},{12,4},{16,24},{20,28},{24,16},{28,20},{1,9},{5... | collective-permute-start | bytes 393224 | tf_op jit(solution)/shard_map/ppermute | solution.py:103
  50.0 1.3 %collective-permute-start.12 = (f32[128,256]{1,0:T(8,128)S(1)}, f32[128,256]{1,0:T(8,128)S(1)}, u32[]{:S(2)}, u32[]{:S(2)}) collective-permute-start(f32[128,256]{1,0:T(8,128)S(1)} %pad_maximum_fusion.12), channel_id=1, source_target_pairs={{0,16},{4,20},{8,24},{12,28},{16,0},{20,4},{24,8},{28,12},{1,17},{... | collective-permute-start | bytes 393224 | tf_op jit(solution)/shard_map/ppermute | solution.py:103
  51.3 1.4 %collective-permute-start.13 = (f32[128,256]{1,0:T(8,128)S(1)}, f32[128,256]{1,0:T(8,128)S(1)}, u32[]{:S(2)}, u32[]{:S(2)}) collective-permute-start(f32[128,256]{1,0:T(8,128)S(1)} %pad_maximum_fusion.12), channel_id=1, source_target_pairs={{0,24},{4,28},{8,16},{12,20},{16,8},{20,12},{24,0},{28,4},{1,25},{... | collective-permute-start | bytes 393224 | tf_op jit(solution)/shard_map/ppermute | solution.py:103
  54.6 0.7 constant_dynamic-update-slice_fusion.2
  55.3 2.6 %collective-permute-done.12 = f32[128,256]{1,0:T(8,128)S(1)} collective-permute-done((f32[128,256]{1,0:T(8,128)S(1)}, f32[128,256]{1,0:T(8,128)S(1)}, u32[]{:S(2)}, u32[]{:S(2)}) %collective-permute-start.12) | collective-permute-done | bytes 131104 | tf_op jit(solution)/shard_map/ppermute | solution.py:103
  57.9 0.7 constant_dynamic-update-slice_fusion.1
  58.7 0.7 constant_dynamic-update-slice_fusion
  59.5 1.7 %fusion.17.refs_1_ = f32[1024,256]{1,0:T(8,128)} fusion(s32[1024]{0:T(1024)S(1)} %get-tuple-element.41, s32[1024]{0:T(1024)S(1)} %get-tuple-element.40, s32[256]{0:T(256)S(1)} %and_select_fusion), kind=kLoop, calls=%fused_computation.37 | loop fusion | flops 4980736 | bytes 1057792 | tf_op jit(solution)/shard_map/mul | solution.py:222
  61.6 1.9 %constant_dynamic-update-slice_fusion.7.refs_0_ = f32[1024,256]{1,0:T(8,128)} fusion(f32[1024,256]{1,0:T(8,128)} %get-tuple-element.29, f32[512,256]{1,0:T(8,128)} %collective-permute-done.14), kind=kLoop, calls=%fused_computation.117 | loop fusion | bytes 1048576 | tf_op jit(solution)/shard_map/concatenate | solution.py:109
  63.5 28.9 %smoother.1 = f32[256,256]{1,0:T(8,128)} custom-call(f32[1024,256]{1,0:T(8,128)} %constant_dynamic-update-slice_fusion.7.refs_0_, f32[1024,256]{1,0:T(8,128)} %fusion.17.refs_1_), custom_call_target="tpu_custom_call" | custom-call | tf_op jit(solution)/shard_map/smoother/pallas_call | solution.py:173
  92.4 2.9 %convolution_add_fusion = f32[1024,256]{1,0:T(8,128)} fusion(f32[1024,256]{1,0:T(8,128)S(1)} %bitcast.17, f32[1024,256]{1,0:T(8,128)S(1)} %bitcast.18, f32[256,256]{1,0:T(8,128)} %smoother.1), kind=kOutput, calls=%fused_computation.20 | convolution fusion | flops 805568512 | bytes 3407872 | tf_op jit(solution)/shard_map/dot_general | solution.py:115
  (63 shorter events, 8.2 us)
Async XLA Ops:
  0.6 4.1 %copy-start = (f32[8,8,16,256]{3,2,1,0:T(8,128)S(1)}, f32[8,8,16,256]{3,2,1,0:T(8,128)}, u32[]{:S(2)}) copy-start(f32[8,8,16,256]{3,2,1,0:T(8,128)} %param.9) | copy-start | bytes 3145732
  4.8 8.0 %copy-start.6 = (s32[32]{0:T(128)S(1)}, s32[32]{0:T(128)}, u32[]{:S(2)}) copy-start(s32[32]{0:T(128)} %param.14) | copy-start | bytes 388
  4.8 8.4 %copy-start.7 = (f32[32]{0:T(128)S(1)}, f32[32]{0:T(128)}, u32[]{:S(2)}) copy-start(f32[32]{0:T(128)} %param.16) | copy-start | bytes 388
  5.5 7.7 %collective-permute-start.3 = (f32[2,1,8,16,256]{4,3,2,1,0:T(8,128)}, f32[2,1,8,16,256]{4,3,2,1,0:T(8,128)}, u32[]{:S(2)}, u32[]{:S(2)}) collective-permute-start(f32[2,1,8,16,256]{4,3,2,1,0:T(8,128)} %broadcast_select_fusion.2), channel_id=1, source_target_pairs={{0,4},{4,0},{8,12},{12,8},{16,20},{20,16},{24,28},{28,24},{1,5},{5... | collective-permute-start | bytes 786440 | tf_op jit(solution)/shard_map/ppermute | solution.py:24
  6.0 7.2 %collective-permute-start.2 = (f32[2,1,8,16,256]{4,3,2,1,0:T(8,128)S(1)}, f32[2,1,8,16,256]{4,3,2,1,0:T(8,128)}, u32[]{:S(2)}, u32[]{:S(2)}) collective-permute-start(f32[2,1,8,16,256]{4,3,2,1,0:T(8,128)S(1)} %get-tuple-element.6), channel_id=1, source_target_pairs={{4,8},{8,4},{12,16},{16,12},{20,24},{24,20},{5,9},{9,5},{13,17},{1... | collective-permute-start | bytes 786440 | tf_op jit(solution)/shard_map/ppermute | solution.py:25
  8.9 8.4 %collective-permute-start.1 = (f32[2,8,1,16,256]{4,3,2,1,0:T(8,128)}, f32[2,8,1,16,256]{4,3,2,1,0:T(8,128)}, u32[]{:S(2)}, u32[]{:S(2)}) collective-permute-start(f32[2,8,1,16,256]{4,3,2,1,0:T(8,128)} %broadcast_select_fusion.6), channel_id=1, source_target_pairs={{0,1},{1,0},{2,3},{3,2},{4,5},{5,4},{6,7},{7,6},{8,9},{9,8},{10,11... | collective-permute-start | bytes 786440 | tf_op jit(solution)/shard_map/ppermute | solution.py:24
  11.4 5.8 %collective-permute-start = (f32[2,8,1,16,256]{4,3,2,1,0:T(8,128)}, f32[2,8,1,16,256]{4,3,2,1,0:T(8,128)}, u32[]{:S(2)}, u32[]{:S(2)}) collective-permute-start(f32[2,8,1,16,256]{4,3,2,1,0:T(8,128)} %get-tuple-element.9), channel_id=1, source_target_pairs={{1,2},{2,1},{5,6},{6,5},{9,10},{10,9},{13,14},{14,13},{17,18},{18,... | collective-permute-start | bytes 786440 | tf_op jit(solution)/shard_map/ppermute | solution.py:25
  18.7 0.7 copy-start.3
  21.3 9.6 %collective-permute-start.6 = (f32[8,1,16,256]{3,2,1,0:T(8,128)S(1)}, f32[8,1,16,256]{3,2,1,0:T(8,128)S(1)}, u32[]{:S(2)}, u32[]{:S(2)}) collective-permute-start(f32[8,1,16,256]{3,2,1,0:T(8,128)S(1)} %get-tuple-element.19), channel_id=1, source_target_pairs={{0,1},{1,0},{2,3},{3,2},{4,5},{5,4},{6,7},{7,6},{8,9},{9,8},{10,11... | collective-permute-start | bytes 393224 | tf_op jit(solution)/shard_map/ppermute | solution.py:24
  26.9 4.1 %collective-permute-start.7 = (f32[8,1,16,256]{3,2,1,0:T(8,128)S(1)}, f32[8,1,16,256]{3,2,1,0:T(8,128)S(1)}, u32[]{:S(2)}, u32[]{:S(2)}) collective-permute-start(f32[8,1,16,256]{3,2,1,0:T(8,128)S(1)} %get-tuple-element.18), channel_id=1, source_target_pairs={{1,2},{2,1},{5,6},{6,5},{9,10},{10,9},{13,14},{14,13},{17,18},{18,... | collective-permute-start | bytes 393224 | tf_op jit(solution)/shard_map/ppermute | solution.py:25
  27.6 3.5 %collective-permute-start.4 = (f32[1,8,16,256]{3,2,1,0:T(8,128)S(1)}, f32[1,8,16,256]{3,2,1,0:T(8,128)S(1)}, u32[]{:S(2)}, u32[]{:S(2)}) collective-permute-start(f32[1,8,16,256]{3,2,1,0:T(8,128)S(1)} %get-tuple-element.17), channel_id=1, source_target_pairs={{0,4},{4,0},{8,12},{12,8},{16,20},{20,16},{24,28},{28,24},{1,5},{5... | collective-permute-start | bytes 393224 | tf_op jit(solution)/shard_map/ppermute | solution.py:24
  28.4 2.6 %collective-permute-start.5 = (f32[1,8,16,256]{3,2,1,0:T(8,128)S(1)}, f32[1,8,16,256]{3,2,1,0:T(8,128)S(1)}, u32[]{:S(2)}, u32[]{:S(2)}) collective-permute-start(f32[1,8,16,256]{3,2,1,0:T(8,128)S(1)} %get-tuple-element.16), channel_id=1, source_target_pairs={{4,8},{8,4},{12,16},{16,12},{20,24},{24,20},{5,9},{9,5},{13,17},{1... | collective-permute-start | bytes 393224 | tf_op jit(solution)/shard_map/ppermute | solution.py:25
  31.5 2.6 %copy-start.5 = (f32[32]{0:T(128)S(1)}, f32[32]{0:T(128)}, u32[]{:S(2)}) copy-start(f32[32]{0:T(128)} %param.15) | copy-start | bytes 388
  31.6 27.8 %copy-start.4 = (s32[256]{0:T(256)S(1)}, s32[256]{0:T(256)}, u32[]{:S(2)}) copy-start(s32[256]{0:T(256)} %param.17) | copy-start | bytes 3076
  33.5 58.9 %copy-start.2 = (f32[8,8,16,256]{3,2,1,0:T(8,128)}, f32[8,8,16,256]{3,2,1,0:T(8,128)S(1)}, u32[]{:S(2)}) copy-start(f32[8,8,16,256]{3,2,1,0:T(8,128)S(1)} %fusion.21) | copy-start | bytes 3145732
  34.8 6.9 %collective-permute-start.10 = (f32[32,256]{1,0:T(8,128)S(1)}, f32[32,256]{1,0:T(8,128)S(1)}, u32[]{:S(2)}, u32[]{:S(2)}) collective-permute-start(f32[32,256]{1,0:T(8,128)S(1)} %get-tuple-element.5), channel_id=1, source_target_pairs={{0,3},{1,2},{2,1},{3,0},{4,7},{5,6},{6,5},{7,4},{8,11},{9,10},{10,... | collective-permute-start | bytes 98312 | tf_op jit(solution)/shard_map/ppermute | solution.py:103
  38.3 4.7 %collective-permute-start.8 = (f32[32,256]{1,0:T(8,128)S(1)}, f32[32,256]{1,0:T(8,128)S(1)}, u32[]{:S(2)}, u32[]{:S(2)}) collective-permute-start(f32[32,256]{1,0:T(8,128)S(1)} %get-tuple-element.5), channel_id=1, source_target_pairs={{0,1},{1,0},{2,3},{3,2},{4,5},{5,4},{6,7},{7,6},{8,9},{9,8},{10,11... | collective-permute-start | bytes 98312 | tf_op jit(solution)/shard_map/ppermute | solution.py:103
  41.1 5.2 %collective-permute-start.9 = (f32[32,256]{1,0:T(8,128)S(1)}, f32[32,256]{1,0:T(8,128)S(1)}, u32[]{:S(2)}, u32[]{:S(2)}) collective-permute-start(f32[32,256]{1,0:T(8,128)S(1)} %get-tuple-element.5), channel_id=1, source_target_pairs={{0,2},{1,3},{2,0},{3,1},{4,6},{5,7},{6,4},{7,5},{8,10},{9,11},{10,... | collective-permute-start | bytes 98312 | tf_op jit(solution)/shard_map/ppermute | solution.py:103
  46.4 8.3 %collective-permute-start.11 = (f32[128,256]{1,0:T(8,128)S(1)}, f32[128,256]{1,0:T(8,128)S(1)}, u32[]{:S(2)}, u32[]{:S(2)}) collective-permute-start(f32[128,256]{1,0:T(8,128)S(1)} %pad_maximum_fusion.12), channel_id=1, source_target_pairs={{0,8},{4,12},{8,0},{12,4},{16,24},{20,28},{24,16},{28,20},{1,9},{5... | collective-permute-start | bytes 393224 | tf_op jit(solution)/shard_map/ppermute | solution.py:103
  50.0 7.9 %collective-permute-start.12 = (f32[128,256]{1,0:T(8,128)S(1)}, f32[128,256]{1,0:T(8,128)S(1)}, u32[]{:S(2)}, u32[]{:S(2)}) collective-permute-start(f32[128,256]{1,0:T(8,128)S(1)} %pad_maximum_fusion.12), channel_id=1, source_target_pairs={{0,16},{4,20},{8,24},{12,28},{16,0},{20,4},{24,8},{28,12},{1,17},{... | collective-permute-start | bytes 393224 | tf_op jit(solution)/shard_map/ppermute | solution.py:103
  51.3 7.3 %collective-permute-start.13 = (f32[128,256]{1,0:T(8,128)S(1)}, f32[128,256]{1,0:T(8,128)S(1)}, u32[]{:S(2)}, u32[]{:S(2)}) collective-permute-start(f32[128,256]{1,0:T(8,128)S(1)} %pad_maximum_fusion.12), channel_id=1, source_target_pairs={{0,24},{4,28},{8,16},{12,20},{16,8},{20,12},{24,0},{28,4},{1,25},{... | collective-permute-start | bytes 393224 | tf_op jit(solution)/shard_map/ppermute | solution.py:103
  58.7 33.8 %copy-start.1 = (f32[8,8,16,256]{3,2,1,0:T(8,128)S(1)}, f32[8,8,16,256]{3,2,1,0:T(8,128)}, u32[]{:S(2)}) copy-start(f32[8,8,16,256]{3,2,1,0:T(8,128)} %param.10) | copy-start | bytes 3145732
  59.4 2.3 %collective-permute-start.14 = (f32[512,256]{1,0:T(8,128)}, f32[512,256]{1,0:T(8,128)}, u32[]{:S(2)}, u32[]{:S(2)}) collective-permute-start(f32[512,256]{1,0:T(8,128)} %get-tuple-element.28), channel_id=1, source_target_pairs={{0,4},{4,0},{8,12},{12,8},{16,20},{20,16},{24,28},{28,24},{1,5},{5... | collective-permute-start | bytes 1572872 | tf_op jit(solution)/shard_map/ppermute | solution.py:103

commit v2 on v1

v2 whole, which is shorter than its diff:
```python
import functools

import jax
import jax.numpy as jnp
from jax import lax
from jax.experimental import pallas as pl
from jax.experimental.pallas import tpu as pltpu
from jax.sharding import PartitionSpec as P

inflation = 4.0
HIGHEST = lax.Precision.HIGHEST
VMEM = pl.BlockSpec(memory_space=pltpu.VMEM)
SMEM = pl.BlockSpec(memory_space=pltpu.SMEM)


def f32(*shape):
    return jax.ShapeDtypeStruct(shape, jnp.float32)


def call(kernel, name, outs, specs, args, scratch=(), flops=0):
    moved = sum(4 * a.size for a in args)
    return pl.pallas_call(
        kernel,
        out_shape=outs,
        in_specs=specs,
        out_specs=jax.tree.map(lambda _: VMEM, outs),
        scratch_shapes=scratch,
        compiler_params=pltpu.CompilerParams(vmem_limit_bytes=24 << 20),
        cost_estimate=pl.CostEstimate(flops=flops, bytes_accessed=moved, transcendentals=0),
        name=name,
    )(*args)


def swap_pairs(count, first):
    pairs = []
    for i in range(first, count - 1, 2):
        pairs += [(i, i + 1), (i + 1, i)]
    return pairs


def is_even(axis):
    return lax.rem(lax.axis_index(axis), 2) == 0


def exchange(faces):
    got = []
    for axis, first, face in zip(("gx", "gx", "gy", "gy"), (0, 1, 0, 1), faces):
        got.append(lax.ppermute(face, axis, swap_pairs(lax.axis_size(axis), first)))
    return got


def store_faces(field_ref, rows, put):
    span_x, span_y = rows
    for axis, base in (("gx", 0), ("gy", 2)):
        even = is_even(axis)
        last = (span_x if axis == "gx" else span_y) - 1
        for n in range(2):
            at = jnp.where(even, last, 0) if n == 0 else jnp.where(even, 0, last)
            for k in range(span_y if axis == "gx" else span_x):
                cell = at * span_y + k if axis == "gx" else k * span_y + at
                put(base + n, k, field_ref[cell])


def prepare(rows, t_ref, log_ref, code_ref, rock_ref, h_ref, *rest):
    face_refs, turned = rest[:4], rest[4]
    span_x, span_y = rows
    depth, members = t_ref.shape[1:]
    turned[...] = jnp.zeros_like(turned)
    for x in range(span_x):
        code = code_ref[x]
        base = jnp.zeros(code.shape, jnp.float32)
        for level in range(rock_ref.shape[0]):
            base = jnp.where(code == level, 0.5 * rock_ref[level], base)
        turned[x * span_y : (x + 1) * span_y, :depth] = base
    columns = jnp.transpose(turned[...])[:depth]
    for cell in range(span_x * span_y):
        base = jnp.broadcast_to(columns[:, cell : cell + 1], (depth, members))
        h_ref[cell] = base * jnp.exp(log_ref[cell])

    def put(field):
        def store(n, k, layer):
            face_refs[n][field, k] = layer

        return store

    store_faces(t_ref, rows, put(0))
    store_faces(h_ref, rows, put(1))


def advance(rows, courant_ref, u_ref, h_ref, u_faces, h_faces, write):
    span_x, span_y = rows
    shape = u_ref.shape[1:]
    depth = shape[0]
    level = lax.broadcasted_iota(jnp.int32, shape, 0)
    courant = jnp.zeros(shape, jnp.float32)
    for z in range(depth):
        courant = jnp.where(level == z, courant_ref[z], courant)
    even_x, even_y = is_even("gx"), is_even("gy")

    def beyond(faces, axis, side, k):
        even = even_x if axis == 0 else even_y
        first, second = faces(2 * axis, k), faces(2 * axis + 1, k)
        return jnp.where(even, second, first) if side < 0 else jnp.where(even, first, second)

    def at(ref, faces, x, y):
        if x < 0 or x == span_x:
            return beyond(faces, 0, -1 if x < 0 else 1, y)
        if y < 0 or y == span_y:
            return beyond(faces, 1, -1 if y < 0 else 1, x)
        return ref[x * span_y + y]

    for x in range(span_x):
        south = None
        for y in range(span_y):
            u, h = u_ref[x * span_y + y], h_ref[x * span_y + y]

            def flow(i, j):
                step = at(u_ref, u_faces, i, j) - u
                return step, (h + at(h_ref, h_faces, i, j)) * step

            rise = jnp.where(level == depth - 1, 0.0, pltpu.roll(u, depth - 1, 0)) - u
            lift = (h + jnp.where(level == depth - 1, 0.0, pltpu.roll(h, depth - 1, 0))) * rise
            sink = jnp.where(level == 0, h * u, pltpu.roll(lift, 1, 0))
            west, from_west = flow(x - 1, y)
            from_east = flow(x + 1, y)[1]
            from_north = flow(x, y + 1)[1]
            from_south = flow(x, y - 1)[1] if south is None else south
            south = -from_north
            change = (from_east + from_west) + (from_north + from_south) + (lift - sink)
            write(x * span_y + y, u + change + courant * west)


def halfway(rows, courant_ref, t_ref, h_ref, *rest):
    got, middle_ref, face_refs = rest[:4], rest[4], rest[5:9]

    def write(cell, value):
        middle_ref[cell] = value

    advance(
        rows, courant_ref, t_ref, h_ref,
        lambda n, k: got[n][0, k], lambda n, k: got[n][1, k], write,
    )

    def put(n, k, layer):
        face_refs[n][k] = layer

    store_faces(middle_ref, rows, put)


def observe(rows, courant_ref, cells_ref, reading_ref, factor_ref, u_ref, h_ref, *rest):
    got_u, got_h, final_ref, scaled_ref = rest[:4], rest[4:8], rest[8], rest[9]
    depth = u_ref.shape[1]

    def write(cell, value):
        final_ref[cell * depth : (cell + 1) * depth, :] = value

    advance(
        rows, courant_ref, u_ref, h_ref,
        lambda n, k: got_u[n][k], lambda n, k: got_h[n][1, k], write,
    )
    for j in range(scaled_ref.shape[0]):
        row = final_ref[pl.ds(cells_ref[j], 1), :]
        scaled_ref[j : j + 1, :] = (row - reading_ref[j]) * factor_ref[j]


def modulo(value, divisor):
    quotient = (value.astype(jnp.float32) * (1.0 / divisor)).astype(jnp.int32)
    rest = value - quotient * divisor
    rest = jnp.where(rest < 0, rest + divisor, rest)
    return jnp.where(rest >= divisor, rest - divisor, rest)


def perturbation(obs_index, random_starters):
    first = random_starters * 7919 % 65521
    second = obs_index * 331 % 65521
    hashed = modulo(
        first[None, :] * (second[:, None] % 32749) + first[None, :] + second[:, None], 65521
    )
    uniform_value = (hashed.astype(jnp.float32) + 0.5) / 65521.0
    return jnp.sqrt(3.0) * (2.0 * uniform_value - 1.0)


def plan_exchange(axes, rows, limit):
    gathers, sums, stride = [], [], 1
    for axis in axes:
        count = lax.axis_size(axis)
        bits = [1 << b for b in range(count.bit_length() - 1)]
        while bits:
            if len(bits) > 1 and rows * 4 <= limit:
                low, high = bits[-2], bits[-1]
                gathers.append((axis, stride, (low, high, low | high)))
                rows, bits = rows * 4, bits[:-2]
            elif rows * 2 <= limit:
                gathers.append((axis, stride, (bits.pop(),)))
                rows *= 2
            else:
                sums.append((axis, bits.pop()))
        stride *= count
    return gathers, sums


def swap(block, axis, step):
    return lax.ppermute(block, axis, [(i, i ^ step) for i in range(lax.axis_size(axis))])


def pack(*refs):
    start = 0
    for ref in refs[:-1]:
        refs[-1][start : start + ref.shape[0], :] = ref[...]
        start += ref.shape[0]


def gather_blocks(block, owner, gathers):
    pieces, owners = [block], owner[None]
    for axis, stride, steps in gathers:
        if len(steps) > 1 and len(pieces) > 1:
            rows = sum(piece.shape[0] for piece in pieces)
            pieces = [
                call(pack, "pack", f32(rows, block.shape[1]), [VMEM] * len(pieces), pieces)
            ]
        pieces = pieces + [swap(piece, axis, step) for step in steps for piece in pieces]
        owners = jnp.concatenate([owners] + [owners ^ (step * stride) for step in steps])
    return pieces, owners


def product(a, b, over_a=1, over_b=0):
    return lax.dot_general(
        a, b, (((over_a,), (over_b,)), ((), ())), precision=HIGHEST,
        preferred_element_type=jnp.float32,
    )


def inverse(block):
    size = block.shape[0]
    shape = (8, size)
    lane = lax.broadcasted_iota(jnp.int32, shape, 1)
    sub = lax.broadcasted_iota(jnp.int32, shape, 0)
    count = size // 8
    rows = [block[8 * i : 8 * i + 8, :] for i in range(count)]
    for g in range(count):
        first = 8 * g
        inside = (lane >= first) & (lane < first + 8)
        columns = [
            jnp.broadcast_to(rows[g][:, first + q : first + q + 1], shape) for q in range(8)
        ]
        held = jnp.where(inside, jnp.where(lane - first == sub, 1.0, 0.0), rows[g])
        for p in range(8):
            pivot = 1.0 / columns[p][p : p + 1, :]
            for q in range(p + 1, 8):
                scaled = columns[q][p : p + 1, :] * pivot
                columns[q] = jnp.where(sub == p, scaled, columns[q] - columns[p] * scaled)
            scaled = held[p : p + 1, :] * pivot
            held = jnp.where(sub == p, scaled, held - columns[p] * scaled)
        rows[g] = held
        spread = [jnp.broadcast_to(held[q : q + 1, :], shape) for q in range(8)]
        for i in [*range(g + 1, count), *range(g)]:
            left = jnp.where(inside, 0.0, rows[i])
            for q in range(8):
                left -= jnp.broadcast_to(rows[i][:, first + q : first + q + 1], shape) * spread[q]
            rows[i] = left
    return jnp.concatenate(rows, 0)


def products(scale, piece_refs, noise_ref, out_ref):
    scaled = jnp.concatenate([ref[...] for ref in piece_refs])
    members = scaled.shape[1]
    spread = scaled - jnp.sum(scaled, axis=1, keepdims=True) * (1.0 / members)
    misfit = noise_ref[...] - scale * scaled
    out_ref[:, :members] = product(spread, spread, 0, 0)
    out_ref[:, members:] = product(spread, misfit, 0, 0)


def update(scale, sums_ref, log_ref, updated_ref, weights_ref):
    members = weights_ref.shape[0]
    half = members // 2
    diagonal = lax.broadcasted_iota(jnp.int32, (half, half), 0) == lax.broadcasted_iota(
        jnp.int32, (half, half), 1
    )
    shift = jnp.where(diagonal, inflation, 0.0)
    upper = product(inverse(sums_ref[:half, :half] + shift), sums_ref[:half, half:])
    lower = sums_ref[half:, half:] - product(sums_ref[half:, :half], upper)
    second = product(inverse(lower[:, :half] + shift), lower[:, half:])
    first = upper[:, half:] - product(upper[:, :half], second)
    mean = (
        jnp.sum(first, axis=0, keepdims=True) + jnp.sum(second, axis=0, keepdims=True)
    ) * (1.0 / members)
    weights_ref[:half] = (first - mean) * (1.0 / scale)
    weights_ref[half:] = (second - mean) * (1.0 / scale)
    updated_ref[...] = log_ref[...] + product(log_ref[...], weights_ref[...])


def smooth(scale, *refs):
    *piece_refs, noise_ref, log_ref, updated_ref, sums_ref, weights_ref = refs
    products(scale, piece_refs, noise_ref, sums_ref)
    update(scale, sums_ref, log_ref, updated_ref, weights_ref)


def assimilate(scale, pieces, noise, log_rows, sums):
    members = noise.shape[1]
    pair = (members, 2 * members)
    weights = pltpu.VMEM((members, members), jnp.float32)
    updated = f32(*log_rows.shape)
    if not sums:
        args = [*pieces, noise, log_rows]
        return call(
            functools.partial(smooth, scale), "smooth", updated, [VMEM] * len(args), args,
            scratch=[pltpu.VMEM(pair, jnp.float32), weights], flops=10**9,
        )
    args = [*pieces, noise]
    total = call(
        lambda *refs: products(scale, refs[:-2], *refs[-2:]), "products", f32(*pair),
        [VMEM] * len(args), args, flops=10**9,
    )
    for axis, step in sums:
        total = total + swap(total, axis, step)
    return call(
        functools.partial(update, scale), "update", updated, [VMEM] * 2, [total, log_rows],
        scratch=[weights], flops=10**9,
    )


def shards(
    initial_thermal_state,
    logarithmic_diffusivity,
    rock_class_code,
    rock_class_diffusivity,
    advection_courant,
    probe_locations,
    observed_readings,
    probe_noise_deviation,
    random_starters,
):
    span_x, span_y, depth, members = initial_thermal_state.shape
    rows = (span_x, span_y)
    cells = span_x * span_y
    temperature = initial_thermal_state.reshape(cells, depth, members)
    log_cond = logarithmic_diffusivity.reshape(cells, depth, members)
    tile = f32(cells, depth, members)
    faces = [(span_y, depth, members)] * 2 + [(span_x, depth, members)] * 2
    half_cond, *sent = call(
        functools.partial(prepare, rows), "prepare",
        (tile, *(f32(2, *face) for face in faces)),
        [VMEM, VMEM, VMEM, SMEM],
        [temperature, log_cond, rock_class_code, rock_class_diffusivity],
        scratch=[pltpu.VMEM((-(-cells // 128) * 128, 128), jnp.float32)],
    )
    got = exchange(sent)
    middle, *sent = call(
        functools.partial(halfway, rows), "halfway",
        (tile, *(f32(*face) for face in faces)),
        [SMEM] + [VMEM] * 6,
        [advection_courant, temperature, half_cond, *got],
    )
    got_middle = exchange(sent)
    scale = (members - 1) ** 0.5
    obs_count = probe_locations.shape[0]
    final, scaled = call(
        functools.partial(observe, rows), "observe",
        (f32(cells * depth, members), f32(obs_count, members)),
        [SMEM] * 4 + [VMEM] * 10,
        [
            advection_courant, probe_locations, observed_readings,
            1.0 / (probe_noise_deviation * scale), middle, half_cond, *got_middle, *got,
        ],
    )
    gathers, sums = plan_exchange(("gy", "gx"), obs_count, 4 * members)
    pieces, owners = gather_blocks(scaled, lax.axis_index(("gx", "gy")), gathers)
    obs_index = (
        owners[:, None] * obs_count + jnp.arange(obs_count, dtype=jnp.int32)[None, :]
    ).reshape(-1)
    noise = inflation**0.5 * perturbation(obs_index, random_starters)
    updated = assimilate(scale, pieces, noise, log_cond.reshape(-1, members), sums)
    shape = initial_thermal_state.shape
    return (final.reshape(shape), updated.reshape(shape))


def solution(mesh):
    placed = (
        P("gx", "gy", None, None),
        P("gx", "gy", None, None),
        P("gx", "gy", None),
        P(),
        P(),
        P(("gx", "gy")),
        P(("gx", "gy")),
        P(("gx", "gy")),
        P(),
    )
    return jax.shard_map(
        shards,
        mesh=mesh,
        in_specs=placed,
        out_specs=(P("gx", "gy", None, None), P("gx", "gy", None, None)),
        check_vma=False,
    )
```

time: 95.8 us -> 68.1 us (0.71)
  other arithmetic: 16 us -> 0.97 us
  Pallas kernels: 28.9 us -> 18.7 us
  waiting for transfers between devices: 12.4 us -> 16.7 us
  local copies, waits for them, and re-layouts: 8.06 us -> 4.12 us
  matrix products: 2.91 us -> 0 us
    pallas_call x1 -> x5, Pallas kernels: 28.9 us -> 18.7 us  [call(): pl.pallas_call(kernel, out_shape=outs, in_specs=specs, out_specs=jax.tree...]
    select_n x11 -> x0, other arithmetic: 4.53 us -> none  [the longest x4 2.18 us: outer_layers(): return (jnp.where(even, second, first), jnp.where(even, first, second))]
    sub x2 -> x0, other arithmetic: 3.86 us -> none  [advance_in_time(): return center + change - advection_courant[:, None] * upwind]
    ppermute x7 -> x10, waiting for transfers between devices: 7.58 us -> 10.7 us  [swap(): lax.ppermute(block, axis, [(i, i ^ step) for i in range(lax.axis_size(axi...]
    dot_general x1 -> x0, matrix products: 2.91 us -> none  [product(): lax.dot_general(a, b, (((over_a,), (over_b,)), ((), ())), precision=HIGHE...]
    concatenate x2 -> x0, local copies, waits for them, and re-layouts: 2.58 us -> none  [gather_blocks(): jnp.concatenate([block] + [swap(block, axis, step) for step in steps])]
    reduce_sum x2 -> x0, other arithmetic: 2.45 us -> none  [the longest x1 1.52 us: shards(): jnp.mean(logarithmic_diffusivity, axis=-1, keepdims=True)]
    div x2 -> x1, other arithmetic: 1.57 us -> 0.01 us  [shards(): 1.0 / (probe_noise_deviation * scale)]
  transfers between devices with their start and end apart: 15 -> 18, of which waited for: 6 -> 8; matrix products, arithmetic and copies ran while one was open for 9% -> 2% of each run, Pallas kernels for 0% -> 0%
where the time goes in v2:
time: 68.1 us; the launch traced here: 67.8 us
  starting transfers between devices  26.5 us (39%)
  Pallas kernels  18.7 us (27%)
  waiting for transfers between devices  16.7 us (25%)
  local copies, waits for them, and re-layouts  4.12 us (6%)
  other arithmetic  0.97 us (1%)
  between operations  0.84 us (1%)
    pallas_call x5, Pallas kernels, call(): pl.pallas_call(kernel, out_shape=outs, in_specs=specs, out_specs=jax.tree...  18.7 us
    ppermute x10, starting transfers between devices, swap(): lax.ppermute(block, axis, [(i, i ^ step) for i in range(lax.axis_size(axi...  13.5 us
    ppermute x8, starting transfers between devices, exchange(): got.append(lax.ppermute(face, axis, swap_pairs(lax.axis_size(axis), first)))  13 us
    ppermute x10, waiting for transfers between devices, swap(): lax.ppermute(block, axis, [(i, i ^ step) for i in range(lax.axis_size(axi...  10.7 us
    ppermute x8, waiting for transfers between devices, exchange(): got.append(lax.ppermute(face, axis, swap_pairs(lax.axis_size(axis), first)))  6 us
    unnamed x22, local copies, waits for them, and re-layouts  3.89 us
  transfers between devices with their start and end apart: 18, of which 8 were waited for; matrix products, arithmetic and copies ran while one was open for 2% of the time, Pallas kernels for 0%

profile of v2, /device:TPU:0, one launch (start us, length us, event | category | flops | bytes accessed | tf_op | source)
XLA Modules:
  0.0 67.8 jit_solution(12605439100189594562)
XLA Ops:
  0.6 0.6 copy-done.6
  1.3 1.2 %copy-done = f32[8,8,16,256]{3,2,1,0:T(8,128)S(1)} copy-done((f32[8,8,16,256]{3,2,1,0:T(8,128)S(1)}, f32[8,8,16,256]{3,2,1,0:T(8,128)}, u32[]{:S(2)}) %copy-start) | copy-done | bytes 1048600
  2.5 1.2 %copy-done.2 = f32[8,8,16,256]{3,2,1,0:T(8,128)S(1)} copy-done((f32[8,8,16,256]{3,2,1,0:T(8,128)S(1)}, f32[8,8,16,256]{3,2,1,0:T(8,128)}, u32[]{:S(2)}) %copy-start.2) | copy-done | bytes 1048600
  3.7 0.8 %copy-done.4 = s32[8,8,16]{2,1,0:T(8,128)S(1)} copy-done((s32[8,8,16]{2,1,0:T(8,128)S(1)}, s32[8,8,16]{2,1,0:T(8,128)}, u32[]{:S(2)}) %copy-start.4) | copy-done | bytes 4120
  4.5 1.8 %prepare.1 = (f32[64,16,256]{2,1,0:T(8,128)S(1)}, f32[2,8,16,256]{3,2,1,0:T(8,128)}, f32[2,8,16,256]{3,2,1,0:T(8,128)}, f32[2,8,16,256]{3,2,1,0:T(8,128)}, f32[2,8,16,256]{3,2,1,0:T(8,128)S(1)}) custom-call(f32[64,16,256]{2,1,0:T(8,128)S(1)} %bitcast.6, f32[64,16,256]{2,1,0:T(8,128)S(1)} %bitcast.8, s32[8,8,16]{2,1,0:T(8,128)S(1)} %copy-done.4, f32[8]{0:T(128)S(1)} %copy-done.6), custom_call_target="tpu_custom_call" | custom-call | bytes 2101280 | tf_op jit(solution)/shard_map/prepare/pallas_call | solution.py:22
  6.3 0.5 collective-permute-start
  6.8 0.7 collective-permute-start.1
  7.4 2.6 %collective-permute-start.2 = (f32[2,8,16,256]{3,2,1,0:T(8,128)}, f32[2,8,16,256]{3,2,1,0:T(8,128)S(1)}, u32[]{:S(2)}, u32[]{:S(2)}) collective-permute-start(f32[2,8,16,256]{3,2,1,0:T(8,128)} %get-tuple-element.17), channel_id=1, source_target_pairs={{0,1},{1,0},{2,3},{3,2},{4,5},{5,4},{6,7},{7,6},{8,9},{9,8},{10,11... | collective-permute-start | bytes 786440 | tf_op jit(solution)/shard_map/ppermute | solution.py:48
  10.1 0.7 collective-permute-start.3
  10.9 0.1 concatenate.27
  11.0 0.1 multiply_remainder_fusion
  11.2 3.9 %collective-permute-done.2.rest_2_.rest_6_ = f32[2,8,16,256]{3,2,1,0:T(8,128)S(1)} collective-permute-done((f32[2,8,16,256]{3,2,1,0:T(8,128)}, f32[2,8,16,256]{3,2,1,0:T(8,128)S(1)}, u32[]{:S(2)}, u32[]{:S(2)}) %collective-permute-start.2) | collective-permute-done | bytes 262176 | tf_op jit(solution)/shard_map/ppermute | solution.py:48
  15.2 1.6 %halfway.1 = (f32[64,16,256]{2,1,0:T(8,128)S(1)}, f32[8,16,256]{2,1,0:T(8,128)S(1)}, f32[8,16,256]{2,1,0:T(8,128)S(1)}, f32[8,16,256]{2,1,0:T(8,128)S(1)}, f32[8,16,256]{2,1,0:T(8,128)S(1)}) custom-call(f32[16]{0:T(128)S(1)} %copy-done.5, f32[64,16,256]{2,1,0:T(8,128)S(1)} %bitcast.7, f32[64,16,256]{2,1,0:T(8,128)S(1)} %get-tuple-element.14.h_ref, ...), custom_call_target="tpu_custom_call" | custom-call | bytes 3145792 | tf_op jit(solution)/shard_map/halfway/pallas_call | solution.py:22
  16.8 2.4 %collective-permute-start.4 = (f32[8,16,256]{2,1,0:T(8,128)S(1)}, f32[8,16,256]{2,1,0:T(8,128)S(1)}, u32[]{:S(2)}, u32[]{:S(2)}) collective-permute-start(f32[8,16,256]{2,1,0:T(8,128)S(1)} %get-tuple-element.20), channel_id=1, source_target_pairs={{0,4},{4,0},{8,12},{12,8},{16,20},{20,16},{24,28},{28,24},{1,5},{5... | collective-permute-start | bytes 393224 | tf_op jit(solution)/shard_map/ppermute | solution.py:48
  19.1 0.7 collective-permute-start.5
  19.8 4.7 %collective-permute-start.6 = (f32[8,16,256]{2,1,0:T(8,128)S(1)}, f32[8,16,256]{2,1,0:T(8,128)S(1)}, u32[]{:S(2)}, u32[]{:S(2)}) collective-permute-start(f32[8,16,256]{2,1,0:T(8,128)S(1)} %get-tuple-element.22), channel_id=1, source_target_pairs={{0,1},{1,0},{2,3},{3,2},{4,5},{5,4},{6,7},{7,6},{8,9},{9,8},{10,11... | collective-permute-start | bytes 393224 | tf_op jit(solution)/shard_map/ppermute | solution.py:48
  24.5 0.8 %collective-permute-start.7 = (f32[8,16,256]{2,1,0:T(8,128)S(1)}, f32[8,16,256]{2,1,0:T(8,128)S(1)}, u32[]{:S(2)}, u32[]{:S(2)}) collective-permute-start(f32[8,16,256]{2,1,0:T(8,128)S(1)} %get-tuple-element.23), channel_id=1, source_target_pairs={{1,2},{2,1},{5,6},{6,5},{9,10},{10,9},{13,14},{14,13},{17,18},{18,... | collective-permute-start | bytes 393224 | tf_op jit(solution)/shard_map/ppermute | solution.py:48
  25.4 2.0 %collective-permute-done.6.rest_2_ = f32[8,16,256]{2,1,0:T(8,128)S(1)} collective-permute-done((f32[8,16,256]{2,1,0:T(8,128)S(1)}, f32[8,16,256]{2,1,0:T(8,128)S(1)}, u32[]{:S(2)}, u32[]{:S(2)}) %collective-permute-start.6) | collective-permute-done | bytes 131104 | tf_op jit(solution)/shard_map/ppermute | solution.py:48
  27.5 2.6 %observe.1 = (f32[1024,256]{1,0:T(8,128)}, f32[32,256]{1,0:T(8,128)S(1)}) custom-call(f32[16]{0:T(128)S(1)} %copy-done.5, s32[32]{0:T(128)S(1)} %copy-done.7, f32[32]{0:T(128)S(1)} %copy-done.8, f32[32]{0:T(128)S(1)} %multiply_divide_fusion.factor_ref, f32[64,16,256]{2,1,0:T(8,128)S(1)} %get-tuple-element.19.u_ref, ...), custom_call_target="tpu_custom_call" | custom-call | bytes 3670464 | tf_op jit(solution)/shard_map/observe/pallas_call | solution.py:22
  30.1 2.9 %collective-permute-start.10 = (f32[32,256]{1,0:T(8,128)S(1)}, f32[32,256]{1,0:T(8,128)S(1)}, u32[]{:S(2)}, u32[]{:S(2)}) collective-permute-start(f32[32,256]{1,0:T(8,128)S(1)} %get-tuple-element.25.refs_0_), channel_id=1, source_target_pairs={{0,3},{1,2},{2,1},{3,0},{4,7},{5,6},{6,5},{7,4},{8,11},{9,10},{10,... | collective-permute-start | bytes 98312 | tf_op jit(solution)/shard_map/ppermute | solution.py:203
  33.0 3.0 %collective-permute-start.8 = (f32[32,256]{1,0:T(8,128)S(1)}, f32[32,256]{1,0:T(8,128)S(1)}, u32[]{:S(2)}, u32[]{:S(2)}) collective-permute-start(f32[32,256]{1,0:T(8,128)S(1)} %get-tuple-element.25.refs_0_), channel_id=1, source_target_pairs={{0,1},{1,0},{2,3},{3,2},{4,5},{5,4},{6,7},{7,6},{8,9},{9,8},{10,11... | collective-permute-start | bytes 98312 | tf_op jit(solution)/shard_map/ppermute | solution.py:203
  36.1 1.9 %collective-permute-done.8.refs_1_ = f32[32,256]{1,0:T(8,128)S(1)} collective-permute-done((f32[32,256]{1,0:T(8,128)S(1)}, f32[32,256]{1,0:T(8,128)S(1)}, u32[]{:S(2)}, u32[]{:S(2)}) %collective-permute-start.8) | collective-permute-done | bytes 32800 | tf_op jit(solution)/shard_map/ppermute | solution.py:203
  37.9 3.0 %collective-permute-done.9.refs_2_ = f32[32,256]{1,0:T(8,128)S(1)} collective-permute-done((f32[32,256]{1,0:T(8,128)S(1)}, f32[32,256]{1,0:T(8,128)S(1)}, u32[]{:S(2)}, u32[]{:S(2)}) %collective-permute-start.9) | collective-permute-done | bytes 32800 | tf_op jit(solution)/shard_map/ppermute | solution.py:203
  41.0 5.4 %collective-permute-start.11 = (f32[128,256]{1,0:T(8,128)S(1)}, f32[128,256]{1,0:T(8,128)S(1)}, u32[]{:S(2)}, u32[]{:S(2)}) collective-permute-start(f32[128,256]{1,0:T(8,128)S(1)} %pack.1.refs_0_), channel_id=1, source_target_pairs={{0,8},{4,12},{8,0},{12,4},{16,24},{20,28},{24,16},{28,20},{1,9},{5... | collective-permute-start | bytes 393224 | tf_op jit(solution)/shard_map/ppermute | solution.py:203
  46.3 1.6 %collective-permute-start.12 = (f32[128,256]{1,0:T(8,128)S(1)}, f32[128,256]{1,0:T(8,128)S(1)}, u32[]{:S(2)}, u32[]{:S(2)}) collective-permute-start(f32[128,256]{1,0:T(8,128)S(1)} %pack.1.refs_0_), channel_id=1, source_target_pairs={{0,16},{4,20},{8,24},{12,28},{16,0},{20,4},{24,8},{28,12},{1,17},{... | collective-permute-start | bytes 393224 | tf_op jit(solution)/shard_map/ppermute | solution.py:203
  47.9 0.5 collective-permute-start.13
  48.6 1.3 %collective-permute-done.11.refs_1_ = f32[128,256]{1,0:T(8,128)S(1)} collective-permute-done((f32[128,256]{1,0:T(8,128)S(1)}, f32[128,256]{1,0:T(8,128)S(1)}, u32[]{:S(2)}, u32[]{:S(2)}) %collective-permute-start.11) | collective-permute-done | bytes 131104 | tf_op jit(solution)/shard_map/ppermute | solution.py:203
  49.9 2.6 %collective-permute-done.12.refs_2_ = f32[128,256]{1,0:T(8,128)S(1)} collective-permute-done((f32[128,256]{1,0:T(8,128)S(1)}, f32[128,256]{1,0:T(8,128)S(1)}, u32[]{:S(2)}, u32[]{:S(2)}) %collective-permute-start.12) | collective-permute-done | bytes 131104 | tf_op jit(solution)/shard_map/ppermute | solution.py:203
  52.5 1.3 %collective-permute-done.13.refs_3_ = f32[128,256]{1,0:T(8,128)S(1)} collective-permute-done((f32[128,256]{1,0:T(8,128)S(1)}, f32[128,256]{1,0:T(8,128)S(1)}, u32[]{:S(2)}, u32[]{:S(2)}) %collective-permute-start.13) | collective-permute-done | bytes 131104 | tf_op jit(solution)/shard_map/ppermute | solution.py:203
  53.8 0.7 %fusion.4.refs_8_ = f32[1024,256]{1,0:T(8,128)S(1)} fusion(s32[1024]{0:T(1024)S(1)} %get-tuple-element.29, s32[1024]{0:T(1024)S(1)} %get-tuple-element.28, s32[256]{0:T(256)S(1)} %and_select_fusion), kind=kLoop, calls=%fused_computation.6 | loop fusion | flops 4980736 | bytes 1057792 | tf_op jit(solution)/shard_map/mul | solution.py:371
  54.6 0.6 collective-permute-done.17.refs_7_
  55.2 12.6 %smooth.1 = f32[1024,256]{1,0:T(8,128)} custom-call(f32[128,256]{1,0:T(8,128)S(1)} %pack.1.refs_0_, f32[128,256]{1,0:T(8,128)S(1)} %collective-permute-done.11.refs_1_, f32[128,256]{1,0:T(8,128)S(1)} %collective-permute-done.12.refs_2_, f32[128,256]{1,0:T(8,128)S(1)} %collective-permute-done.13.refs_3_, f32[128,256]{1,0:T(8,128)S(1)} %collective-permute-done.14.refs_4_, ...), custom_call_target="tpu_custom_call" | custom-call | flops 1000000000 | bytes 3145728 | tf_op jit(solution)/shard_map/smooth/pallas_call | solution.py:22
  (43 shorter events, 0.4 us)
Async XLA Ops:
  0.6 0.7 copy-start.6
  1.3 1.2 %copy-start = (f32[8,8,16,256]{3,2,1,0:T(8,128)S(1)}, f32[8,8,16,256]{3,2,1,0:T(8,128)}, u32[]{:S(2)}) copy-start(f32[8,8,16,256]{3,2,1,0:T(8,128)} %param.9) | copy-start | bytes 3145732
  2.5 1.2 %copy-start.2 = (f32[8,8,16,256]{3,2,1,0:T(8,128)S(1)}, f32[8,8,16,256]{3,2,1,0:T(8,128)}, u32[]{:S(2)}) copy-start(f32[8,8,16,256]{3,2,1,0:T(8,128)} %param.10) | copy-start | bytes 3145732
  3.7 0.8 %copy-start.4 = (s32[8,8,16]{2,1,0:T(8,128)S(1)}, s32[8,8,16]{2,1,0:T(8,128)}, u32[]{:S(2)}) copy-start(s32[8,8,16]{2,1,0:T(8,128)} %code_ref.1) | copy-start | bytes 12292
  4.5 10.7 %copy-start.1 = (f32[8,8,16,256]{3,2,1,0:T(8,128)S(1)}, f32[8,8,16,256]{3,2,1,0:T(8,128)}, u32[]{:S(2)}) copy-start(f32[8,8,16,256]{3,2,1,0:T(8,128)} %param.9) | copy-start | bytes 3145732
  6.3 4.9 %collective-permute-start = (f32[2,8,16,256]{3,2,1,0:T(8,128)}, f32[2,8,16,256]{3,2,1,0:T(8,128)S(1)}, u32[]{:S(2)}, u32[]{:S(2)}) collective-permute-start(f32[2,8,16,256]{3,2,1,0:T(8,128)} %get-tuple-element.15), channel_id=1, source_target_pairs={{0,4},{4,0},{8,12},{12,8},{16,20},{20,16},{24,28},{28,24},{1,5},{5... | collective-permute-start | bytes 786440 | tf_op jit(solution)/shard_map/ppermute | solution.py:48
  6.8 4.4 %collective-permute-start.1 = (f32[2,8,16,256]{3,2,1,0:T(8,128)}, f32[2,8,16,256]{3,2,1,0:T(8,128)S(1)}, u32[]{:S(2)}, u32[]{:S(2)}) collective-permute-start(f32[2,8,16,256]{3,2,1,0:T(8,128)} %get-tuple-element.16), channel_id=1, source_target_pairs={{4,8},{8,4},{12,16},{16,12},{20,24},{24,20},{5,9},{9,5},{13,17},{1... | collective-permute-start | bytes 786440 | tf_op jit(solution)/shard_map/ppermute | solution.py:48
  7.4 7.7 %collective-permute-start.2 = (f32[2,8,16,256]{3,2,1,0:T(8,128)}, f32[2,8,16,256]{3,2,1,0:T(8,128)S(1)}, u32[]{:S(2)}, u32[]{:S(2)}) collective-permute-start(f32[2,8,16,256]{3,2,1,0:T(8,128)} %get-tuple-element.17), channel_id=1, source_target_pairs={{0,1},{1,0},{2,3},{3,2},{4,5},{5,4},{6,7},{7,6},{8,9},{9,8},{10,11... | collective-permute-start | bytes 786440 | tf_op jit(solution)/shard_map/ppermute | solution.py:48
  10.1 5.1 %collective-permute-start.3 = (f32[2,8,16,256]{3,2,1,0:T(8,128)S(1)}, f32[2,8,16,256]{3,2,1,0:T(8,128)S(1)}, u32[]{:S(2)}, u32[]{:S(2)}) collective-permute-start(f32[2,8,16,256]{3,2,1,0:T(8,128)S(1)} %get-tuple-element.18), channel_id=1, source_target_pairs={{1,2},{2,1},{5,6},{6,5},{9,10},{10,9},{13,14},{14,13},{17,18},{18,... | collective-permute-start | bytes 786440 | tf_op jit(solution)/shard_map/ppermute | solution.py:48
  11.2 4.0 %copy-start.5 = (f32[16]{0:T(128)S(1)}, f32[16]{0:T(128)}, u32[]{:S(2)}) copy-start(f32[16]{0:T(128)} %courant_ref.3) | copy-start | bytes 196
  16.8 8.6 %collective-permute-start.4 = (f32[8,16,256]{2,1,0:T(8,128)S(1)}, f32[8,16,256]{2,1,0:T(8,128)S(1)}, u32[]{:S(2)}, u32[]{:S(2)}) collective-permute-start(f32[8,16,256]{2,1,0:T(8,128)S(1)} %get-tuple-element.20), channel_id=1, source_target_pairs={{0,4},{4,0},{8,12},{12,8},{16,20},{20,16},{24,28},{28,24},{1,5},{5... | collective-permute-start | bytes 393224 | tf_op jit(solution)/shard_map/ppermute | solution.py:48
  19.1 6.3 %collective-permute-start.5 = (f32[8,16,256]{2,1,0:T(8,128)S(1)}, f32[8,16,256]{2,1,0:T(8,128)S(1)}, u32[]{:S(2)}, u32[]{:S(2)}) collective-permute-start(f32[8,16,256]{2,1,0:T(8,128)S(1)} %get-tuple-element.21), channel_id=1, source_target_pairs={{4,8},{8,4},{12,16},{16,12},{20,24},{24,20},{5,9},{9,5},{13,17},{1... | collective-permute-start | bytes 393224 | tf_op jit(solution)/shard_map/ppermute | solution.py:48
  19.8 5.6 %copy-start.10 = (f32[32]{0:T(128)S(1)}, f32[32]{0:T(128)}, u32[]{:S(2)}) copy-start(f32[32]{0:T(128)} %param.16) | copy-start | bytes 388
  19.8 7.6 %collective-permute-start.6 = (f32[8,16,256]{2,1,0:T(8,128)S(1)}, f32[8,16,256]{2,1,0:T(8,128)S(1)}, u32[]{:S(2)}, u32[]{:S(2)}) collective-permute-start(f32[8,16,256]{2,1,0:T(8,128)S(1)} %get-tuple-element.22), channel_id=1, source_target_pairs={{0,1},{1,0},{2,3},{3,2},{4,5},{5,4},{6,7},{7,6},{8,9},{9,8},{10,11... | collective-permute-start | bytes 393224 | tf_op jit(solution)/shard_map/ppermute | solution.py:48
  24.5 3.0 %collective-permute-start.7 = (f32[8,16,256]{2,1,0:T(8,128)S(1)}, f32[8,16,256]{2,1,0:T(8,128)S(1)}, u32[]{:S(2)}, u32[]{:S(2)}) collective-permute-start(f32[8,16,256]{2,1,0:T(8,128)S(1)} %get-tuple-element.23), channel_id=1, source_target_pairs={{1,2},{2,1},{5,6},{6,5},{9,10},{10,9},{13,14},{14,13},{17,18},{18,... | collective-permute-start | bytes 393224 | tf_op jit(solution)/shard_map/ppermute | solution.py:48
  25.4 2.1 %copy-start.7 = (s32[32]{0:T(128)S(1)}, s32[32]{0:T(128)}, u32[]{:S(2)}) copy-start(s32[32]{0:T(128)} %cells_ref.1) | copy-start | bytes 388
  25.4 2.1 %copy-start.8 = (f32[32]{0:T(128)S(1)}, f32[32]{0:T(128)}, u32[]{:S(2)}) copy-start(f32[32]{0:T(128)} %reading_ref.1) | copy-start | bytes 388
  27.5 21.0 %copy-start.9 = (s32[256]{0:T(256)S(1)}, s32[256]{0:T(256)}, u32[]{:S(2)}) copy-start(s32[256]{0:T(256)} %param.17) | copy-start | bytes 3076
  30.1 25.1 %copy-start.3 = (f32[8,8,16,256]{3,2,1,0:T(8,128)S(1)}, f32[8,8,16,256]{3,2,1,0:T(8,128)}, u32[]{:S(2)}) copy-start(f32[8,8,16,256]{3,2,1,0:T(8,128)} %param.10) | copy-start | bytes 3145732
  30.1 5.9 %collective-permute-start.10 = (f32[32,256]{1,0:T(8,128)S(1)}, f32[32,256]{1,0:T(8,128)S(1)}, u32[]{:S(2)}, u32[]{:S(2)}) collective-permute-start(f32[32,256]{1,0:T(8,128)S(1)} %get-tuple-element.25.refs_0_), channel_id=1, source_target_pairs={{0,3},{1,2},{2,1},{3,0},{4,7},{5,6},{6,5},{7,4},{8,11},{9,10},{10,... | collective-permute-start | bytes 98312 | tf_op jit(solution)/shard_map/ppermute | solution.py:203
  33.0 4.9 %collective-permute-start.8 = (f32[32,256]{1,0:T(8,128)S(1)}, f32[32,256]{1,0:T(8,128)S(1)}, u32[]{:S(2)}, u32[]{:S(2)}) collective-permute-start(f32[32,256]{1,0:T(8,128)S(1)} %get-tuple-element.25.refs_0_), channel_id=1, source_target_pairs={{0,1},{1,0},{2,3},{3,2},{4,5},{5,4},{6,7},{7,6},{8,9},{9,8},{10,11... | collective-permute-start | bytes 98312 | tf_op jit(solution)/shard_map/ppermute | solution.py:203
  36.0 4.9 %collective-permute-start.9 = (f32[32,256]{1,0:T(8,128)S(1)}, f32[32,256]{1,0:T(8,128)S(1)}, u32[]{:S(2)}, u32[]{:S(2)}) collective-permute-start(f32[32,256]{1,0:T(8,128)S(1)} %get-tuple-element.25.refs_0_), channel_id=1, source_target_pairs={{0,2},{1,3},{2,0},{3,1},{4,6},{5,7},{6,4},{7,5},{8,10},{9,11},{10,... | collective-permute-start | bytes 98312 | tf_op jit(solution)/shard_map/ppermute | solution.py:203
  41.0 8.9 %collective-permute-start.11 = (f32[128,256]{1,0:T(8,128)S(1)}, f32[128,256]{1,0:T(8,128)S(1)}, u32[]{:S(2)}, u32[]{:S(2)}) collective-permute-start(f32[128,256]{1,0:T(8,128)S(1)} %pack.1.refs_0_), channel_id=1, source_target_pairs={{0,8},{4,12},{8,0},{12,4},{16,24},{20,28},{24,16},{28,20},{1,9},{5... | collective-permute-start | bytes 393224 | tf_op jit(solution)/shard_map/ppermute | solution.py:203
  46.3 6.1 %collective-permute-start.12 = (f32[128,256]{1,0:T(8,128)S(1)}, f32[128,256]{1,0:T(8,128)S(1)}, u32[]{:S(2)}, u32[]{:S(2)}) collective-permute-start(f32[128,256]{1,0:T(8,128)S(1)} %pack.1.refs_0_), channel_id=1, source_target_pairs={{0,16},{4,20},{8,24},{12,28},{16,0},{20,4},{24,8},{28,12},{1,17},{... | collective-permute-start | bytes 393224 | tf_op jit(solution)/shard_map/ppermute | solution.py:203
  47.9 5.9 %collective-permute-start.13 = (f32[128,256]{1,0:T(8,128)S(1)}, f32[128,256]{1,0:T(8,128)S(1)}, u32[]{:S(2)}, u32[]{:S(2)}) collective-permute-start(f32[128,256]{1,0:T(8,128)S(1)} %pack.1.refs_0_), channel_id=1, source_target_pairs={{0,24},{4,28},{8,16},{12,20},{16,8},{20,12},{24,0},{28,4},{1,25},{... | collective-permute-start | bytes 393224 | tf_op jit(solution)/shard_map/ppermute | solution.py:203
  48.5 6.1 %collective-permute-start.14 = (f32[128,256]{1,0:T(8,128)S(1)}, f32[128,256]{1,0:T(8,128)S(1)}, u32[]{:S(2)}, u32[]{:S(2)}) collective-permute-start(f32[128,256]{1,0:T(8,128)S(1)} %pack.1.refs_0_), channel_id=1, source_target_pairs={{0,4},{4,0},{8,12},{12,8},{16,20},{20,16},{24,28},{28,24},{1,5},{5... | collective-permute-start | bytes 393224 | tf_op jit(solution)/shard_map/ppermute | solution.py:203
  49.9 4.7 %collective-permute-start.15 = (f32[128,256]{1,0:T(8,128)S(1)}, f32[128,256]{1,0:T(8,128)S(1)}, u32[]{:S(2)}, u32[]{:S(2)}) collective-permute-start(f32[128,256]{1,0:T(8,128)S(1)} %collective-permute-done.11.refs_1_), channel_id=1, source_target_pairs={{0,4},{4,0},{8,12},{12,8},{16,20},{20,16},{24,28},{28,24},{1,5},{5... | collective-permute-start | bytes 393224 | tf_op jit(solution)/shard_map/ppermute | solution.py:203
  52.5 2.1 %collective-permute-start.16 = (f32[128,256]{1,0:T(8,128)S(1)}, f32[128,256]{1,0:T(8,128)S(1)}, u32[]{:S(2)}, u32[]{:S(2)}) collective-permute-start(f32[128,256]{1,0:T(8,128)S(1)} %collective-permute-done.12.refs_2_), channel_id=1, source_target_pairs={{0,4},{4,0},{8,12},{12,8},{16,20},{20,16},{24,28},{28,24},{1,5},{5... | collective-permute-start | bytes 393224 | tf_op jit(solution)/shard_map/ppermute | solution.py:203
  53.8 1.3 %collective-permute-start.17 = (f32[128,256]{1,0:T(8,128)S(1)}, f32[128,256]{1,0:T(8,128)S(1)}, u32[]{:S(2)}, u32[]{:S(2)}) collective-permute-start(f32[128,256]{1,0:T(8,128)S(1)} %collective-permute-done.13.refs_3_), channel_id=1, source_target_pairs={{0,4},{4,0},{8,12},{12,8},{16,20},{20,16},{24,28},{28,24},{1,5},{5... | collective-permute-start | bytes 393224 | tf_op jit(solution)/shard_map/ppermute | solution.py:203

commit v3 on v2

v3 whole, which is shorter than its diff:
```python
import functools

import jax
import jax.numpy as jnp
from jax import lax
from jax.experimental import pallas as pl
from jax.experimental.pallas import tpu as pltpu
from jax.sharding import PartitionSpec as P

inflation = 4.0
HIGHEST = lax.Precision.HIGHEST
VMEM = pl.BlockSpec(memory_space=pltpu.VMEM)
SMEM = pl.BlockSpec(memory_space=pltpu.SMEM)


HBM = pl.BlockSpec(memory_space=pltpu.HBM)


def f32(*shape):
    return jax.ShapeDtypeStruct(shape, jnp.float32)


def call(kernel, name, outs, specs, args, scratch=(), flops=0, out_specs=None, aliases={}):
    moved = sum(4 * a.size for a in args)
    return pl.pallas_call(
        kernel,
        out_shape=outs,
        in_specs=specs,
        out_specs=jax.tree.map(lambda _: VMEM, outs) if out_specs is None else out_specs,
        scratch_shapes=scratch,
        input_output_aliases=aliases,
        compiler_params=pltpu.CompilerParams(vmem_limit_bytes=20 << 20),
        cost_estimate=pl.CostEstimate(flops=flops, bytes_accessed=moved, transcendentals=0),
        name=name,
    )(*args)


def halo_routes(count_x, count_y):
    def flat(i, j):
        return i * count_y + j

    def turn(i, j):
        ahead = j + 1 if i % 2 == 0 else j - 1
        return (i, ahead) if 0 <= ahead < count_y else (i ^ 1, j)

    places = [(i, j) for i in range(count_x) for j in range(count_y)]
    right = [(flat(i, j), flat((i + 1) % count_x, j)) for i, j in places]
    along = [(flat(i, j), flat(*turn(i, j))) for i, j in places]
    return [right, back(right), along, back(along)]


def back(route):
    return [(b, a) for a, b in route]


def exchange(faces):
    routes = halo_routes(lax.axis_size("gx"), lax.axis_size("gy"))
    return [lax.ppermute(face, ("gx", "gy"), route) for face, route in zip(faces, routes)]


def border(rows, wanted):
    span_x, span_y = rows
    return [
        (x, y)
        for x in range(span_x)
        for y in range(span_y)
        if (x in (0, span_x - 1) or y in (0, span_y - 1)) == wanted
    ]


def is_even():
    return lax.rem(lax.axis_index("gx"), 2) == 0


def store_faces(field_ref, rows, put):
    span_x, span_y = rows
    even = is_even()
    for y in range(span_y):
        put(0, y, field_ref[(span_x - 1) * span_y + y])
        put(1, y, field_ref[y])
    for x in range(span_x):
        for route, at in (
            (2, jnp.where(even, span_y - 1, 0)),
            (3, jnp.where(even, 0, span_y - 1)),
        ):
            put(route, x, field_ref[x * span_y + at])


def conductivity(rows, cells, log_ref, columns_ref, h_ref):
    depth, members = log_ref.shape[1:]
    columns = columns_ref[...]
    for x, y in cells:
        cell = x * rows[1] + y
        base = jnp.broadcast_to(columns[:, cell : cell + 1], (depth, members))
        h_ref[cell] = base * jnp.exp(log_ref[cell])


def prepare(rows, t_hbm, log_hbm, code_hbm, rock_hbm, *rest):
    t_ref, log_ref, h_ref, columns_ref, *face_refs, turned, code_ref, rock_ref, sems = rest
    span_x, span_y = rows
    depth = t_ref.shape[1]
    copies = [
        pltpu.make_async_copy(source, target, sems.at[n])
        for n, (source, target) in enumerate(
            ((code_hbm, code_ref), (rock_hbm, rock_ref), (log_hbm, log_ref), (t_hbm, t_ref))
        )
    ]
    for copy in copies:
        copy.start()
    turned[...] = jnp.zeros_like(turned)
    copies[0].wait()
    copies[1].wait()
    for x in range(span_x):
        code = code_ref[x]
        base = jnp.zeros(code.shape, jnp.float32)
        for level in range(rock_ref.shape[0]):
            base = jnp.where(code == level, 0.5 * rock_ref[level], base)
        turned[x * span_y : (x + 1) * span_y, :depth] = base
    columns_ref[...] = jnp.transpose(turned[...])[:depth]
    copies[2].wait()
    conductivity(rows, border(rows, True), log_ref, columns_ref, h_ref)

    def put(field):
        def store(n, k, layer):
            face_refs[n][field, k] = layer

        return store

    store_faces(h_ref, rows, put(1))
    copies[3].wait()
    store_faces(t_ref, rows, put(0))


def advance(rows, cells, courant_ref, u_ref, h_ref, u_faces, h_faces, write):
    span_x, span_y = rows
    shape = u_ref.shape[1:]
    depth = shape[0]
    level = lax.broadcasted_iota(jnp.int32, shape, 0)
    courant = jnp.zeros(shape, jnp.float32)
    for z in range(depth):
        courant = jnp.where(level == z, courant_ref[z], courant)
    even = is_even()

    def beyond(faces, axis, after, k):
        name = ("gx", "gy")[axis]
        edge = lax.axis_index(name) == (lax.axis_size(name) - 1 if after else 0)
        if axis == 0:
            layer = faces(1 if after else 0, k)
        else:
            layer = jnp.where(even == after, faces(3, k), faces(2, k))
        return jnp.where(edge, 0.0, layer)

    def at(ref, faces, x, y):
        if x < 0 or x == span_x:
            return beyond(faces, 0, x > 0, y)
        if y < 0 or y == span_y:
            return beyond(faces, 1, y > 0, x)
        return ref[x * span_y + y]

    before, from_before = None, None
    for x, y in cells:
        u, h = u_ref[x * span_y + y], h_ref[x * span_y + y]

        def flow(i, j):
            step = at(u_ref, u_faces, i, j) - u
            return step, (h + at(h_ref, h_faces, i, j)) * step

        rise = jnp.where(level == depth - 1, 0.0, pltpu.roll(u, depth - 1, 0)) - u
        lift = (h + jnp.where(level == depth - 1, 0.0, pltpu.roll(h, depth - 1, 0))) * rise
        sink = jnp.where(level == 0, h * u, pltpu.roll(lift, 1, 0))
        west, from_west = flow(x - 1, y)
        from_east = flow(x + 1, y)[1]
        from_north = flow(x, y + 1)[1]
        from_south = from_before if before == (x, y - 1) else flow(x, y - 1)[1]
        before, from_before = (x, y), -from_north
        change = (from_east + from_west) + (from_north + from_south) + (lift - sink)
        write(x * span_y + y, u + change + courant * west)


def into(ref):
    def write(cell, value):
        ref[cell] = value

    return write


def middle_inside(rows, courant_ref, t_ref, log_ref, columns_ref, outer_ref, h_ref, middle_ref):
    del outer_ref
    inside = border(rows, False)
    conductivity(rows, inside, log_ref, columns_ref, h_ref)
    advance(rows, inside, courant_ref, t_ref, h_ref, None, None, into(middle_ref))


def middle_border(rows, courant_ref, t_ref, h_ref, *rest):
    got, middle_ref, face_refs = rest[:4], rest[5], rest[6:]
    advance(
        rows, border(rows, True), courant_ref, t_ref, h_ref,
        lambda n, k: got[n][0, k], lambda n, k: got[n][1, k], into(middle_ref),
    )

    def put(n, k, layer):
        face_refs[n][k] = layer

    store_faces(middle_ref, rows, put)


def final_inside(rows, courant_ref, u_ref, h_ref, final_ref):
    advance(rows, border(rows, False), courant_ref, u_ref, h_ref, None, None, into(final_ref))


def observe(rows, courant_ref, cells_ref, reading_ref, factor_ref, u_ref, h_ref, *rest):
    got_u, got_h, final_ref, scaled_ref = rest[:4], rest[4:8], rest[9], rest[10]
    depth = u_ref.shape[1]
    advance(
        rows, border(rows, True), courant_ref, u_ref, h_ref,
        lambda n, k: got_u[n][k], lambda n, k: got_h[n][1, k], into(final_ref),
    )
    for j in range(scaled_ref.shape[0]):
        cell = cells_ref[j]
        row = final_ref[lax.div(cell, depth), pl.ds(lax.rem(cell, depth), 1), :]
        scaled_ref[j : j + 1, :] = (row - reading_ref[j]) * factor_ref[j]


def modulo(value, divisor):
    quotient = (value.astype(jnp.float32) * (1.0 / divisor)).astype(jnp.int32)
    rest = value - quotient * divisor
    rest = jnp.where(rest < 0, rest + divisor, rest)
    return jnp.where(rest >= divisor, rest - divisor, rest)


def perturbation(obs_index, random_starters):
    first = random_starters * 7919 % 65521
    second = obs_index * 331 % 65521
    hashed = modulo(
        first[None, :] * (second[:, None] % 32749) + first[None, :] + second[:, None], 65521
    )
    uniform_value = (hashed.astype(jnp.float32) + 0.5) / 65521.0
    return jnp.sqrt(3.0) * (2.0 * uniform_value - 1.0)


def plan_exchange(count_x, count_y, rows, limit):
    def route(move):
        return [
            (i * count_y + j, a * count_y + b)
            for i in range(count_x)
            for j in range(count_y)
            for a, b in [move(i, j)]
        ]

    def shifted(axis, i, j, step):
        return (i ^ step, j) if axis == "gx" else (i, j ^ step)

    def across(axis, step):
        def move(i, j):
            at = i if axis == "gx" else j
            a, b = shifted(axis, i, j, step)
            return (a, b) if at < at ^ step else (a ^ 1, b)

        return route(move)

    def around(axis, low, high):
        def move(i, j):
            at = i if axis == "gx" else j
            step = low if bool(at & low) == bool(at & high) else high
            return shifted(axis, i, j, step)

        return route(move)

    gathers, sums = [], []
    for axis, count in (("gy", count_y), ("gx", count_x)):
        bits = [1 << b for b in range(count.bit_length() - 1)]
        while bits:
            if len(bits) > 1 and rows * 4 <= limit:
                high, low = bits.pop(), bits.pop()
                ring = around(axis, low, high)
                gathers.append([across(axis, low | high), ring, back(ring)])
                rows *= 4
                continue
            step = bits.pop()
            swap = route(functools.partial(shifted, axis, step=step))
            if rows * 2 <= limit:
                gathers.append([swap])
                rows *= 2
            else:
                sums.append(swap)
    return gathers, sums


def send(block, route):
    return lax.ppermute(block, ("gx", "gy"), route)


def pack(*refs):
    start = 0
    for ref in refs[:-1]:
        refs[-1][start : start + ref.shape[0], :] = ref[...]
        start += ref.shape[0]


def gather_blocks(block, gathers, devices):
    pieces, owners = [block], [[d] for d in range(devices)]
    for routes in gathers:
        if len(routes) > 1 and len(pieces) > 1:
            rows = sum(piece.shape[0] for piece in pieces)
            pieces = [
                call(pack, "pack", f32(rows, block.shape[1]), [VMEM] * len(pieces), pieces)
            ]
        pieces = pieces + [send(piece, route) for route in routes for piece in pieces]
        held = [list(own) for own in owners]
        for route in routes:
            for source, target in route:
                held[target] += owners[source]
        owners = held
    return pieces, owners


def product(a, b, over_a=1, over_b=0):
    return lax.dot_general(
        a, b, (((over_a,), (over_b,)), ((), ())), precision=HIGHEST,
        preferred_element_type=jnp.float32,
    )


def inverse(block):
    size = block.shape[0]
    shape = (8, size)
    lane = lax.broadcasted_iota(jnp.int32, shape, 1)
    sub = lax.broadcasted_iota(jnp.int32, shape, 0)
    count = size // 8
    rows = [block[8 * i : 8 * i + 8, :] for i in range(count)]
    for g in range(count):
        first = 8 * g
        inside = (lane >= first) & (lane < first + 8)
        columns = [
            jnp.broadcast_to(rows[g][:, first + q : first + q + 1], shape) for q in range(8)
        ]
        held = jnp.where(inside, jnp.where(lane - first == sub, 1.0, 0.0), rows[g])
        for p in range(8):
            pivot = 1.0 / columns[p][p : p + 1, :]
            for q in range(p + 1, 8):
                scaled = columns[q][p : p + 1, :] * pivot
                columns[q] = jnp.where(sub == p, scaled, columns[q] - columns[p] * scaled)
            scaled = held[p : p + 1, :] * pivot
            held = jnp.where(sub == p, scaled, held - columns[p] * scaled)
        rows[g] = held
        spread = [jnp.broadcast_to(held[q : q + 1, :], shape) for q in range(8)]
        for i in [*range(g + 1, count), *range(g)]:
            left = jnp.where(inside, 0.0, rows[i])
            for q in range(8):
                left -= jnp.broadcast_to(rows[i][:, first + q : first + q + 1], shape) * spread[q]
            rows[i] = left
    return jnp.concatenate(rows, 0)


def products(scale, piece_refs, noise_ref, out_ref):
    scaled = jnp.concatenate([ref[...] for ref in piece_refs])
    members = scaled.shape[1]
    spread = scaled - jnp.sum(scaled, axis=1, keepdims=True) * (1.0 / members)
    misfit = noise_ref[...] - scale * scaled
    out_ref[:, :members] = product(spread, spread, 0, 0)
    out_ref[:, members:] = product(spread, misfit, 0, 0)


def update(scale, sums_ref, log_ref, updated_hbm, weights_ref, held_ref, sems):
    members = weights_ref.shape[0]
    half = members // 2
    diagonal = lax.broadcasted_iota(jnp.int32, (half, half), 0) == lax.broadcasted_iota(
        jnp.int32, (half, half), 1
    )
    shift = jnp.where(diagonal, inflation, 0.0)
    upper = product(inverse(sums_ref[:half, :half] + shift), sums_ref[:half, half:])
    lower = sums_ref[half:, half:] - product(sums_ref[half:, :half], upper)
    second = product(inverse(lower[:, :half] + shift), lower[:, half:])
    first = upper[:, half:] - product(upper[:, :half], second)
    mean = (
        jnp.sum(first, axis=0, keepdims=True) + jnp.sum(second, axis=0, keepdims=True)
    ) * (1.0 / members)
    weights_ref[:half] = (first - mean) * (1.0 / scale)
    weights_ref[half:] = (second - mean) * (1.0 / scale)
    chunk = log_ref.shape[0] // sems.shape[0]
    copies = []
    for n in range(sems.shape[0]):
        part = pl.ds(n * chunk, chunk)
        held_ref[part] = log_ref[part] + product(log_ref[part], weights_ref[...])
        copies.append(pltpu.make_async_copy(held_ref.at[part], updated_hbm.at[part], sems.at[n]))
        copies[-1].start()
    for copy in copies:
        copy.wait()


def smooth(scale, *refs):
    *piece_refs, noise_ref, log_ref, inner_ref, updated_hbm, final_hbm = refs[:-5]
    sums_ref, weights_ref, held_ref, sems, final_sem = refs[-5:]
    keep = pltpu.make_async_copy(inner_ref, final_hbm, final_sem)
    keep.start()
    products(scale, piece_refs, noise_ref, sums_ref)
    update(scale, sums_ref, log_ref, updated_hbm, weights_ref, held_ref, sems)
    keep.wait()


def finish(scale, sums_ref, log_ref, inner_ref, updated_hbm, final_hbm, *scratch):
    weights_ref, held_ref, sems, final_sem = scratch
    keep = pltpu.make_async_copy(inner_ref, final_hbm, final_sem)
    keep.start()
    update(scale, sums_ref, log_ref, updated_hbm, weights_ref, held_ref, sems)
    keep.wait()


def assimilate(scale, pieces, noise, log_rows, final, sums):
    members = noise.shape[1]
    pair = (members, 2 * members)
    outs = (f32(*log_rows.shape), f32(*final.shape))
    scratch = [
        pltpu.VMEM((members, members), jnp.float32),
        pltpu.VMEM(log_rows.shape, jnp.float32),
        pltpu.SemaphoreType.DMA((4,)),
        pltpu.SemaphoreType.DMA,
    ]
    if not sums:
        args = [*pieces, noise, log_rows, final]
        return call(
            functools.partial(smooth, scale), "smooth", outs, [VMEM] * len(args), args,
            scratch=[pltpu.VMEM(pair, jnp.float32), *scratch], flops=10**9,
            out_specs=(HBM, HBM),
        )
    args = [*pieces, noise]
    total = call(
        lambda *refs: products(scale, refs[:-2], *refs[-2:]), "products", f32(*pair),
        [VMEM] * len(args), args, flops=10**9,
    )
    for route in sums:
        total = total + send(total, route)
    args = [total, log_rows, final]
    return call(
        functools.partial(finish, scale), "finish", outs, [VMEM] * 3, args,
        scratch=scratch, flops=10**9, out_specs=(HBM, HBM),
    )


def shards(
    initial_thermal_state,
    logarithmic_diffusivity,
    rock_class_code,
    rock_class_diffusivity,
    advection_courant,
    probe_locations,
    observed_readings,
    probe_noise_deviation,
    random_starters,
):
    span_x, span_y, depth, members = initial_thermal_state.shape
    rows = (span_x, span_y)
    cells = span_x * span_y
    temperature = initial_thermal_state.reshape(cells, depth, members)
    log_cond = logarithmic_diffusivity.reshape(cells, depth, members)
    tile = f32(cells, depth, members)
    faces = [(span_y, depth, members)] * 2 + [(span_x, depth, members)] * 2
    levels = rock_class_diffusivity.shape
    columns = -(-cells // 128) * 128
    temperature, log_cond, outer, base, *sent = call(
        functools.partial(prepare, rows), "prepare",
        (tile, tile, tile, f32(depth, columns), *(f32(2, *face) for face in faces)),
        [HBM] * 4,
        [temperature, log_cond, rock_class_code, rock_class_diffusivity],
        scratch=[
            pltpu.VMEM((columns, 128), jnp.float32),
            pltpu.VMEM(rock_class_code.shape, jnp.int32),
            pltpu.SMEM(levels, jnp.float32),
            pltpu.SemaphoreType.DMA((4,)),
        ],
    )
    got = exchange(sent)
    half_cond, middle = call(
        functools.partial(middle_inside, rows), "middle_inside", (tile, tile),
        [SMEM] + [VMEM] * 4,
        [advection_courant, temperature, log_cond, base, outer],
        flops=10**7, aliases={4: 0},
    )
    middle, *sent = call(
        functools.partial(middle_border, rows), "middle_border",
        (tile, *(f32(*face) for face in faces)),
        [SMEM] + [VMEM] * 7,
        [advection_courant, temperature, half_cond, *got, middle],
        flops=10**7, aliases={7: 0},
    )
    got_middle = exchange(sent)
    final = call(
        functools.partial(final_inside, rows), "final_inside", tile,
        [SMEM] + [VMEM] * 2, [advection_courant, middle, half_cond], flops=10**7,
    )
    scale = (members - 1) ** 0.5
    obs_count = probe_locations.shape[0]
    final, scaled = call(
        functools.partial(observe, rows), "observe", (tile, f32(obs_count, members)),
        [SMEM] * 4 + [VMEM] * 11,
        [
            advection_courant, probe_locations, observed_readings,
            1.0 / (probe_noise_deviation * scale), middle, half_cond, *got_middle, *got, final,
        ],
        flops=10**7, aliases={14: 0},
    )
    count_x, count_y = lax.axis_size("gx"), lax.axis_size("gy")
    gathers, sums = plan_exchange(count_x, count_y, obs_count, 4 * members)
    pieces, owners = gather_blocks(scaled, gathers, count_x * count_y)
    owner = jnp.asarray(owners, jnp.int32)[lax.axis_index(("gx", "gy"))]
    obs_index = (
        owner[:, None] * obs_count + jnp.arange(obs_count, dtype=jnp.int32)[None, :]
    ).reshape(-1)
    noise = inflation**0.5 * perturbation(obs_index, random_starters)
    updated, final = assimilate(
        scale, pieces, noise, log_cond.reshape(-1, members), final, sums
    )
    shape = initial_thermal_state.shape
    return (final.reshape(shape), updated.reshape(shape))


def solution(mesh):
    placed = (
        P("gx", "gy", None, None),
        P("gx", "gy", None, None),
        P("gx", "gy", None),
        P(),
        P(),
        P(("gx", "gy")),
        P(("gx", "gy")),
        P(("gx", "gy")),
        P(),
    )
    return jax.shard_map(
        shards,
        mesh=mesh,
        in_specs=placed,
        out_specs=(P("gx", "gy", None, None), P("gx", "gy", None, None)),
        check_vma=False,
    )
```

time: 68.1 us -> 63.1 us (0.927)
  starting transfers between devices: 26.5 us -> 17.1 us
  waiting for transfers between devices: 16.7 us -> 18.4 us
  Pallas kernels: 18.7 us -> 20.2 us
    ppermute x18, starting transfers between devices: 26.5 us -> 17.1 us  [the longest x8 9.99 us: exchange(): lax.ppermute(face, ('gx', 'gy'), route)]
    ppermute x18, waiting for transfers between devices: 16.7 us -> 18.4 us  [the longest x10 10.6 us: send(): return lax.ppermute(block, ('gx', 'gy'), route)]
    pallas_call x5 -> x7, Pallas kernels: 18.7 us -> 20.2 us  [call(): pl.pallas_call(kernel, out_shape=outs, in_specs=specs, out_specs=jax.tree...]
    mul x1, other arithmetic: 0.01 us -> 0.69 us  [shards(): owner[:, None] * obs_count + jnp.arange(obs_count, dtype=jnp.int32)[None, :]]
    unnamed x22 -> x18, local copies, waits for them, and re-layouts: 3.89 us -> 4.53 us
  transfers between devices with their start and end apart: 18 -> 18, of which waited for: 8 -> 12; matrix products, arithmetic and copies ran while one was open for 2% -> 3% of each run, Pallas kernels for 0% -> 4%
where the time goes in v3:
time: 63.1 us; the launch traced here: 62.7 us
  Pallas kernels  20.2 us (32%)
  waiting for transfers between devices  18.4 us (29%)
  starting transfers between devices  17.1 us (27%)
  local copies, waits for them, and re-layouts  4.6 us (7%)
  other arithmetic  1.56 us (2%)
  between operations  0.95 us (2%)
    pallas_call x7, Pallas kernels, call(): pl.pallas_call(kernel, out_shape=outs, in_specs=specs, out_specs=jax.tree...  20.2 us
    ppermute x10, waiting for transfers between devices, send(): return lax.ppermute(block, ('gx', 'gy'), route)  10.6 us
    ppermute x8, starting transfers between devices, exchange(): lax.ppermute(face, ('gx', 'gy'), route)  9.99 us
    ppermute x8, waiting for transfers between devices, exchange(): lax.ppermute(face, ('gx', 'gy'), route)  7.73 us
    ppermute x10, starting transfers between devices, send(): return lax.ppermute(block, ('gx', 'gy'), route)  7.11 us
    unnamed x18, local copies, waits for them, and re-layouts  4.53 us
  transfers between devices with their start and end apart: 18, of which 12 were waited for; matrix products, arithmetic and copies ran while one was open for 3% of the time, Pallas kernels for 4%

profile of v3, /device:TPU:0, one launch (start us, length us, event | category | flops | bytes accessed | tf_op | source)
XLA Modules:
  0.0 62.7 jit_solution(13380727982555955800)
XLA Ops:
  0.6 0.6 %copy-done.4 = f32[8]{0:T(128)S(1)} copy-done((f32[8]{0:T(128)S(1)}, f32[8]{0:T(128)}, u32[]{:S(2)}) %copy-start.4) | copy-done | bytes 56
  1.3 1.2 %copy-done = f32[8,8,16,256]{3,2,1,0:T(8,128)S(1)} copy-done((f32[8,8,16,256]{3,2,1,0:T(8,128)S(1)}, f32[8,8,16,256]{3,2,1,0:T(8,128)}, u32[]{:S(2)}) %copy-start) | copy-done | bytes 1048600
  2.5 1.2 %copy-done.1 = f32[8,8,16,256]{3,2,1,0:T(8,128)S(1)} copy-done((f32[8,8,16,256]{3,2,1,0:T(8,128)S(1)}, f32[8,8,16,256]{3,2,1,0:T(8,128)}, u32[]{:S(2)}) %copy-start.1) | copy-done | bytes 1048600
  3.7 0.8 %copy-done.2 = s32[8,8,16]{2,1,0:T(8,128)S(1)} copy-done((s32[8,8,16]{2,1,0:T(8,128)S(1)}, s32[8,8,16]{2,1,0:T(8,128)}, u32[]{:S(2)}) %copy-start.2) | copy-done | bytes 4120
  4.5 1.9 %prepare.1 = (f32[64,16,256]{2,1,0:T(8,128)S(1)}, f32[64,16,256]{2,1,0:T(8,128)S(1)}, f32[64,16,256]{2,1,0:T(8,128)S(1)}, f32[16,128]{1,0:T(8,128)S(1)}, f32[2,8...) custom-call(f32[64,16,256]{2,1,0:T(8,128)S(1)} %bitcast.8, ...), custom_call_target="tpu_custom_call" | custom-call | bytes 2101280 | tf_op jit(solution)/shard_map/prepare/pallas_call | solution.py:25
  6.9 2.9 %collective-permute-start.1 = (f32[2,8,16,256]{3,2,1,0:T(8,128)}, f32[2,8,16,256]{3,2,1,0:T(8,128)}, u32[]{:S(2)}, u32[]{:S(2)}) collective-permute-start(f32[2,8,16,256]{3,2,1,0:T(8,128)} %get-tuple-element.27), channel_id=1, source_target_pairs={{4,0},{5,1},{6,2},{7,3},{8,4},{9,5},{10,6},{11,7},{12,8},{13,9},{1... | collective-permute-start | bytes 786440 | tf_op jit(solution)/shard_map/ppermute | solution.py:58
  9.8 2.3 %collective-permute-start.2 = (f32[2,8,16,256]{3,2,1,0:T(8,128)}, f32[2,8,16,256]{3,2,1,0:T(8,128)}, u32[]{:S(2)}, u32[]{:S(2)}) collective-permute-start(f32[2,8,16,256]{3,2,1,0:T(8,128)} %get-tuple-element.28), channel_id=1, source_target_pairs={{0,1},{1,2},{2,3},{3,7},{4,0},{5,4},{6,5},{7,6},{8,9},{9,10},{10,1... | collective-permute-start | bytes 786440 | tf_op jit(solution)/shard_map/ppermute | solution.py:58
  12.1 0.7 %multiply_bitcast_fusion = s32[32]{0:T(128)S(1)} fusion(s32[32,32]{1,0:T(8,128)} %constant.73.clone, s32[]{:T(128)S(6)} %select_n.42), kind=kLoop, calls=%fused_computation.11 | loop fusion | flops 32 | bytes 260 | tf_op jit(solution)/shard_map/mul | solution.py:507
  13.0 0.7 %copy-done.3 = f32[16]{0:T(128)S(1)} copy-done((f32[16]{0:T(128)S(1)}, f32[16]{0:T(128)}, u32[]{:S(2)}) %copy-start.3) | copy-done | bytes 88
  13.6 1.2 %middle_inside.1 = (f32[64,16,256]{2,1,0:T(8,128)S(1)}, f32[64,16,256]{2,1,0:T(8,128)S(1)}) custom-call(f32[16]{0:T(128)S(1)} %copy-done.3, f32[64,16,256]{2,1,0:T(8,128)S(1)} %get-tuple-element.21.t_ref, f32[64,16,256]{2,1,0:T(8,128)S(1)} %get-tuple-element.22.log_ref, ...), custom_call_target="tpu_custom_call", output_to_operand_aliasing={{0}: (4, {})} | custom-call | flops 10000000 | bytes 3153984 | tf_op jit(solution)/shard_map/middle_inside/pallas_call | solution.py:25
  14.9 0.9 %collective-permute-done.1.rest_1_.rest_5_ = f32[2,8,16,256]{3,2,1,0:T(8,128)} collective-permute-done((f32[2,8,16,256]{3,2,1,0:T(8,128)}, f32[2,8,16,256]{3,2,1,0:T(8,128)}, u32[]{:S(2)}, u32[]{:S(2)}) %collective-permute-start.1) | collective-permute-done | bytes 262176 | tf_op jit(solution)/shard_map/ppermute | solution.py:58
  15.8 1.5 %collective-permute-done.2.rest_2_.rest_6_ = f32[2,8,16,256]{3,2,1,0:T(8,128)} collective-permute-done((f32[2,8,16,256]{3,2,1,0:T(8,128)}, f32[2,8,16,256]{3,2,1,0:T(8,128)}, u32[]{:S(2)}, u32[]{:S(2)}) %collective-permute-start.2) | collective-permute-done | bytes 262176 | tf_op jit(solution)/shard_map/ppermute | solution.py:58
  17.3 1.5 %collective-permute-done.3.rest_3_.rest_7_ = f32[2,8,16,256]{3,2,1,0:T(8,128)} collective-permute-done((f32[2,8,16,256]{3,2,1,0:T(8,128)}, f32[2,8,16,256]{3,2,1,0:T(8,128)}, u32[]{:S(2)}, u32[]{:S(2)}) %collective-permute-start.3) | collective-permute-done | bytes 262176 | tf_op jit(solution)/shard_map/ppermute | solution.py:58
  18.8 1.6 %middle_border.1 = (f32[64,16,256]{2,1,0:T(8,128)S(1)}, f32[8,16,256]{2,1,0:T(8,128)S(1)}, f32[8,16,256]{2,1,0:T(8,128)S(1)}, f32[8,16,256]{2,1,0:T(8,128)S(1)}, f32[8,16,256]{2,1,0:T(8,128)S(1)}) custom-call(f32[16]{0:T(128)S(1)} %copy-done.3, f32[64,16,256]{2,1,0:T(8,128)S(1)} %get-tuple-element.21.t_ref, ...), custom_call_target="tpu_custom_call", output_to_operand_aliasing={{0}: (7, {})} | custom-call | flops 10000000 | bytes 4194368 | tf_op jit(solution)/shard_map/middle_border/pallas_call | solution.py:25
  20.5 2.6 %collective-permute-start.5 = (f32[8,16,256]{2,1,0:T(8,128)S(1)}, f32[8,16,256]{2,1,0:T(8,128)S(1)}, u32[]{:S(2)}, u32[]{:S(2)}) collective-permute-start(f32[8,16,256]{2,1,0:T(8,128)S(1)} %get-tuple-element.33), channel_id=1, source_target_pairs={{4,0},{5,1},{6,2},{7,3},{8,4},{9,5},{10,6},{11,7},{12,8},{13,9},{1... | collective-permute-start | bytes 393224 | tf_op jit(solution)/shard_map/ppermute | solution.py:58
  23.1 1.6 %collective-permute-start.6 = (f32[8,16,256]{2,1,0:T(8,128)S(1)}, f32[8,16,256]{2,1,0:T(8,128)S(1)}, u32[]{:S(2)}, u32[]{:S(2)}) collective-permute-start(f32[8,16,256]{2,1,0:T(8,128)S(1)} %get-tuple-element.34), channel_id=1, source_target_pairs={{0,1},{1,2},{2,3},{3,7},{4,0},{5,4},{6,5},{7,6},{8,9},{9,10},{10,1... | collective-permute-start | bytes 393224 | tf_op jit(solution)/shard_map/ppermute | solution.py:58
  24.7 1.1 %final_inside.1.rest_8_ = f32[64,16,256]{2,1,0:T(8,128)S(1)} custom-call(f32[16]{0:T(128)S(1)} %copy-done.3, f32[64,16,256]{2,1,0:T(8,128)S(1)} %get-tuple-element.31.u_ref, f32[64,16,256]{2,1,0:T(8,128)S(1)} %get-tuple-element.25.h_ref), custom_call_target="tpu_custom_call" | custom-call | flops 10000000 | bytes 2097216 | tf_op jit(solution)/shard_map/final_inside/pallas_call | solution.py:25
  26.2 1.0 %collective-permute-done.6.rest_2_ = f32[8,16,256]{2,1,0:T(8,128)S(1)} collective-permute-done((f32[8,16,256]{2,1,0:T(8,128)S(1)}, f32[8,16,256]{2,1,0:T(8,128)S(1)}, u32[]{:S(2)}, u32[]{:S(2)}) %collective-permute-start.6) | collective-permute-done | bytes 131104 | tf_op jit(solution)/shard_map/ppermute | solution.py:58
  27.2 2.4 %collective-permute-done.7.rest_3_ = f32[8,16,256]{2,1,0:T(8,128)S(1)} collective-permute-done((f32[8,16,256]{2,1,0:T(8,128)S(1)}, f32[8,16,256]{2,1,0:T(8,128)S(1)}, u32[]{:S(2)}, u32[]{:S(2)}) %collective-permute-start.7) | collective-permute-done | bytes 131104 | tf_op jit(solution)/shard_map/ppermute | solution.py:58
  29.7 1.7 %observe.1 = (f32[64,16,256]{2,1,0:T(8,128)S(1)}, f32[32,256]{1,0:T(8,128)S(1)}) custom-call(f32[16]{0:T(128)S(1)} %copy-done.3, s32[32]{0:T(128)S(1)} %copy-done.5, f32[32]{0:T(128)S(1)} %copy-done.6, f32[32]{0:T(128)S(1)} %multiply_divide_fusion.factor_ref, f32[64,16,256]{2,1,0:T(8,128)S(1)} %get-tuple-element.31.u_ref, ...), custom_call_target="tpu_custom_call", output_to_operand_aliasing={{0}: (14, {})} | custom-call | flops 10000000 | bytes 4719040 | tf_op jit(solution)/shard_map/observe/pallas_call | solution.py:25
  31.4 2.0 %collective-permute-start.10 = (f32[32,256]{1,0:T(8,128)S(1)}, f32[32,256]{1,0:T(8,128)S(1)}, u32[]{:S(2)}, u32[]{:S(2)}) collective-permute-start(f32[32,256]{1,0:T(8,128)S(1)} %get-tuple-element.36.refs_0_), channel_id=1, source_target_pairs={{1,0},{3,1},{0,2},{2,3},{5,4},{7,5},{4,6},{6,7},{9,8},{11,9},{8,10... | collective-permute-start | bytes 98312 | tf_op jit(solution)/shard_map/ppermute | solution.py:290
  33.4 1.9 %collective-permute-start.8 = (f32[32,256]{1,0:T(8,128)S(1)}, f32[32,256]{1,0:T(8,128)S(1)}, u32[]{:S(2)}, u32[]{:S(2)}) collective-permute-start(f32[32,256]{1,0:T(8,128)S(1)} %get-tuple-element.36.refs_0_), channel_id=1, source_target_pairs={{0,3},{1,2},{2,5},{3,4},{4,7},{5,6},{6,1},{7,0},{8,11},{9,10},{10,... | collective-permute-start | bytes 98312 | tf_op jit(solution)/shard_map/ppermute | solution.py:290
  35.4 3.1 %collective-permute-done.8.refs_1_ = f32[32,256]{1,0:T(8,128)S(1)} collective-permute-done((f32[32,256]{1,0:T(8,128)S(1)}, f32[32,256]{1,0:T(8,128)S(1)}, u32[]{:S(2)}, u32[]{:S(2)}) %collective-permute-start.8) | collective-permute-done | bytes 32800 | tf_op jit(solution)/shard_map/ppermute | solution.py:290
  38.6 1.6 %collective-permute-done.9.refs_2_ = f32[32,256]{1,0:T(8,128)S(1)} collective-permute-done((f32[32,256]{1,0:T(8,128)S(1)}, f32[32,256]{1,0:T(8,128)S(1)}, u32[]{:S(2)}, u32[]{:S(2)}) %collective-permute-start.9) | collective-permute-done | bytes 32800 | tf_op jit(solution)/shard_map/ppermute | solution.py:290
  40.2 0.7 %collective-permute-start.11 = (f32[128,256]{1,0:T(8,128)S(1)}, f32[128,256]{1,0:T(8,128)S(1)}, u32[]{:S(2)}, u32[]{:S(2)}) collective-permute-start(f32[128,256]{1,0:T(8,128)S(1)} %pack.1.refs_0_), channel_id=1, source_target_pairs={{0,24},{1,25},{2,26},{3,27},{4,28},{5,29},{6,30},{7,31},{8,16},{9,... | collective-permute-start | bytes 393224 | tf_op jit(solution)/shard_map/ppermute | solution.py:290
  40.9 2.3 %collective-permute-start.12 = (f32[128,256]{1,0:T(8,128)S(1)}, f32[128,256]{1,0:T(8,128)S(1)}, u32[]{:S(2)}, u32[]{:S(2)}) collective-permute-start(f32[128,256]{1,0:T(8,128)S(1)} %pack.1.refs_0_), channel_id=1, source_target_pairs={{0,8},{1,9},{2,10},{3,11},{4,12},{5,13},{6,14},{7,15},{8,24},{9,25... | collective-permute-start | bytes 393224 | tf_op jit(solution)/shard_map/ppermute | solution.py:290
  43.3 3.0 %collective-permute-done.11.refs_1_ = f32[128,256]{1,0:T(8,128)S(1)} collective-permute-done((f32[128,256]{1,0:T(8,128)S(1)}, f32[128,256]{1,0:T(8,128)S(1)}, u32[]{:S(2)}, u32[]{:S(2)}) %collective-permute-start.11) | collective-permute-done | bytes 131104 | tf_op jit(solution)/shard_map/ppermute | solution.py:290
  46.3 1.8 %collective-permute-done.12.refs_2_ = f32[128,256]{1,0:T(8,128)S(1)} collective-permute-done((f32[128,256]{1,0:T(8,128)S(1)}, f32[128,256]{1,0:T(8,128)S(1)}, u32[]{:S(2)}, u32[]{:S(2)}) %collective-permute-start.12) | collective-permute-done | bytes 131104 | tf_op jit(solution)/shard_map/ppermute | solution.py:290
  48.1 0.6 collective-permute-done.13.refs_3_
  48.7 0.7 %fusion.4.refs_8_ = f32[1024,256]{1,0:T(8,128)S(1)} fusion(s32[1024]{0:T(1024)S(1)} %get-tuple-element.41, s32[1024]{0:T(1024)S(1)} %get-tuple-element.40, s32[256]{0:T(256)S(1)} %and_select_fusion), kind=kLoop, calls=%fused_computation.6 | loop fusion | flops 4980736 | bytes 1057792 | tf_op jit(solution)/shard_map/mul | solution.py:509
  49.4 0.6 collective-permute-done.17.refs_7_
  50.0 12.6 %smooth.1 = (f32[1024,256]{1,0:T(8,128)}, f32[64,16,256]{2,1,0:T(8,128)}) custom-call(f32[128,256]{1,0:T(8,128)S(1)} %pack.1.refs_0_, f32[128,256]{1,0:T(8,128)S(1)} %collective-permute-done.11.refs_1_, f32[128,256]{1,0:T(8,128)S(1)} %collective-permute-done.12.refs_2_, f32[128,256]{1,0:T(8,128)S(1)} %collective-permute-done.13.refs_3_, ...), custom_call_target="tpu_custom_call" | custom-call | flops 1000000000 | bytes 4194304 | tf_op jit(solution)/shard_map/smooth/pallas_call | solution.py:25
  (36 shorter events, 1.3 us)
Async XLA Ops:
  0.6 0.7 %copy-start.4 = (f32[8]{0:T(128)S(1)}, f32[8]{0:T(128)}, u32[]{:S(2)}) copy-start(f32[8]{0:T(128)} %rock_hbm.1) | copy-start | bytes 100
  1.3 1.2 %copy-start = (f32[8,8,16,256]{3,2,1,0:T(8,128)S(1)}, f32[8,8,16,256]{3,2,1,0:T(8,128)}, u32[]{:S(2)}) copy-start(f32[8,8,16,256]{3,2,1,0:T(8,128)} %param.10) | copy-start | bytes 3145732
  2.5 1.2 %copy-start.1 = (f32[8,8,16,256]{3,2,1,0:T(8,128)S(1)}, f32[8,8,16,256]{3,2,1,0:T(8,128)}, u32[]{:S(2)}) copy-start(f32[8,8,16,256]{3,2,1,0:T(8,128)} %param.11) | copy-start | bytes 3145732
  3.7 0.8 %copy-start.2 = (s32[8,8,16]{2,1,0:T(8,128)S(1)}, s32[8,8,16]{2,1,0:T(8,128)}, u32[]{:S(2)}) copy-start(s32[8,8,16]{2,1,0:T(8,128)} %code_hbm.1) | copy-start | bytes 12292
  6.4 8.5 %collective-permute-start = (f32[2,8,16,256]{3,2,1,0:T(8,128)}, f32[2,8,16,256]{3,2,1,0:T(8,128)S(1)}, u32[]{:S(2)}, u32[]{:S(2)}) collective-permute-start(f32[2,8,16,256]{3,2,1,0:T(8,128)} %get-tuple-element.26), channel_id=1, source_target_pairs={{0,4},{1,5},{2,6},{3,7},{4,8},{5,9},{6,10},{7,11},{8,12},{9,13},{1... | collective-permute-start | bytes 786440 | tf_op jit(solution)/shard_map/ppermute | solution.py:58
  6.9 8.9 %collective-permute-start.1 = (f32[2,8,16,256]{3,2,1,0:T(8,128)}, f32[2,8,16,256]{3,2,1,0:T(8,128)}, u32[]{:S(2)}, u32[]{:S(2)}) collective-permute-start(f32[2,8,16,256]{3,2,1,0:T(8,128)} %get-tuple-element.27), channel_id=1, source_target_pairs={{4,0},{5,1},{6,2},{7,3},{8,4},{9,5},{10,6},{11,7},{12,8},{13,9},{1... | collective-permute-start | bytes 786440 | tf_op jit(solution)/shard_map/ppermute | solution.py:58
  9.8 7.5 %collective-permute-start.2 = (f32[2,8,16,256]{3,2,1,0:T(8,128)}, f32[2,8,16,256]{3,2,1,0:T(8,128)}, u32[]{:S(2)}, u32[]{:S(2)}) collective-permute-start(f32[2,8,16,256]{3,2,1,0:T(8,128)} %get-tuple-element.28), channel_id=1, source_target_pairs={{0,1},{1,2},{2,3},{3,7},{4,0},{5,4},{6,5},{7,6},{8,9},{9,10},{10,1... | collective-permute-start | bytes 786440 | tf_op jit(solution)/shard_map/ppermute | solution.py:58
  12.1 6.7 %collective-permute-start.3 = (f32[2,8,16,256]{3,2,1,0:T(8,128)}, f32[2,8,16,256]{3,2,1,0:T(8,128)}, u32[]{:S(2)}, u32[]{:S(2)}) collective-permute-start(f32[2,8,16,256]{3,2,1,0:T(8,128)} %get-tuple-element.29), channel_id=1, source_target_pairs={{1,0},{2,1},{3,2},{7,3},{0,4},{4,5},{5,6},{6,7},{9,8},{10,9},{11,1... | collective-permute-start | bytes 786440 | tf_op jit(solution)/shard_map/ppermute | solution.py:58
  13.0 0.7 %copy-start.3 = (f32[16]{0:T(128)S(1)}, f32[16]{0:T(128)}, u32[]{:S(2)}) copy-start(f32[16]{0:T(128)} %courant_ref.7) | copy-start | bytes 196
  20.4 5.8 %collective-permute-start.4 = (f32[8,16,256]{2,1,0:T(8,128)S(1)}, f32[8,16,256]{2,1,0:T(8,128)S(1)}, u32[]{:S(2)}, u32[]{:S(2)}) collective-permute-start(f32[8,16,256]{2,1,0:T(8,128)S(1)} %get-tuple-element.32), channel_id=1, source_target_pairs={{0,4},{1,5},{2,6},{3,7},{4,8},{5,9},{6,10},{7,11},{8,12},{9,13},{1... | collective-permute-start | bytes 393224 | tf_op jit(solution)/shard_map/ppermute | solution.py:58
  20.5 5.7 %collective-permute-start.5 = (f32[8,16,256]{2,1,0:T(8,128)S(1)}, f32[8,16,256]{2,1,0:T(8,128)S(1)}, u32[]{:S(2)}, u32[]{:S(2)}) collective-permute-start(f32[8,16,256]{2,1,0:T(8,128)S(1)} %get-tuple-element.33), channel_id=1, source_target_pairs={{4,0},{5,1},{6,2},{7,3},{8,4},{9,5},{10,6},{11,7},{12,8},{13,9},{1... | collective-permute-start | bytes 393224 | tf_op jit(solution)/shard_map/ppermute | solution.py:58
  23.1 1.6 %copy-start.8 = (f32[32]{0:T(128)S(1)}, f32[32]{0:T(128)}, u32[]{:S(2)}) copy-start(f32[32]{0:T(128)} %param.17) | copy-start | bytes 388
  23.1 4.1 %collective-permute-start.6 = (f32[8,16,256]{2,1,0:T(8,128)S(1)}, f32[8,16,256]{2,1,0:T(8,128)S(1)}, u32[]{:S(2)}, u32[]{:S(2)}) collective-permute-start(f32[8,16,256]{2,1,0:T(8,128)S(1)} %get-tuple-element.34), channel_id=1, source_target_pairs={{0,1},{1,2},{2,3},{3,7},{4,0},{5,4},{6,5},{7,6},{8,9},{9,10},{10,1... | collective-permute-start | bytes 393224 | tf_op jit(solution)/shard_map/ppermute | solution.py:58
  24.7 5.0 %collective-permute-start.7 = (f32[8,16,256]{2,1,0:T(8,128)S(1)}, f32[8,16,256]{2,1,0:T(8,128)S(1)}, u32[]{:S(2)}, u32[]{:S(2)}) collective-permute-start(f32[8,16,256]{2,1,0:T(8,128)S(1)} %get-tuple-element.35), channel_id=1, source_target_pairs={{1,0},{2,1},{3,2},{7,3},{0,4},{4,5},{5,6},{6,7},{9,8},{10,9},{11,1... | collective-permute-start | bytes 393224 | tf_op jit(solution)/shard_map/ppermute | solution.py:58
  24.7 5.0 %copy-start.5 = (s32[32]{0:T(128)S(1)}, s32[32]{0:T(128)}, u32[]{:S(2)}) copy-start(s32[32]{0:T(128)} %cells_ref.1) | copy-start | bytes 388
  24.7 4.9 %copy-start.6 = (f32[32]{0:T(128)S(1)}, f32[32]{0:T(128)}, u32[]{:S(2)}) copy-start(f32[32]{0:T(128)} %reading_ref.1) | copy-start | bytes 388
  31.4 4.0 %collective-permute-start.10 = (f32[32,256]{1,0:T(8,128)S(1)}, f32[32,256]{1,0:T(8,128)S(1)}, u32[]{:S(2)}, u32[]{:S(2)}) collective-permute-start(f32[32,256]{1,0:T(8,128)S(1)} %get-tuple-element.36.refs_0_), channel_id=1, source_target_pairs={{1,0},{3,1},{0,2},{2,3},{5,4},{7,5},{4,6},{6,7},{9,8},{11,9},{8,10... | collective-permute-start | bytes 98312 | tf_op jit(solution)/shard_map/ppermute | solution.py:290
  33.4 5.1 %collective-permute-start.8 = (f32[32,256]{1,0:T(8,128)S(1)}, f32[32,256]{1,0:T(8,128)S(1)}, u32[]{:S(2)}, u32[]{:S(2)}) collective-permute-start(f32[32,256]{1,0:T(8,128)S(1)} %get-tuple-element.36.refs_0_), channel_id=1, source_target_pairs={{0,3},{1,2},{2,5},{3,4},{4,7},{5,6},{6,1},{7,0},{8,11},{9,10},{10,... | collective-permute-start | bytes 98312 | tf_op jit(solution)/shard_map/ppermute | solution.py:290
  35.4 4.8 %collective-permute-start.9 = (f32[32,256]{1,0:T(8,128)S(1)}, f32[32,256]{1,0:T(8,128)S(1)}, u32[]{:S(2)}, u32[]{:S(2)}) collective-permute-start(f32[32,256]{1,0:T(8,128)S(1)} %get-tuple-element.36.refs_0_), channel_id=1, source_target_pairs={{0,1},{1,3},{2,0},{3,2},{4,5},{5,7},{6,4},{7,6},{8,9},{9,11},{10,8... | collective-permute-start | bytes 98312 | tf_op jit(solution)/shard_map/ppermute | solution.py:290
  35.4 7.8 %copy-start.7 = (s32[256]{0:T(256)S(1)}, s32[256]{0:T(256)}, u32[]{:S(2)}) copy-start(s32[256]{0:T(256)} %param.18) | copy-start | bytes 3076
  40.2 6.1 %collective-permute-start.11 = (f32[128,256]{1,0:T(8,128)S(1)}, f32[128,256]{1,0:T(8,128)S(1)}, u32[]{:S(2)}, u32[]{:S(2)}) collective-permute-start(f32[128,256]{1,0:T(8,128)S(1)} %pack.1.refs_0_), channel_id=1, source_target_pairs={{0,24},{1,25},{2,26},{3,27},{4,28},{5,29},{6,30},{7,31},{8,16},{9,... | collective-permute-start | bytes 393224 | tf_op jit(solution)/shard_map/ppermute | solution.py:290
  40.9 7.2 %collective-permute-start.12 = (f32[128,256]{1,0:T(8,128)S(1)}, f32[128,256]{1,0:T(8,128)S(1)}, u32[]{:S(2)}, u32[]{:S(2)}) collective-permute-start(f32[128,256]{1,0:T(8,128)S(1)} %pack.1.refs_0_), channel_id=1, source_target_pairs={{0,8},{1,9},{2,10},{3,11},{4,12},{5,13},{6,14},{7,15},{8,24},{9,25... | collective-permute-start | bytes 393224 | tf_op jit(solution)/shard_map/ppermute | solution.py:290
  43.2 5.4 %collective-permute-start.13 = (f32[128,256]{1,0:T(8,128)S(1)}, f32[128,256]{1,0:T(8,128)S(1)}, u32[]{:S(2)}, u32[]{:S(2)}) collective-permute-start(f32[128,256]{1,0:T(8,128)S(1)} %pack.1.refs_0_), channel_id=1, source_target_pairs={{8,0},{9,1},{10,2},{11,3},{12,4},{13,5},{14,6},{15,7},{24,8},{25,9... | collective-permute-start | bytes 393224 | tf_op jit(solution)/shard_map/ppermute | solution.py:290
  43.3 6.1 %collective-permute-start.14 = (f32[128,256]{1,0:T(8,128)S(1)}, f32[128,256]{1,0:T(8,128)S(1)}, u32[]{:S(2)}, u32[]{:S(2)}) collective-permute-start(f32[128,256]{1,0:T(8,128)S(1)} %pack.1.refs_0_), channel_id=1, source_target_pairs={{0,4},{1,5},{2,6},{3,7},{4,0},{5,1},{6,2},{7,3},{8,12},{9,13},{10,... | collective-permute-start | bytes 393224 | tf_op jit(solution)/shard_map/ppermute | solution.py:290
  46.3 3.1 %collective-permute-start.15 = (f32[128,256]{1,0:T(8,128)S(1)}, f32[128,256]{1,0:T(8,128)S(1)}, u32[]{:S(2)}, u32[]{:S(2)}) collective-permute-start(f32[128,256]{1,0:T(8,128)S(1)} %collective-permute-done.11.refs_1_), channel_id=1, source_target_pairs={{0,4},{1,5},{2,6},{3,7},{4,0},{5,1},{6,2},{7,3},{8,12},{9,13},{10,... | collective-permute-start | bytes 393224 | tf_op jit(solution)/shard_map/ppermute | solution.py:290
  48.1 1.4 %collective-permute-start.16 = (f32[128,256]{1,0:T(8,128)S(1)}, f32[128,256]{1,0:T(8,128)S(1)}, u32[]{:S(2)}, u32[]{:S(2)}) collective-permute-start(f32[128,256]{1,0:T(8,128)S(1)} %collective-permute-done.12.refs_2_), channel_id=1, source_target_pairs={{0,4},{1,5},{2,6},{3,7},{4,0},{5,1},{6,2},{7,3},{8,12},{9,13},{10,... | collective-permute-start | bytes 393224 | tf_op jit(solution)/shard_map/ppermute | solution.py:290
  48.7 1.3 %collective-permute-start.17 = (f32[128,256]{1,0:T(8,128)S(1)}, f32[128,256]{1,0:T(8,128)S(1)}, u32[]{:S(2)}, u32[]{:S(2)}) collective-permute-start(f32[128,256]{1,0:T(8,128)S(1)} %collective-permute-done.13.refs_3_), channel_id=1, source_target_pairs={{0,4},{1,5},{2,6},{3,7},{4,0},{5,1},{6,2},{7,3},{8,12},{9,13},{10,... | collective-permute-start | bytes 393224 | tf_op jit(solution)/shard_map/ppermute | solution.py:290

commit v4 on v3

--- a/solution.py
+++ b/solution.py
@@ -9,6 +9,7 @@
 
 inflation = 4.0
 HIGHEST = lax.Precision.HIGHEST
+UPDATE = lax.Precision.HIGH
 VMEM = pl.BlockSpec(memory_space=pltpu.VMEM)
 SMEM = pl.BlockSpec(memory_space=pltpu.SMEM)
 
@@ -314,51 +315,64 @@
     return pieces, owners
 
 
-def product(a, b, over_a=1, over_b=0):
+def product(a, b, over_a=1, over_b=0, precision=HIGHEST):
     return lax.dot_general(
-        a, b, (((over_a,), (over_b,)), ((), ())), precision=HIGHEST,
+        a, b, (((over_a,), (over_b,)), ((), ())), precision=precision,
         preferred_element_type=jnp.float32,
     )
 
 
-def inverse(block):
-    size = block.shape[0]
-    shape = (8, size)
+def tree_sum(terms):
+    while len(terms) > 1:
+        terms = [sum(terms[n : n + 2]) for n in range(0, len(terms), 2)]
+    return terms[0]
+
+
+def factors(block):
+    size, group = block.shape[0], 16
+    shape = (group, size)
     lane = lax.broadcasted_iota(jnp.int32, shape, 1)
     sub = lax.broadcasted_iota(jnp.int32, shape, 0)
-    count = size // 8
-    rows = [block[8 * i : 8 * i + 8, :] for i in range(count)]
+    count = size // group
+    rows = [block[group * i : group * (i + 1), :] for i in range(count)]
+    left, right = [], []
+
+    def spread(values, at):
+        return jnp.broadcast_to(values[:, at : at + 1], shape)
+
     for g in range(count):
-        first = 8 * g
-        inside = (lane >= first) & (lane < first + 8)
-        columns = [
-            jnp.broadcast_to(rows[g][:, first + q : first + q + 1], shape) for q in range(8)
-        ]
-        held = jnp.where(inside, jnp.where(lane - first == sub, 1.0, 0.0), rows[g])
-        for p in range(8):
+        first = group * g
+        inside = (lane >= first) & (lane < first + group)
+        unit = jnp.where(lane - first == sub, 1.0, 0.0)
+        columns = [spread(rows[g], first + q) for q in range(group)]
+        held = jnp.where(inside, unit, rows[g])
+        left.append(jnp.where(lane < first, rows[g], unit))
+        for p in range(group):
             pivot = 1.0 / columns[p][p : p + 1, :]
-            for q in range(p + 1, 8):
+            for q in range(p + 1, group):
                 scaled = columns[q][p : p + 1, :] * pivot
                 columns[q] = jnp.where(sub == p, scaled, columns[q] - columns[p] * scaled)
             scaled = held[p : p + 1, :] * pivot
             held = jnp.where(sub == p, scaled, held - columns[p] * scaled)
-        rows[g] = held
-        spread = [jnp.broadcast_to(held[q : q + 1, :], shape) for q in range(8)]
-        for i in [*range(g + 1, count), *range(g)]:
-            left = jnp.where(inside, 0.0, rows[i])
-            for q in range(8):
-                left -= jnp.broadcast_to(rows[i][:, first + q : first + q + 1], shape) * spread[q]
-            rows[i] = left
-    return jnp.concatenate(rows, 0)
-
-
-def products(scale, piece_refs, noise_ref, out_ref):
+        right.append(jnp.where(lane < first + group, held, 0.0))
+        for i in range(g + 1, count):
+            rows[i] = jnp.where(inside, 0.0, rows[i]) - tree_sum(
+                [spread(rows[i], first + q) * held[q : q + 1, :] for q in range(group)]
+            )
+    return jnp.concatenate(left), jnp.concatenate(right)
+
+
+def products(scale, piece_refs, noise_ref):
     scaled = jnp.concatenate([ref[...] for ref in piece_refs])
     members = scaled.shape[1]
     spread = scaled - jnp.sum(scaled, axis=1, keepdims=True) * (1.0 / members)
     misfit = noise_ref[...] - scale * scaled
-    out_ref[:, :members] = product(spread, spread, 0, 0)
-    out_ref[:, members:] = product(spread, misfit, 0, 0)
+    return product(spread, jnp.concatenate([spread, misfit], axis=1), 0, 0)
+
+
+def partial_products(scale, *refs):
+    *piece_refs, noise_ref, sums_ref = refs
+    sums_ref[...] = products(scale, piece_refs, noise_ref)
 
 
 def update(scale, sums_ref, log_ref, updated_hbm, weights_ref, held_ref, sems):
@@ -368,9 +382,13 @@
         jnp.int32, (half, half), 1
     )
     shift = jnp.where(diagonal, inflation, 0.0)
-    upper = product(inverse(sums_ref[:half, :half] + shift), sums_ref[:half, half:])
-    lower = sums_ref[half:, half:] - product(sums_ref[half:, :half], upper)
-    second = product(inverse(lower[:, :half] + shift), lower[:, half:])
+    left, right = factors(sums_ref[:half, :half] + shift)
+    both = product(jnp.concatenate([left, right]), sums_ref[:half, half:])
+    upper = both[half:]
+    lower = sums_ref[half:, half:] - product(both[:half, :half], upper, 0, 0)
+    upper = product(left, upper, 0, 0)
+    left, right = factors(lower[:, :half] + shift)
+    second = product(product(left, right, 0, 0), lower[:, half:])
     first = upper[:, half:] - product(upper[:, :half], second)
     mean = (
         jnp.sum(first, axis=0, keepdims=True) + jnp.sum(second, axis=0, keepdims=True)
@@ -381,7 +399,9 @@
     copies = []
     for n in range(sems.shape[0]):
         part = pl.ds(n * chunk, chunk)
-        held_ref[part] = log_ref[part] + product(log_ref[part], weights_ref[...])
+        held_ref[part] = log_ref[part] + product(
+            log_ref[part], weights_ref[...], precision=UPDATE
+        )
         copies.append(pltpu.make_async_copy(held_ref.at[part], updated_hbm.at[part], sems.at[n]))
         copies[-1].start()
     for copy in copies:
@@ -389,11 +409,11 @@
 
 
 def smooth(scale, *refs):
-    *piece_refs, noise_ref, log_ref, inner_ref, updated_hbm, final_hbm = refs[:-5]
+    *piece_refs, noise_ref, near_ref, log_ref, inner_ref, updated_hbm, final_hbm = refs[:-5]
     sums_ref, weights_ref, held_ref, sems, final_sem = refs[-5:]
     keep = pltpu.make_async_copy(inner_ref, final_hbm, final_sem)
     keep.start()
-    products(scale, piece_refs, noise_ref, sums_ref)
+    sums_ref[...] = near_ref[...] + products(scale, piece_refs, noise_ref)
     update(scale, sums_ref, log_ref, updated_hbm, weights_ref, held_ref, sems)
     keep.wait()
 
@@ -407,7 +427,7 @@
 
 
 def assimilate(scale, pieces, noise, log_rows, final, sums):
-    members = noise.shape[1]
+    members = log_rows.shape[1]
     pair = (members, 2 * members)
     outs = (f32(*log_rows.shape), f32(*final.shape))
     scratch = [
@@ -416,18 +436,25 @@
         pltpu.SemaphoreType.DMA((4,)),
         pltpu.SemaphoreType.DMA,
     ]
+    def partial(blocks, noise_rows):
+        args = [*blocks, noise_rows]
+        return call(
+            functools.partial(partial_products, scale), "partial_products", f32(*pair),
+            [VMEM] * len(args), args, flops=10**8,
+        )
+
     if not sums:
-        args = [*pieces, noise, log_rows, final]
+        near = len(pieces) // 2
+        split = sum(piece.shape[0] for piece in pieces[:near])
+        args = [
+            *pieces[near:], noise[split:], partial(pieces[:near], noise[:split]), log_rows, final
+        ]
         return call(
             functools.partial(smooth, scale), "smooth", outs, [VMEM] * len(args), args,
             scratch=[pltpu.VMEM(pair, jnp.float32), *scratch], flops=10**9,
             out_specs=(HBM, HBM),
         )
-    args = [*pieces, noise]
-    total = call(
-        lambda *refs: products(scale, refs[:-2], *refs[-2:]), "products", f32(*pair),
-        [VMEM] * len(args), args, flops=10**9,
-    )
+    total = partial(pieces, noise)
     for route in sums:
         total = total + send(total, route)
     args = [total, log_rows, final]
@@ -461,7 +488,10 @@
         functools.partial(prepare, rows), "prepare",
         (tile, tile, tile, f32(depth, columns), *(f32(2, *face) for face in faces)),
         [HBM] * 4,
-        [temperature, log_cond, rock_class_code, rock_class_diffusivity],
+        [
+            pltpu.with_memory_space_constraint(array, pltpu.HBM)
+            for array in (temperature, log_cond, rock_class_code, rock_class_diffusivity)
+        ],
         scratch=[
             pltpu.VMEM((columns, 128), jnp.float32),
             pltpu.VMEM(rock_class_code.shape, jnp.int32),

time: 63.1 us -> 56.4 us (0.89)
  waiting for transfers between devices: 18.4 us -> 15.6 us
  Pallas kernels: 20.2 us -> 18 us
  local copies, waits for them, and re-layouts: 4.6 us -> 3.02 us
    pallas_call x7 -> x8, Pallas kernels: 20.2 us -> 18 us  [call(): pl.pallas_call(kernel, out_shape=outs, in_specs=specs, out_specs=jax.tree...]
    unnamed x18 -> x16, local copies, waits for them, and re-layouts: 4.53 us -> 2.88 us
    ppermute x8, waiting for transfers between devices: 7.73 us -> 6.14 us  [exchange(): lax.ppermute(face, ('gx', 'gy'), route)]
    ppermute x10, waiting for transfers between devices: 10.6 us -> 9.43 us  [send(): return lax.ppermute(block, ('gx', 'gy'), route)]
  transfers between devices with their start and end apart: 18 -> 18, of which waited for: 12 -> 11; matrix products, arithmetic and copies ran while one was open for 3% -> 3% of each run, Pallas kernels for 4% -> 6%
where the time goes in v4:
time: 56.4 us; the launch traced here: 56.1 us
  Pallas kernels  18 us (32%)
  starting transfers between devices  17 us (30%)
  waiting for transfers between devices  15.6 us (28%)
  local copies, waits for them, and re-layouts  3.02 us (5%)
  other arithmetic  1.56 us (3%)
  between operations  0.97 us (2%)
    pallas_call x8, Pallas kernels, call(): pl.pallas_call(kernel, out_shape=outs, in_specs=specs, out_specs=jax.tree...  18 us
    ppermute x8, starting transfers between devices, exchange(): lax.ppermute(face, ('gx', 'gy'), route)  9.94 us
    ppermute x10, waiting for transfers between devices, send(): return lax.ppermute(block, ('gx', 'gy'), route)  9.43 us
    ppermute x10, starting transfers between devices, send(): return lax.ppermute(block, ('gx', 'gy'), route)  7.11 us
    ppermute x8, waiting for transfers between devices, exchange(): lax.ppermute(face, ('gx', 'gy'), route)  6.14 us
    unnamed x16, local copies, waits for them, and re-layouts  2.88 us
  transfers between devices with their start and end apart: 18, of which 11 were waited for; matrix products, arithmetic and copies ran while one was open for 3% of the time, Pallas kernels for 6%

profile of v4, /device:TPU:0, one launch (start us, length us, event | category | flops | bytes accessed | tf_op | source)
XLA Modules:
  0.0 56.1 jit_solution(15822657996564561769)
XLA Ops:
  0.6 2.5 %prepare.1 = (f32[64,16,256]{2,1,0:T(8,128)S(1)}, f32[64,16,256]{2,1,0:T(8,128)S(1)}, f32[64,16,256]{2,1,0:T(8,128)S(1)}, f32[16,128]{1,0:T(8,128)S(1)}, f32[2,8...) custom-call(f32[64,16,256]{2,1,0:T(8,128)} %bitcast.8, ...), custom_call_target="tpu_custom_call" | custom-call | bytes 2101280 | tf_op jit(solution)/shard_map/prepare/pallas_call | solution.py:26
  3.1 1.0 %copy-done = f32[64,16,256]{2,1,0:T(8,128)} copy-done((f32[64,16,256]{2,1,0:T(8,128)}, f32[64,16,256]{2,1,0:T(8,128)S(1)}, u32[]{:S(2)}) %copy-start) | copy-done | bytes 1048600
  4.1 0.5 collective-permute-start
  4.6 2.9 %collective-permute-start.1 = (f32[2,8,16,256]{3,2,1,0:T(8,128)}, f32[2,8,16,256]{3,2,1,0:T(8,128)S(1)}, u32[]{:S(2)}, u32[]{:S(2)}) collective-permute-start(f32[2,8,16,256]{3,2,1,0:T(8,128)} %get-tuple-element.27), channel_id=1, source_target_pairs={{4,0},{5,1},{6,2},{7,3},{8,4},{9,5},{10,6},{11,7},{12,8},{13,9},{1... | collective-permute-start | bytes 786440 | tf_op jit(solution)/shard_map/ppermute | solution.py:59
  7.4 2.3 %collective-permute-start.2 = (f32[2,8,16,256]{3,2,1,0:T(8,128)}, f32[2,8,16,256]{3,2,1,0:T(8,128)S(1)}, u32[]{:S(2)}, u32[]{:S(2)}) collective-permute-start(f32[2,8,16,256]{3,2,1,0:T(8,128)} %get-tuple-element.28), channel_id=1, source_target_pairs={{0,1},{1,2},{2,3},{3,7},{4,0},{5,4},{6,5},{7,6},{8,9},{9,10},{10,1... | collective-permute-start | bytes 786440 | tf_op jit(solution)/shard_map/ppermute | solution.py:59
  9.8 0.7 %multiply_bitcast_fusion = s32[32]{0:T(128)S(1)} fusion(s32[32,32]{1,0:T(8,128)} %constant.73.clone, s32[]{:T(128)S(6)} %select_n.42), kind=kLoop, calls=%fused_computation.11 | loop fusion | flops 32 | bytes 260 | tf_op jit(solution)/shard_map/mul | solution.py:537
  10.5 0.1 multiply_remainder_fusion
  10.6 0.7 %copy-done.3 = f32[16]{0:T(128)S(1)} copy-done((f32[16]{0:T(128)S(1)}, f32[16]{0:T(128)}, u32[]{:S(2)}) %copy-start.3) | copy-done | bytes 88
  11.3 1.2 %copy-done.1 = f32[64,16,256]{2,1,0:T(8,128)S(1)} copy-done((f32[64,16,256]{2,1,0:T(8,128)S(1)}, f32[64,16,256]{2,1,0:T(8,128)}, u32[]{:S(2)}) %copy-start.1) | copy-done | bytes 1048600
  12.5 1.3 %middle_inside.1 = (f32[64,16,256]{2,1,0:T(8,128)S(1)}, f32[64,16,256]{2,1,0:T(8,128)S(1)}) custom-call(f32[16]{0:T(128)S(1)} %copy-done.3, f32[64,16,256]{2,1,0:T(8,128)S(1)} %get-tuple-element.21.t_ref, f32[64,16,256]{2,1,0:T(8,128)S(1)} %copy-done.1, f32[16,128]{1,0:T(8,128)S(1)} %get-tuple-element.23.columns_ref, ...), custom_call_target="tpu_custom_call", output_to_operand_aliasing={{0}: (4, {})} | custom-call | flops 10000000 | bytes 3153984 | tf_op jit(solution)/shard_map/middle_inside/pallas_call | solution.py:26
  13.8 0.9 %collective-permute-done.2.rest_2_.rest_6_ = f32[2,8,16,256]{3,2,1,0:T(8,128)S(1)} collective-permute-done((f32[2,8,16,256]{3,2,1,0:T(8,128)}, f32[2,8,16,256]{3,2,1,0:T(8,128)S(1)}, u32[]{:S(2)}, u32[]{:S(2)}) %collective-permute-start.2) | collective-permute-done | bytes 262176 | tf_op jit(solution)/shard_map/ppermute | solution.py:59
  14.8 1.4 %collective-permute-done.3.rest_3_.rest_7_ = f32[2,8,16,256]{3,2,1,0:T(8,128)S(1)} collective-permute-done((f32[2,8,16,256]{3,2,1,0:T(8,128)S(1)}, f32[2,8,16,256]{3,2,1,0:T(8,128)S(1)}, u32[]{:S(2)}, u32[]{:S(2)}) %collective-permute-start.3) | collective-permute-done | bytes 262176 | tf_op jit(solution)/shard_map/ppermute | solution.py:59
  16.2 1.0 %middle_border.1 = (f32[64,16,256]{2,1,0:T(8,128)S(1)}, f32[8,16,256]{2,1,0:T(8,128)S(1)}, f32[8,16,256]{2,1,0:T(8,128)S(1)}, f32[8,16,256]{2,1,0:T(8,128)S(1)}, f32[8,16,256]{2,1,0:T(8,128)S(1)}) custom-call(f32[16]{0:T(128)S(1)} %copy-done.3, f32[64,16,256]{2,1,0:T(8,128)S(1)} %get-tuple-element.21.t_ref, ...), custom_call_target="tpu_custom_call", output_to_operand_aliasing={{0}: (7, {})} | custom-call | flops 10000000 | bytes 4194368 | tf_op jit(solution)/shard_map/middle_border/pallas_call | solution.py:26
  17.3 2.6 %collective-permute-start.5 = (f32[8,16,256]{2,1,0:T(8,128)S(1)}, f32[8,16,256]{2,1,0:T(8,128)S(1)}, u32[]{:S(2)}, u32[]{:S(2)}) collective-permute-start(f32[8,16,256]{2,1,0:T(8,128)S(1)} %get-tuple-element.33), channel_id=1, source_target_pairs={{4,0},{5,1},{6,2},{7,3},{8,4},{9,5},{10,6},{11,7},{12,8},{13,9},{1... | collective-permute-start | bytes 393224 | tf_op jit(solution)/shard_map/ppermute | solution.py:59
  19.9 1.6 %collective-permute-start.6 = (f32[8,16,256]{2,1,0:T(8,128)S(1)}, f32[8,16,256]{2,1,0:T(8,128)S(1)}, u32[]{:S(2)}, u32[]{:S(2)}) collective-permute-start(f32[8,16,256]{2,1,0:T(8,128)S(1)} %get-tuple-element.34), channel_id=1, source_target_pairs={{0,1},{1,2},{2,3},{3,7},{4,0},{5,4},{6,5},{7,6},{8,9},{9,10},{10,1... | collective-permute-start | bytes 393224 | tf_op jit(solution)/shard_map/ppermute | solution.py:59
  21.5 1.1 %final_inside.1.rest_8_ = f32[64,16,256]{2,1,0:T(8,128)S(1)} custom-call(f32[16]{0:T(128)S(1)} %copy-done.3, f32[64,16,256]{2,1,0:T(8,128)S(1)} %get-tuple-element.31.u_ref, f32[64,16,256]{2,1,0:T(8,128)S(1)} %get-tuple-element.25.h_ref), custom_call_target="tpu_custom_call" | custom-call | flops 10000000 | bytes 2097216 | tf_op jit(solution)/shard_map/final_inside/pallas_call | solution.py:26
  22.6 0.4 collective-permute-done.4.rest_0_
  23.0 1.0 %collective-permute-done.6.rest_2_ = f32[8,16,256]{2,1,0:T(8,128)S(1)} collective-permute-done((f32[8,16,256]{2,1,0:T(8,128)S(1)}, f32[8,16,256]{2,1,0:T(8,128)S(1)}, u32[]{:S(2)}, u32[]{:S(2)}) %collective-permute-start.6) | collective-permute-done | bytes 131104 | tf_op jit(solution)/shard_map/ppermute | solution.py:59
  24.0 2.4 %collective-permute-done.7.rest_3_ = f32[8,16,256]{2,1,0:T(8,128)S(1)} collective-permute-done((f32[8,16,256]{2,1,0:T(8,128)S(1)}, f32[8,16,256]{2,1,0:T(8,128)S(1)}, u32[]{:S(2)}, u32[]{:S(2)}) %collective-permute-start.7) | collective-permute-done | bytes 131104 | tf_op jit(solution)/shard_map/ppermute | solution.py:59
  26.5 1.2 %observe.1 = (f32[64,16,256]{2,1,0:T(8,128)S(1)}, f32[32,256]{1,0:T(8,128)S(1)}) custom-call(f32[16]{0:T(128)S(1)} %copy-done.3, s32[32]{0:T(128)S(1)} %copy-done.4, f32[32]{0:T(128)S(1)} %copy-done.5, f32[32]{0:T(128)S(1)} %multiply_divide_fusion.factor_ref, f32[64,16,256]{2,1,0:T(8,128)S(1)} %get-tuple-element.31.u_ref, ...), custom_call_target="tpu_custom_call", output_to_operand_aliasing={{0}: (14, {})} | custom-call | flops 10000000 | bytes 4719040 | tf_op jit(solution)/shard_map/observe/pallas_call | solution.py:26
  27.6 2.0 %collective-permute-start.10 = (f32[32,256]{1,0:T(8,128)S(1)}, f32[32,256]{1,0:T(8,128)S(1)}, u32[]{:S(2)}, u32[]{:S(2)}) collective-permute-start(f32[32,256]{1,0:T(8,128)S(1)} %get-tuple-element.36.refs_0_), channel_id=1, source_target_pairs={{1,0},{3,1},{0,2},{2,3},{5,4},{7,5},{4,6},{6,7},{9,8},{11,9},{8,10... | collective-permute-start | bytes 98312 | tf_op jit(solution)/shard_map/ppermute | solution.py:291
  29.7 1.9 %collective-permute-start.8 = (f32[32,256]{1,0:T(8,128)S(1)}, f32[32,256]{1,0:T(8,128)S(1)}, u32[]{:S(2)}, u32[]{:S(2)}) collective-permute-start(f32[32,256]{1,0:T(8,128)S(1)} %get-tuple-element.36.refs_0_), channel_id=1, source_target_pairs={{0,3},{1,2},{2,5},{3,4},{4,7},{5,6},{6,1},{7,0},{8,11},{9,10},{10,... | collective-permute-start | bytes 98312 | tf_op jit(solution)/shard_map/ppermute | solution.py:291
  31.7 3.2 %collective-permute-done.8.refs_1_ = f32[32,256]{1,0:T(8,128)S(1)} collective-permute-done((f32[32,256]{1,0:T(8,128)S(1)}, f32[32,256]{1,0:T(8,128)S(1)}, u32[]{:S(2)}, u32[]{:S(2)}) %collective-permute-start.8) | collective-permute-done | bytes 32800 | tf_op jit(solution)/shard_map/ppermute | solution.py:291
  34.8 1.6 %collective-permute-done.9.refs_2_ = f32[32,256]{1,0:T(8,128)S(1)} collective-permute-done((f32[32,256]{1,0:T(8,128)S(1)}, f32[32,256]{1,0:T(8,128)S(1)}, u32[]{:S(2)}, u32[]{:S(2)}) %collective-permute-start.9) | collective-permute-done | bytes 32800 | tf_op jit(solution)/shard_map/ppermute | solution.py:291
  36.5 0.7 %collective-permute-start.12 = (f32[128,256]{1,0:T(8,128)S(1)}, f32[128,256]{1,0:T(8,128)S(1)}, u32[]{:S(2)}, u32[]{:S(2)}) collective-permute-start(f32[128,256]{1,0:T(8,128)S(1)} %pack.1.refs_0_), channel_id=1, source_target_pairs={{0,24},{1,25},{2,26},{3,27},{4,28},{5,29},{6,30},{7,31},{8,16},{9,... | collective-permute-start | bytes 393224 | tf_op jit(solution)/shard_map/ppermute | solution.py:291
  37.2 2.3 %collective-permute-start.14 = (f32[128,256]{1,0:T(8,128)S(1)}, f32[128,256]{1,0:T(8,128)S(1)}, u32[]{:S(2)}, u32[]{:S(2)}) collective-permute-start(f32[128,256]{1,0:T(8,128)S(1)} %pack.1.refs_0_), channel_id=1, source_target_pairs={{0,8},{1,9},{2,10},{3,11},{4,12},{5,13},{6,14},{7,15},{8,24},{9,25... | collective-permute-start | bytes 393224 | tf_op jit(solution)/shard_map/ppermute | solution.py:291
  39.5 0.7 %fusion.4 = f32[1024,256]{1,0:T(8,128)S(1)} fusion(s32[1024]{0:T(1024)S(1)} %get-tuple-element.43, s32[1024]{0:T(1024)S(1)} %get-tuple-element.42, s32[256]{0:T(256)S(1)} %and_select_fusion), kind=kLoop, calls=%fused_computation.6 | loop fusion | flops 4980736 | bytes 1057792 | tf_op jit(solution)/shard_map/mul | solution.py:539
  40.3 2.2 %collective-permute-done.12.refs_1_ = f32[128,256]{1,0:T(8,128)S(1)} collective-permute-done((f32[128,256]{1,0:T(8,128)S(1)}, f32[128,256]{1,0:T(8,128)S(1)}, u32[]{:S(2)}, u32[]{:S(2)}) %collective-permute-start.12) | collective-permute-done | bytes 131104 | tf_op jit(solution)/shard_map/ppermute | solution.py:291
  42.6 1.8 %collective-permute-done.14.refs_2_ = f32[128,256]{1,0:T(8,128)S(1)} collective-permute-done((f32[128,256]{1,0:T(8,128)S(1)}, f32[128,256]{1,0:T(8,128)S(1)}, u32[]{:S(2)}, u32[]{:S(2)}) %collective-permute-start.14) | collective-permute-done | bytes 131104 | tf_op jit(solution)/shard_map/ppermute | solution.py:291
  44.3 0.6 %collective-permute-done.16.refs_3_ = f32[128,256]{1,0:T(8,128)S(1)} collective-permute-done((f32[128,256]{1,0:T(8,128)S(1)}, f32[128,256]{1,0:T(8,128)S(1)}, u32[]{:S(2)}, u32[]{:S(2)}) %collective-permute-start.16) | collective-permute-done | bytes 131104 | tf_op jit(solution)/shard_map/ppermute | solution.py:291
  45.0 1.1 %partial_products.1.refs_5_ = f32[256,512]{1,0:T(8,128)S(1)} custom-call(f32[128,256]{1,0:T(8,128)S(1)} %pack.1.refs_0_, f32[128,256]{1,0:T(8,128)S(1)} %collective-permute-done.12.refs_1_, f32[128,256]{1,0:T(8,128)S(1)} %collective-permute-done.14.refs_2_, f32[128,256]{1,0:T(8,128)S(1)} %collective-permute-done.16.refs_3_, ...), custom_call_target="tpu_custom_call" | custom-call | flops 100000000 | bytes 1048576 | tf_op jit(solution)/shard_map/partial_products/pallas_call | solution.py:26
  46.2 9.7 %smooth.1 = (f32[1024,256]{1,0:T(8,128)}, f32[64,16,256]{2,1,0:T(8,128)}) custom-call(f32[128,256]{1,0:T(8,128)S(1)} %collective-permute-done.11.refs_0_, f32[128,256]{1,0:T(8,128)S(1)} %collective-permute-done.13.refs_1_, f32[128,256]{1,0:T(8,128)S(1)} %collective-permute-done.15.refs_2_, f32[128,256]{1,0:T(8,128)S(1)} %collective-permute-done.17.refs_3_, ...), custom_call_target="tpu_custom_call" | custom-call | flops 1000000000 | bytes 3670016 | tf_op jit(solution)/shard_map/smooth/pallas_call | solution.py:26
  (36 shorter events, 0.5 us)
Async XLA Ops:
  3.1 1.0 %copy-start = (f32[64,16,256]{2,1,0:T(8,128)}, f32[64,16,256]{2,1,0:T(8,128)S(1)}, u32[]{:S(2)}) copy-start(f32[64,16,256]{2,1,0:T(8,128)S(1)} %get-tuple-element.22.log_ref) | copy-start | bytes 3145732
  4.1 9.7 %collective-permute-start = (f32[2,8,16,256]{3,2,1,0:T(8,128)}, f32[2,8,16,256]{3,2,1,0:T(8,128)S(1)}, u32[]{:S(2)}, u32[]{:S(2)}) collective-permute-start(f32[2,8,16,256]{3,2,1,0:T(8,128)} %get-tuple-element.26), channel_id=1, source_target_pairs={{0,4},{1,5},{2,6},{3,7},{4,8},{5,9},{6,10},{7,11},{8,12},{9,13},{1... | collective-permute-start | bytes 786440 | tf_op jit(solution)/shard_map/ppermute | solution.py:59
  4.6 9.3 %collective-permute-start.1 = (f32[2,8,16,256]{3,2,1,0:T(8,128)}, f32[2,8,16,256]{3,2,1,0:T(8,128)S(1)}, u32[]{:S(2)}, u32[]{:S(2)}) collective-permute-start(f32[2,8,16,256]{3,2,1,0:T(8,128)} %get-tuple-element.27), channel_id=1, source_target_pairs={{4,0},{5,1},{6,2},{7,3},{8,4},{9,5},{10,6},{11,7},{12,8},{13,9},{1... | collective-permute-start | bytes 786440 | tf_op jit(solution)/shard_map/ppermute | solution.py:59
  7.4 7.3 %collective-permute-start.2 = (f32[2,8,16,256]{3,2,1,0:T(8,128)}, f32[2,8,16,256]{3,2,1,0:T(8,128)S(1)}, u32[]{:S(2)}, u32[]{:S(2)}) collective-permute-start(f32[2,8,16,256]{3,2,1,0:T(8,128)} %get-tuple-element.28), channel_id=1, source_target_pairs={{0,1},{1,2},{2,3},{3,7},{4,0},{5,4},{6,5},{7,6},{8,9},{9,10},{10,1... | collective-permute-start | bytes 786440 | tf_op jit(solution)/shard_map/ppermute | solution.py:59
  9.8 6.4 %collective-permute-start.3 = (f32[2,8,16,256]{3,2,1,0:T(8,128)S(1)}, f32[2,8,16,256]{3,2,1,0:T(8,128)S(1)}, u32[]{:S(2)}, u32[]{:S(2)}) collective-permute-start(f32[2,8,16,256]{3,2,1,0:T(8,128)S(1)} %get-tuple-element.29), channel_id=1, source_target_pairs={{1,0},{2,1},{3,2},{7,3},{0,4},{4,5},{5,6},{6,7},{9,8},{10,9},{11,1... | collective-permute-start | bytes 786440 | tf_op jit(solution)/shard_map/ppermute | solution.py:59
  10.6 0.7 %copy-start.3 = (f32[16]{0:T(128)S(1)}, f32[16]{0:T(128)}, u32[]{:S(2)}) copy-start(f32[16]{0:T(128)} %courant_ref.7) | copy-start | bytes 196
  11.3 1.2 %copy-start.1 = (f32[64,16,256]{2,1,0:T(8,128)S(1)}, f32[64,16,256]{2,1,0:T(8,128)}, u32[]{:S(2)}) copy-start(f32[64,16,256]{2,1,0:T(8,128)} %copy-done) | copy-start | bytes 3145732
  17.2 5.8 %collective-permute-start.4 = (f32[8,16,256]{2,1,0:T(8,128)S(1)}, f32[8,16,256]{2,1,0:T(8,128)S(1)}, u32[]{:S(2)}, u32[]{:S(2)}) collective-permute-start(f32[8,16,256]{2,1,0:T(8,128)S(1)} %get-tuple-element.32), channel_id=1, source_target_pairs={{0,4},{1,5},{2,6},{3,7},{4,8},{5,9},{6,10},{7,11},{8,12},{9,13},{1... | collective-permute-start | bytes 393224 | tf_op jit(solution)/shard_map/ppermute | solution.py:59
  17.3 5.7 %collective-permute-start.5 = (f32[8,16,256]{2,1,0:T(8,128)S(1)}, f32[8,16,256]{2,1,0:T(8,128)S(1)}, u32[]{:S(2)}, u32[]{:S(2)}) collective-permute-start(f32[8,16,256]{2,1,0:T(8,128)S(1)} %get-tuple-element.33), channel_id=1, source_target_pairs={{4,0},{5,1},{6,2},{7,3},{8,4},{9,5},{10,6},{11,7},{12,8},{13,9},{1... | collective-permute-start | bytes 393224 | tf_op jit(solution)/shard_map/ppermute | solution.py:59
  19.9 1.6 %copy-start.7 = (f32[32]{0:T(128)S(1)}, f32[32]{0:T(128)}, u32[]{:S(2)}) copy-start(f32[32]{0:T(128)} %param.17) | copy-start | bytes 388
  19.9 4.1 %collective-permute-start.6 = (f32[8,16,256]{2,1,0:T(8,128)S(1)}, f32[8,16,256]{2,1,0:T(8,128)S(1)}, u32[]{:S(2)}, u32[]{:S(2)}) collective-permute-start(f32[8,16,256]{2,1,0:T(8,128)S(1)} %get-tuple-element.34), channel_id=1, source_target_pairs={{0,1},{1,2},{2,3},{3,7},{4,0},{5,4},{6,5},{7,6},{8,9},{9,10},{10,1... | collective-permute-start | bytes 393224 | tf_op jit(solution)/shard_map/ppermute | solution.py:59
  21.5 5.0 %collective-permute-start.7 = (f32[8,16,256]{2,1,0:T(8,128)S(1)}, f32[8,16,256]{2,1,0:T(8,128)S(1)}, u32[]{:S(2)}, u32[]{:S(2)}) collective-permute-start(f32[8,16,256]{2,1,0:T(8,128)S(1)} %get-tuple-element.35), channel_id=1, source_target_pairs={{1,0},{2,1},{3,2},{7,3},{0,4},{4,5},{5,6},{6,7},{9,8},{10,9},{11,1... | collective-permute-start | bytes 393224 | tf_op jit(solution)/shard_map/ppermute | solution.py:59
  21.5 5.0 %copy-start.4 = (s32[32]{0:T(128)S(1)}, s32[32]{0:T(128)}, u32[]{:S(2)}) copy-start(s32[32]{0:T(128)} %cells_ref.1) | copy-start | bytes 388
  21.5 4.9 %copy-start.5 = (f32[32]{0:T(128)S(1)}, f32[32]{0:T(128)}, u32[]{:S(2)}) copy-start(f32[32]{0:T(128)} %reading_ref.1) | copy-start | bytes 388
  27.6 4.0 %copy-start.6 = (s32[256]{0:T(256)S(1)}, s32[256]{0:T(256)}, u32[]{:S(2)}) copy-start(s32[256]{0:T(256)} %param.18) | copy-start | bytes 3076
  27.6 4.0 %collective-permute-start.10 = (f32[32,256]{1,0:T(8,128)S(1)}, f32[32,256]{1,0:T(8,128)S(1)}, u32[]{:S(2)}, u32[]{:S(2)}) collective-permute-start(f32[32,256]{1,0:T(8,128)S(1)} %get-tuple-element.36.refs_0_), channel_id=1, source_target_pairs={{1,0},{3,1},{0,2},{2,3},{5,4},{7,5},{4,6},{6,7},{9,8},{11,9},{8,10... | collective-permute-start | bytes 98312 | tf_op jit(solution)/shard_map/ppermute | solution.py:291
  29.7 5.1 %collective-permute-start.8 = (f32[32,256]{1,0:T(8,128)S(1)}, f32[32,256]{1,0:T(8,128)S(1)}, u32[]{:S(2)}, u32[]{:S(2)}) collective-permute-start(f32[32,256]{1,0:T(8,128)S(1)} %get-tuple-element.36.refs_0_), channel_id=1, source_target_pairs={{0,3},{1,2},{2,5},{3,4},{4,7},{5,6},{6,1},{7,0},{8,11},{9,10},{10,... | collective-permute-start | bytes 98312 | tf_op jit(solution)/shard_map/ppermute | solution.py:291
  31.6 4.8 %collective-permute-start.9 = (f32[32,256]{1,0:T(8,128)S(1)}, f32[32,256]{1,0:T(8,128)S(1)}, u32[]{:S(2)}, u32[]{:S(2)}) collective-permute-start(f32[32,256]{1,0:T(8,128)S(1)} %get-tuple-element.36.refs_0_), channel_id=1, source_target_pairs={{0,1},{1,3},{2,0},{3,2},{4,5},{5,7},{6,4},{7,6},{8,9},{9,11},{10,8... | collective-permute-start | bytes 98312 | tf_op jit(solution)/shard_map/ppermute | solution.py:291
  36.5 6.1 %collective-permute-start.12 = (f32[128,256]{1,0:T(8,128)S(1)}, f32[128,256]{1,0:T(8,128)S(1)}, u32[]{:S(2)}, u32[]{:S(2)}) collective-permute-start(f32[128,256]{1,0:T(8,128)S(1)} %pack.1.refs_0_), channel_id=1, source_target_pairs={{0,24},{1,25},{2,26},{3,27},{4,28},{5,29},{6,30},{7,31},{8,16},{9,... | collective-permute-start | bytes 393224 | tf_op jit(solution)/shard_map/ppermute | solution.py:291
  37.2 7.2 %collective-permute-start.14 = (f32[128,256]{1,0:T(8,128)S(1)}, f32[128,256]{1,0:T(8,128)S(1)}, u32[]{:S(2)}, u32[]{:S(2)}) collective-permute-start(f32[128,256]{1,0:T(8,128)S(1)} %pack.1.refs_0_), channel_id=1, source_target_pairs={{0,8},{1,9},{2,10},{3,11},{4,12},{5,13},{6,14},{7,15},{8,24},{9,25... | collective-permute-start | bytes 393224 | tf_op jit(solution)/shard_map/ppermute | solution.py:291
  39.5 5.4 %collective-permute-start.16 = (f32[128,256]{1,0:T(8,128)S(1)}, f32[128,256]{1,0:T(8,128)S(1)}, u32[]{:S(2)}, u32[]{:S(2)}) collective-permute-start(f32[128,256]{1,0:T(8,128)S(1)} %pack.1.refs_0_), channel_id=1, source_target_pairs={{8,0},{9,1},{10,2},{11,3},{12,4},{13,5},{14,6},{15,7},{24,8},{25,9... | collective-permute-start | bytes 393224 | tf_op jit(solution)/shard_map/ppermute | solution.py:291
  40.2 5.9 %collective-permute-start.11 = (f32[128,256]{1,0:T(8,128)S(1)}, f32[128,256]{1,0:T(8,128)S(1)}, u32[]{:S(2)}, u32[]{:S(2)}) collective-permute-start(f32[128,256]{1,0:T(8,128)S(1)} %pack.1.refs_0_), channel_id=1, source_target_pairs={{0,4},{1,5},{2,6},{3,7},{4,0},{5,1},{6,2},{7,3},{8,12},{9,13},{10,... | collective-permute-start | bytes 393224 | tf_op jit(solution)/shard_map/ppermute | solution.py:291
  42.6 3.6 %collective-permute-start.13 = (f32[128,256]{1,0:T(8,128)S(1)}, f32[128,256]{1,0:T(8,128)S(1)}, u32[]{:S(2)}, u32[]{:S(2)}) collective-permute-start(f32[128,256]{1,0:T(8,128)S(1)} %collective-permute-done.12.refs_1_), channel_id=1, source_target_pairs={{0,4},{1,5},{2,6},{3,7},{4,0},{5,1},{6,2},{7,3},{8,12},{9,13},{10,... | collective-permute-start | bytes 393224 | tf_op jit(solution)/shard_map/ppermute | solution.py:291
  44.3 1.8 %collective-permute-start.15 = (f32[128,256]{1,0:T(8,128)S(1)}, f32[128,256]{1,0:T(8,128)S(1)}, u32[]{:S(2)}, u32[]{:S(2)}) collective-permute-start(f32[128,256]{1,0:T(8,128)S(1)} %collective-permute-done.14.refs_2_), channel_id=1, source_target_pairs={{0,4},{1,5},{2,6},{3,7},{4,0},{5,1},{6,2},{7,3},{8,12},{9,13},{10,... | collective-permute-start | bytes 393224 | tf_op jit(solution)/shard_map/ppermute | solution.py:291
  44.9 1.3 %collective-permute-start.17 = (f32[128,256]{1,0:T(8,128)S(1)}, f32[128,256]{1,0:T(8,128)S(1)}, u32[]{:S(2)}, u32[]{:S(2)}) collective-permute-start(f32[128,256]{1,0:T(8,128)S(1)} %collective-permute-done.16.refs_3_), channel_id=1, source_target_pairs={{0,4},{1,5},{2,6},{3,7},{4,0},{5,1},{6,2},{7,3},{8,12},{9,13},{10,... | collective-permute-start | bytes 393224 | tf_op jit(solution)/shard_map/ppermute | solution.py:291
  45.0 1.3 %copy-start.2 = (f32[64,16,256]{2,1,0:T(8,128)S(1)}, f32[64,16,256]{2,1,0:T(8,128)}, u32[]{:S(2)}) copy-start(f32[64,16,256]{2,1,0:T(8,128)} %copy-done) | copy-start | bytes 3145732

commit v5 on v4

--- a/solution.py
+++ b/solution.py
@@ -14,6 +14,8 @@
 SMEM = pl.BlockSpec(memory_space=pltpu.SMEM)
 
 
+ORDER = (0, 2, 3, 1)
+AT = (0, 3, 1, 2)
 HBM = pl.BlockSpec(memory_space=pltpu.HBM)
 
 
@@ -97,7 +99,7 @@
 
 
 def prepare(rows, t_hbm, log_hbm, code_hbm, rock_hbm, *rest):
-    t_ref, log_ref, h_ref, columns_ref, *face_refs, turned, code_ref, rock_ref, sems = rest
+    t_ref, log_ref, columns_ref, *face_refs, h_ref, turned, code_ref, rock_ref, sems = rest
     span_x, span_y = rows
     depth = t_ref.shape[1]
     copies = [
@@ -185,10 +187,9 @@
     return write
 
 
-def middle_inside(rows, courant_ref, t_ref, log_ref, columns_ref, outer_ref, h_ref, middle_ref):
-    del outer_ref
+def middle_inside(rows, courant_ref, t_ref, log_ref, columns_ref, h_ref, middle_ref):
     inside = border(rows, False)
-    conductivity(rows, inside, log_ref, columns_ref, h_ref)
+    conductivity(rows, border(rows, True) + inside, log_ref, columns_ref, h_ref)
     advance(rows, inside, courant_ref, t_ref, h_ref, None, None, into(middle_ref))
 
 
@@ -196,7 +197,7 @@
     got, middle_ref, face_refs = rest[:4], rest[5], rest[6:]
     advance(
         rows, border(rows, True), courant_ref, t_ref, h_ref,
-        lambda n, k: got[n][0, k], lambda n, k: got[n][1, k], into(middle_ref),
+        lambda n, k: got[AT[n]][0, k], lambda n, k: got[AT[n]][1, k], into(middle_ref),
     )
 
     def put(n, k, layer):
@@ -214,7 +215,7 @@
     depth = u_ref.shape[1]
     advance(
         rows, border(rows, True), courant_ref, u_ref, h_ref,
-        lambda n, k: got_u[n][k], lambda n, k: got_h[n][1, k], into(final_ref),
+        lambda n, k: got_u[AT[n]][k], lambda n, k: got_h[AT[n]][1, k], into(final_ref),
     )
     for j in range(scaled_ref.shape[0]):
         cell = cells_ref[j]
@@ -274,7 +275,7 @@
             if len(bits) > 1 and rows * 4 <= limit:
                 high, low = bits.pop(), bits.pop()
                 ring = around(axis, low, high)
-                gathers.append([across(axis, low | high), ring, back(ring)])
+                gathers.append([ring, back(ring), across(axis, low | high)])
                 rows *= 4
                 continue
             step = bits.pop()
@@ -484,15 +485,16 @@
     faces = [(span_y, depth, members)] * 2 + [(span_x, depth, members)] * 2
     levels = rock_class_diffusivity.shape
     columns = -(-cells // 128) * 128
-    temperature, log_cond, outer, base, *sent = call(
+    temperature, log_cond, base, *sent = call(
         functools.partial(prepare, rows), "prepare",
-        (tile, tile, tile, f32(depth, columns), *(f32(2, *face) for face in faces)),
+        (tile, tile, f32(depth, columns), *(f32(2, *face) for face in faces)),
         [HBM] * 4,
         [
             pltpu.with_memory_space_constraint(array, pltpu.HBM)
             for array in (temperature, log_cond, rock_class_code, rock_class_diffusivity)
         ],
         scratch=[
+            pltpu.VMEM((cells, depth, members), jnp.float32),
             pltpu.VMEM((columns, 128), jnp.float32),
             pltpu.VMEM(rock_class_code.shape, jnp.int32),
             pltpu.SMEM(levels, jnp.float32),
@@ -502,15 +504,14 @@
     got = exchange(sent)
     half_cond, middle = call(
         functools.partial(middle_inside, rows), "middle_inside", (tile, tile),
-        [SMEM] + [VMEM] * 4,
-        [advection_courant, temperature, log_cond, base, outer],
-        flops=10**7, aliases={4: 0},
+        [SMEM] + [VMEM] * 3, [advection_courant, temperature, log_cond, base],
+        flops=10**7,
     )
     middle, *sent = call(
         functools.partial(middle_border, rows), "middle_border",
         (tile, *(f32(*face) for face in faces)),
         [SMEM] + [VMEM] * 7,
-        [advection_courant, temperature, half_cond, *got, middle],
+        [advection_courant, temperature, half_cond, *[got[n] for n in ORDER], middle],
         flops=10**7, aliases={7: 0},
     )
     got_middle = exchange(sent)
@@ -525,7 +526,7 @@
         [SMEM] * 4 + [VMEM] * 11,
         [
             advection_courant, probe_locations, observed_readings,
-            1.0 / (probe_noise_deviation * scale), middle, half_cond, *got_middle, *got, final,
+            1.0 / (probe_noise_deviation * scale), middle, half_cond, *[got_middle[n] for n in ORDER], *[got[n] for n in ORDER], final,
         ],
         flops=10**7, aliases={14: 0},
     )

time: 56.4 us -> 51.8 us (0.918)
  waiting for transfers between devices: 15.6 us -> 11 us
  local copies, waits for them, and re-layouts: 3.02 us -> 0.82 us
  starting transfers between devices: 17 us -> 19.1 us
    ppermute x10, waiting for transfers between devices: 9.43 us -> 6.01 us  [send(): return lax.ppermute(block, ('gx', 'gy'), route)]
    ppermute x10, starting transfers between devices: 7.11 us -> 9.52 us  [send(): return lax.ppermute(block, ('gx', 'gy'), route)]
    unnamed x16 -> x10, local copies, waits for them, and re-layouts: 2.88 us -> 0.68 us
    ppermute x8, waiting for transfers between devices: 6.14 us -> 4.97 us  [exchange(): lax.ppermute(face, ('gx', 'gy'), route)]
  transfers between devices with their start and end apart: 18 -> 18, of which waited for: 11 -> 9; matrix products, arithmetic and copies ran while one was open for 3% -> 3% of each run, Pallas kernels for 6% -> 7%
where the time goes in v5:
time: 51.8 us; the launch traced here: 51.5 us
  starting transfers between devices  19.1 us (37%)
  Pallas kernels  18 us (35%)
  waiting for transfers between devices  11 us (21%)
  other arithmetic  1.56 us (3%)
  between operations  0.95 us (2%)
  local copies, waits for them, and re-layouts  0.82 us (2%)
    pallas_call x8, Pallas kernels, call(): pl.pallas_call(kernel, out_shape=outs, in_specs=specs, out_specs=jax.tree...  18 us
    ppermute x8, starting transfers between devices, exchange(): lax.ppermute(face, ('gx', 'gy'), route)  9.6 us
    ppermute x10, starting transfers between devices, send(): return lax.ppermute(block, ('gx', 'gy'), route)  9.52 us
    ppermute x10, waiting for transfers between devices, send(): return lax.ppermute(block, ('gx', 'gy'), route)  6.01 us
    ppermute x8, waiting for transfers between devices, exchange(): lax.ppermute(face, ('gx', 'gy'), route)  4.97 us
  transfers between devices with their start and end apart: 18, of which 9 were waited for; matrix products, arithmetic and copies ran while one was open for 3% of the time, Pallas kernels for 7%

profile of v5, /device:TPU:0, one launch (start us, length us, event | category | flops | bytes accessed | tf_op | source)
XLA Modules:
  0.0 51.5 jit_solution(4340018441354369560)
XLA Ops:
  0.6 2.5 %prepare.1 = (f32[64,16,256]{2,1,0:T(8,128)S(1)}, f32[64,16,256]{2,1,0:T(8,128)S(1)}, f32[16,128]{1,0:T(8,128)S(1)}, f32[2,8,16,256]{3,2,1,0:T(8,128)}, f32[2,8,...) custom-call(f32[64,16,256]{2,1,0:T(8,128)} %bitcast.8, f32[64,16,256]{2,1,0:T(8,128)} %bitcast.9, ...), custom_call_target="tpu_custom_call" | custom-call | bytes 2101280 | tf_op jit(solution)/shard_map/prepare/pallas_call | solution.py:28
  3.1 0.5 collective-permute-start
  3.6 2.6 %collective-permute-start.1 = (f32[2,8,16,256]{3,2,1,0:T(8,128)}, f32[2,8,16,256]{3,2,1,0:T(8,128)S(1)}, u32[]{:S(2)}, u32[]{:S(2)}) collective-permute-start(f32[2,8,16,256]{3,2,1,0:T(8,128)} %get-tuple-element.25), channel_id=1, source_target_pairs={{0,1},{1,2},{2,3},{3,7},{4,0},{5,4},{6,5},{7,6},{8,9},{9,10},{10,1... | collective-permute-start | bytes 786440 | tf_op jit(solution)/shard_map/ppermute | solution.py:61
  6.2 2.3 %collective-permute-start.3 = (f32[2,8,16,256]{3,2,1,0:T(8,128)S(1)}, f32[2,8,16,256]{3,2,1,0:T(8,128)S(1)}, u32[]{:S(2)}, u32[]{:S(2)}) collective-permute-start(f32[2,8,16,256]{3,2,1,0:T(8,128)S(1)} %get-tuple-element.27), channel_id=1, source_target_pairs={{4,0},{5,1},{6,2},{7,3},{8,4},{9,5},{10,6},{11,7},{12,8},{13,9},{1... | collective-permute-start | bytes 786440 | tf_op jit(solution)/shard_map/ppermute | solution.py:61
  8.6 0.7 %multiply_bitcast_fusion = s32[32]{0:T(128)S(1)} fusion(s32[32,32]{1,0:T(8,128)} %constant.73.clone, s32[]{:T(128)S(6)} %select_n.42), kind=kLoop, calls=%fused_computation.11 | loop fusion | flops 32 | bytes 260 | tf_op jit(solution)/shard_map/mul | solution.py:538
  9.3 0.1 multiply_remainder_fusion
  9.4 0.1 rem.45
  9.4 0.7 %copy-done = f32[16]{0:T(128)S(1)} copy-done((f32[16]{0:T(128)S(1)}, f32[16]{0:T(128)}, u32[]{:S(2)}) %copy-start) | copy-done | bytes 88
  10.1 1.3 %middle_inside.1 = (f32[64,16,256]{2,1,0:T(8,128)S(1)}, f32[64,16,256]{2,1,0:T(8,128)S(1)}) custom-call(f32[16]{0:T(128)S(1)} %copy-done, f32[64,16,256]{2,1,0:T(8,128)S(1)} %get-tuple-element.20.t_ref, f32[64,16,256]{2,1,0:T(8,128)S(1)} %get-tuple-element.21.log_ref, f32[16,128]{1,0:T(8,128)S(1)} %get-tuple-element.22.columns_ref), custom_call_target="tpu_custom_call" | custom-call | flops 10000000 | bytes 2105408 | tf_op jit(solution)/shard_map/middle_inside/pallas_call | solution.py:28
  11.5 1.1 %collective-permute-done.1.rest_1_.rest_5_ = f32[2,8,16,256]{3,2,1,0:T(8,128)S(1)} collective-permute-done((f32[2,8,16,256]{3,2,1,0:T(8,128)}, f32[2,8,16,256]{3,2,1,0:T(8,128)S(1)}, u32[]{:S(2)}, u32[]{:S(2)}) %collective-permute-start.1) | collective-permute-done | bytes 262176 | tf_op jit(solution)/shard_map/ppermute | solution.py:61
  12.5 2.2 %collective-permute-done.2.rest_2_.rest_6_ = f32[2,8,16,256]{3,2,1,0:T(8,128)S(1)} collective-permute-done((f32[2,8,16,256]{3,2,1,0:T(8,128)}, f32[2,8,16,256]{3,2,1,0:T(8,128)S(1)}, u32[]{:S(2)}, u32[]{:S(2)}) %collective-permute-start.2) | collective-permute-done | bytes 262176 | tf_op jit(solution)/shard_map/ppermute | solution.py:61
  14.7 1.0 %middle_border.1 = (f32[64,16,256]{2,1,0:T(8,128)S(1)}, f32[8,16,256]{2,1,0:T(8,128)S(1)}, f32[8,16,256]{2,1,0:T(8,128)S(1)}, f32[8,16,256]{2,1,0:T(8,128)S(1)}, f32[8,16,256]{2,1,0:T(8,128)S(1)}) custom-call(f32[16]{0:T(128)S(1)} %copy-done, f32[64,16,256]{2,1,0:T(8,128)S(1)} %get-tuple-element.20.t_ref, ...), custom_call_target="tpu_custom_call", output_to_operand_aliasing={{0}: (7, {})} | custom-call | flops 10000000 | bytes 4194368 | tf_op jit(solution)/shard_map/middle_border/pallas_call | solution.py:28
  15.8 1.6 %collective-permute-start.5 = (f32[8,16,256]{2,1,0:T(8,128)S(1)}, f32[8,16,256]{2,1,0:T(8,128)S(1)}, u32[]{:S(2)}, u32[]{:S(2)}) collective-permute-start(f32[8,16,256]{2,1,0:T(8,128)S(1)} %get-tuple-element.31), channel_id=1, source_target_pairs={{0,1},{1,2},{2,3},{3,7},{4,0},{5,4},{6,5},{7,6},{8,9},{9,10},{10,1... | collective-permute-start | bytes 393224 | tf_op jit(solution)/shard_map/ppermute | solution.py:61
  17.4 2.5 %collective-permute-start.7 = (f32[8,16,256]{2,1,0:T(8,128)S(1)}, f32[8,16,256]{2,1,0:T(8,128)S(1)}, u32[]{:S(2)}, u32[]{:S(2)}) collective-permute-start(f32[8,16,256]{2,1,0:T(8,128)S(1)} %get-tuple-element.33), channel_id=1, source_target_pairs={{4,0},{5,1},{6,2},{7,3},{8,4},{9,5},{10,6},{11,7},{12,8},{13,9},{1... | collective-permute-start | bytes 393224 | tf_op jit(solution)/shard_map/ppermute | solution.py:61
  19.9 1.1 %final_inside.1.rest_8_ = f32[64,16,256]{2,1,0:T(8,128)S(1)} custom-call(f32[16]{0:T(128)S(1)} %copy-done, f32[64,16,256]{2,1,0:T(8,128)S(1)} %get-tuple-element.29.u_ref, f32[64,16,256]{2,1,0:T(8,128)S(1)} %get-tuple-element.23.h_ref), custom_call_target="tpu_custom_call" | custom-call | flops 10000000 | bytes 2097216 | tf_op jit(solution)/shard_map/final_inside/pallas_call | solution.py:28
  21.1 1.7 %collective-permute-done.6.rest_2_ = f32[8,16,256]{2,1,0:T(8,128)S(1)} collective-permute-done((f32[8,16,256]{2,1,0:T(8,128)S(1)}, f32[8,16,256]{2,1,0:T(8,128)S(1)}, u32[]{:S(2)}, u32[]{:S(2)}) %collective-permute-start.6) | collective-permute-done | bytes 131104 | tf_op jit(solution)/shard_map/ppermute | solution.py:61
  22.8 1.2 %observe.1 = (f32[64,16,256]{2,1,0:T(8,128)S(1)}, f32[32,256]{1,0:T(8,128)S(1)}) custom-call(f32[16]{0:T(128)S(1)} %copy-done, s32[32]{0:T(128)S(1)} %copy-done.1, f32[32]{0:T(128)S(1)} %copy-done.2, f32[32]{0:T(128)S(1)} %multiply_divide_fusion.factor_ref, f32[64,16,256]{2,1,0:T(8,128)S(1)} %get-tuple-element.29.u_ref, ...), custom_call_target="tpu_custom_call", output_to_operand_aliasing={{0}: (14, {})} | custom-call | flops 10000000 | bytes 4719040 | tf_op jit(solution)/shard_map/observe/pallas_call | solution.py:28
  24.0 2.0 %collective-permute-start.10 = (f32[32,256]{1,0:T(8,128)S(1)}, f32[32,256]{1,0:T(8,128)S(1)}, u32[]{:S(2)}, u32[]{:S(2)}) collective-permute-start(f32[32,256]{1,0:T(8,128)S(1)} %get-tuple-element.34.refs_0_), channel_id=1, source_target_pairs={{0,3},{1,2},{2,5},{3,4},{4,7},{5,6},{6,1},{7,0},{8,11},{9,10},{10,... | collective-permute-start | bytes 98312 | tf_op jit(solution)/shard_map/ppermute | solution.py:292
  26.0 1.2 %collective-permute-start.8 = (f32[32,256]{1,0:T(8,128)S(1)}, f32[32,256]{1,0:T(8,128)S(1)}, u32[]{:S(2)}, u32[]{:S(2)}) collective-permute-start(f32[32,256]{1,0:T(8,128)S(1)} %get-tuple-element.34.refs_0_), channel_id=1, source_target_pairs={{0,1},{1,3},{2,0},{3,2},{4,5},{5,7},{6,4},{7,6},{8,9},{9,11},{10,8... | collective-permute-start | bytes 98312 | tf_op jit(solution)/shard_map/ppermute | solution.py:292
  27.2 1.7 %collective-permute-start.9 = (f32[32,256]{1,0:T(8,128)S(1)}, f32[32,256]{1,0:T(8,128)S(1)}, u32[]{:S(2)}, u32[]{:S(2)}) collective-permute-start(f32[32,256]{1,0:T(8,128)S(1)} %get-tuple-element.34.refs_0_), channel_id=1, source_target_pairs={{1,0},{3,1},{0,2},{2,3},{5,4},{7,5},{4,6},{6,7},{9,8},{11,9},{8,10... | collective-permute-start | bytes 98312 | tf_op jit(solution)/shard_map/ppermute | solution.py:292
  28.9 0.4 collective-permute-done.10.refs_3_
  29.3 1.5 %collective-permute-done.8.refs_1_ = f32[32,256]{1,0:T(8,128)S(1)} collective-permute-done((f32[32,256]{1,0:T(8,128)S(1)}, f32[32,256]{1,0:T(8,128)S(1)}, u32[]{:S(2)}, u32[]{:S(2)}) %collective-permute-start.8) | collective-permute-done | bytes 32800 | tf_op jit(solution)/shard_map/ppermute | solution.py:292
  30.8 0.5 collective-permute-done.9.refs_2_
  31.3 2.1 %collective-permute-start.12 = (f32[128,256]{1,0:T(8,128)S(1)}, f32[128,256]{1,0:T(8,128)S(1)}, u32[]{:S(2)}, u32[]{:S(2)}) collective-permute-start(f32[128,256]{1,0:T(8,128)S(1)} %pack.1.refs_0_), channel_id=1, source_target_pairs={{0,8},{1,9},{2,10},{3,11},{4,12},{5,13},{6,14},{7,15},{8,24},{9,25... | collective-permute-start | bytes 393224 | tf_op jit(solution)/shard_map/ppermute | solution.py:292
  33.4 2.3 %collective-permute-start.16 = (f32[128,256]{1,0:T(8,128)S(1)}, f32[128,256]{1,0:T(8,128)S(1)}, u32[]{:S(2)}, u32[]{:S(2)}) collective-permute-start(f32[128,256]{1,0:T(8,128)S(1)} %pack.1.refs_0_), channel_id=1, source_target_pairs={{0,24},{1,25},{2,26},{3,27},{4,28},{5,29},{6,30},{7,31},{8,16},{9,... | collective-permute-start | bytes 393224 | tf_op jit(solution)/shard_map/ppermute | solution.py:292
  35.7 0.7 %fusion.4 = f32[1024,256]{1,0:T(8,128)S(1)} fusion(s32[1024]{0:T(1024)S(1)} %get-tuple-element.41, s32[1024]{0:T(1024)S(1)} %get-tuple-element.40, s32[256]{0:T(256)S(1)} %and_select_fusion), kind=kLoop, calls=%fused_computation.6 | loop fusion | flops 4980736 | bytes 1057792 | tf_op jit(solution)/shard_map/mul | solution.py:540
  36.5 0.7 %collective-permute-done.12.refs_1_ = f32[128,256]{1,0:T(8,128)S(1)} collective-permute-done((f32[128,256]{1,0:T(8,128)S(1)}, f32[128,256]{1,0:T(8,128)S(1)}, u32[]{:S(2)}, u32[]{:S(2)}) %collective-permute-start.12) | collective-permute-done | bytes 131104 | tf_op jit(solution)/shard_map/ppermute | solution.py:292
  37.3 2.5 %collective-permute-done.14.refs_2_ = f32[128,256]{1,0:T(8,128)S(1)} collective-permute-done((f32[128,256]{1,0:T(8,128)S(1)}, f32[128,256]{1,0:T(8,128)S(1)}, u32[]{:S(2)}, u32[]{:S(2)}) %collective-permute-start.14) | collective-permute-done | bytes 131104 | tf_op jit(solution)/shard_map/ppermute | solution.py:292
  39.8 0.3 collective-permute-done.16.refs_3_
  40.1 0.2 collective-permute-start.17
  40.4 1.2 %partial_products.1.refs_5_ = f32[256,512]{1,0:T(8,128)S(1)} custom-call(f32[128,256]{1,0:T(8,128)S(1)} %pack.1.refs_0_, f32[128,256]{1,0:T(8,128)S(1)} %collective-permute-done.12.refs_1_, f32[128,256]{1,0:T(8,128)S(1)} %collective-permute-done.14.refs_2_, f32[128,256]{1,0:T(8,128)S(1)} %collective-permute-done.16.refs_3_, ...), custom_call_target="tpu_custom_call" | custom-call | flops 100000000 | bytes 1048576 | tf_op jit(solution)/shard_map/partial_products/pallas_call | solution.py:28
  41.6 9.7 %smooth.1 = (f32[1024,256]{1,0:T(8,128)}, f32[64,16,256]{2,1,0:T(8,128)}) custom-call(f32[128,256]{1,0:T(8,128)S(1)} %collective-permute-done.11.refs_0_, f32[128,256]{1,0:T(8,128)S(1)} %collective-permute-done.13.refs_1_, f32[128,256]{1,0:T(8,128)S(1)} %collective-permute-done.15.refs_2_, f32[128,256]{1,0:T(8,128)S(1)} %collective-permute-done.17.refs_3_, ...), custom_call_target="tpu_custom_call" | custom-call | flops 1000000000 | bytes 3670016 | tf_op jit(solution)/shard_map/smooth/pallas_call | solution.py:28
  (30 shorter events, 0.4 us)
Async XLA Ops:
  3.1 8.3 %collective-permute-start = (f32[2,8,16,256]{3,2,1,0:T(8,128)}, f32[2,8,16,256]{3,2,1,0:T(8,128)S(1)}, u32[]{:S(2)}, u32[]{:S(2)}) collective-permute-start(f32[2,8,16,256]{3,2,1,0:T(8,128)} %get-tuple-element.24), channel_id=1, source_target_pairs={{0,4},{1,5},{2,6},{3,7},{4,8},{5,9},{6,10},{7,11},{8,12},{9,13},{1... | collective-permute-start | bytes 786440 | tf_op jit(solution)/shard_map/ppermute | solution.py:61
  3.6 8.9 %collective-permute-start.1 = (f32[2,8,16,256]{3,2,1,0:T(8,128)}, f32[2,8,16,256]{3,2,1,0:T(8,128)S(1)}, u32[]{:S(2)}, u32[]{:S(2)}) collective-permute-start(f32[2,8,16,256]{3,2,1,0:T(8,128)} %get-tuple-element.25), channel_id=1, source_target_pairs={{0,1},{1,2},{2,3},{3,7},{4,0},{5,4},{6,5},{7,6},{8,9},{9,10},{10,1... | collective-permute-start | bytes 786440 | tf_op jit(solution)/shard_map/ppermute | solution.py:61
  6.2 8.4 %collective-permute-start.2 = (f32[2,8,16,256]{3,2,1,0:T(8,128)}, f32[2,8,16,256]{3,2,1,0:T(8,128)S(1)}, u32[]{:S(2)}, u32[]{:S(2)}) collective-permute-start(f32[2,8,16,256]{3,2,1,0:T(8,128)} %get-tuple-element.26), channel_id=1, source_target_pairs={{1,0},{2,1},{3,2},{7,3},{0,4},{4,5},{5,6},{6,7},{9,8},{10,9},{11,1... | collective-permute-start | bytes 786440 | tf_op jit(solution)/shard_map/ppermute | solution.py:61
  6.2 8.4 %collective-permute-start.3 = (f32[2,8,16,256]{3,2,1,0:T(8,128)S(1)}, f32[2,8,16,256]{3,2,1,0:T(8,128)S(1)}, u32[]{:S(2)}, u32[]{:S(2)}) collective-permute-start(f32[2,8,16,256]{3,2,1,0:T(8,128)S(1)} %get-tuple-element.27), channel_id=1, source_target_pairs={{4,0},{5,1},{6,2},{7,3},{8,4},{9,5},{10,6},{11,7},{12,8},{13,9},{1... | collective-permute-start | bytes 786440 | tf_op jit(solution)/shard_map/ppermute | solution.py:61
  9.4 0.7 %copy-start = (f32[16]{0:T(128)S(1)}, f32[16]{0:T(128)}, u32[]{:S(2)}) copy-start(f32[16]{0:T(128)} %courant_ref.7) | copy-start | bytes 196
  15.7 5.3 %collective-permute-start.4 = (f32[8,16,256]{2,1,0:T(8,128)S(1)}, f32[8,16,256]{2,1,0:T(8,128)S(1)}, u32[]{:S(2)}, u32[]{:S(2)}) collective-permute-start(f32[8,16,256]{2,1,0:T(8,128)S(1)} %get-tuple-element.30), channel_id=1, source_target_pairs={{0,4},{1,5},{2,6},{3,7},{4,8},{5,9},{6,10},{7,11},{8,12},{9,13},{1... | collective-permute-start | bytes 393224 | tf_op jit(solution)/shard_map/ppermute | solution.py:61
  15.8 5.3 %collective-permute-start.5 = (f32[8,16,256]{2,1,0:T(8,128)S(1)}, f32[8,16,256]{2,1,0:T(8,128)S(1)}, u32[]{:S(2)}, u32[]{:S(2)}) collective-permute-start(f32[8,16,256]{2,1,0:T(8,128)S(1)} %get-tuple-element.31), channel_id=1, source_target_pairs={{0,1},{1,2},{2,3},{3,7},{4,0},{5,4},{6,5},{7,6},{8,9},{9,10},{10,1... | collective-permute-start | bytes 393224 | tf_op jit(solution)/shard_map/ppermute | solution.py:61
  17.4 2.5 %copy-start.4 = (f32[32]{0:T(128)S(1)}, f32[32]{0:T(128)}, u32[]{:S(2)}) copy-start(f32[32]{0:T(128)} %param.17) | copy-start | bytes 388
  17.4 5.4 %collective-permute-start.6 = (f32[8,16,256]{2,1,0:T(8,128)S(1)}, f32[8,16,256]{2,1,0:T(8,128)S(1)}, u32[]{:S(2)}, u32[]{:S(2)}) collective-permute-start(f32[8,16,256]{2,1,0:T(8,128)S(1)} %get-tuple-element.32), channel_id=1, source_target_pairs={{1,0},{2,1},{3,2},{7,3},{0,4},{4,5},{5,6},{6,7},{9,8},{10,9},{11,1... | collective-permute-start | bytes 393224 | tf_op jit(solution)/shard_map/ppermute | solution.py:61
  17.4 5.4 %collective-permute-start.7 = (f32[8,16,256]{2,1,0:T(8,128)S(1)}, f32[8,16,256]{2,1,0:T(8,128)S(1)}, u32[]{:S(2)}, u32[]{:S(2)}) collective-permute-start(f32[8,16,256]{2,1,0:T(8,128)S(1)} %get-tuple-element.33), channel_id=1, source_target_pairs={{4,0},{5,1},{6,2},{7,3},{8,4},{9,5},{10,6},{11,7},{12,8},{13,9},{1... | collective-permute-start | bytes 393224 | tf_op jit(solution)/shard_map/ppermute | solution.py:61
  19.9 2.9 %copy-start.1 = (s32[32]{0:T(128)S(1)}, s32[32]{0:T(128)}, u32[]{:S(2)}) copy-start(s32[32]{0:T(128)} %cells_ref.1) | copy-start | bytes 388
  19.9 2.9 %copy-start.2 = (f32[32]{0:T(128)S(1)}, f32[32]{0:T(128)}, u32[]{:S(2)}) copy-start(f32[32]{0:T(128)} %reading_ref.1) | copy-start | bytes 388
  24.0 4.9 %copy-start.3 = (s32[256]{0:T(256)S(1)}, s32[256]{0:T(256)}, u32[]{:S(2)}) copy-start(s32[256]{0:T(256)} %param.18) | copy-start | bytes 3076
  24.0 5.3 %collective-permute-start.10 = (f32[32,256]{1,0:T(8,128)S(1)}, f32[32,256]{1,0:T(8,128)S(1)}, u32[]{:S(2)}, u32[]{:S(2)}) collective-permute-start(f32[32,256]{1,0:T(8,128)S(1)} %get-tuple-element.34.refs_0_), channel_id=1, source_target_pairs={{0,3},{1,2},{2,5},{3,4},{4,7},{5,6},{6,1},{7,0},{8,11},{9,10},{10,... | collective-permute-start | bytes 98312 | tf_op jit(solution)/shard_map/ppermute | solution.py:292
  26.0 4.9 %collective-permute-start.8 = (f32[32,256]{1,0:T(8,128)S(1)}, f32[32,256]{1,0:T(8,128)S(1)}, u32[]{:S(2)}, u32[]{:S(2)}) collective-permute-start(f32[32,256]{1,0:T(8,128)S(1)} %get-tuple-element.34.refs_0_), channel_id=1, source_target_pairs={{0,1},{1,3},{2,0},{3,2},{4,5},{5,7},{6,4},{7,6},{8,9},{9,11},{10,8... | collective-permute-start | bytes 98312 | tf_op jit(solution)/shard_map/ppermute | solution.py:292
  27.2 4.1 %collective-permute-start.9 = (f32[32,256]{1,0:T(8,128)S(1)}, f32[32,256]{1,0:T(8,128)S(1)}, u32[]{:S(2)}, u32[]{:S(2)}) collective-permute-start(f32[32,256]{1,0:T(8,128)S(1)} %get-tuple-element.34.refs_0_), channel_id=1, source_target_pairs={{1,0},{3,1},{0,2},{2,3},{5,4},{7,5},{4,6},{6,7},{9,8},{11,9},{8,10... | collective-permute-start | bytes 98312 | tf_op jit(solution)/shard_map/ppermute | solution.py:292
  31.3 5.9 %collective-permute-start.12 = (f32[128,256]{1,0:T(8,128)S(1)}, f32[128,256]{1,0:T(8,128)S(1)}, u32[]{:S(2)}, u32[]{:S(2)}) collective-permute-start(f32[128,256]{1,0:T(8,128)S(1)} %pack.1.refs_0_), channel_id=1, source_target_pairs={{0,8},{1,9},{2,10},{3,11},{4,12},{5,13},{6,14},{7,15},{8,24},{9,25... | collective-permute-start | bytes 393224 | tf_op jit(solution)/shard_map/ppermute | solution.py:292
  33.4 6.4 %collective-permute-start.14 = (f32[128,256]{1,0:T(8,128)S(1)}, f32[128,256]{1,0:T(8,128)S(1)}, u32[]{:S(2)}, u32[]{:S(2)}) collective-permute-start(f32[128,256]{1,0:T(8,128)S(1)} %pack.1.refs_0_), channel_id=1, source_target_pairs={{8,0},{9,1},{10,2},{11,3},{12,4},{13,5},{14,6},{15,7},{24,8},{25,9... | collective-permute-start | bytes 393224 | tf_op jit(solution)/shard_map/ppermute | solution.py:292
  33.4 6.7 %collective-permute-start.16 = (f32[128,256]{1,0:T(8,128)S(1)}, f32[128,256]{1,0:T(8,128)S(1)}, u32[]{:S(2)}, u32[]{:S(2)}) collective-permute-start(f32[128,256]{1,0:T(8,128)S(1)} %pack.1.refs_0_), channel_id=1, source_target_pairs={{0,24},{1,25},{2,26},{3,27},{4,28},{5,29},{6,30},{7,31},{8,16},{9,... | collective-permute-start | bytes 393224 | tf_op jit(solution)/shard_map/ppermute | solution.py:292
  36.4 5.1 %collective-permute-start.11 = (f32[128,256]{1,0:T(8,128)S(1)}, f32[128,256]{1,0:T(8,128)S(1)}, u32[]{:S(2)}, u32[]{:S(2)}) collective-permute-start(f32[128,256]{1,0:T(8,128)S(1)} %pack.1.refs_0_), channel_id=1, source_target_pairs={{0,4},{1,5},{2,6},{3,7},{4,0},{5,1},{6,2},{7,3},{8,12},{9,13},{10,... | collective-permute-start | bytes 393224 | tf_op jit(solution)/shard_map/ppermute | solution.py:292
  37.3 4.3 %collective-permute-start.13 = (f32[128,256]{1,0:T(8,128)S(1)}, f32[128,256]{1,0:T(8,128)S(1)}, u32[]{:S(2)}, u32[]{:S(2)}) collective-permute-start(f32[128,256]{1,0:T(8,128)S(1)} %collective-permute-done.12.refs_1_), channel_id=1, source_target_pairs={{0,4},{1,5},{2,6},{3,7},{4,0},{5,1},{6,2},{7,3},{8,12},{9,13},{10,... | collective-permute-start | bytes 393224 | tf_op jit(solution)/shard_map/ppermute | solution.py:292
  39.8 1.8 %collective-permute-start.15 = (f32[128,256]{1,0:T(8,128)S(1)}, f32[128,256]{1,0:T(8,128)S(1)}, u32[]{:S(2)}, u32[]{:S(2)}) collective-permute-start(f32[128,256]{1,0:T(8,128)S(1)} %collective-permute-done.14.refs_2_), channel_id=1, source_target_pairs={{0,4},{1,5},{2,6},{3,7},{4,0},{5,1},{6,2},{7,3},{8,12},{9,13},{10,... | collective-permute-start | bytes 393224 | tf_op jit(solution)/shard_map/ppermute | solution.py:292
  40.1 1.4 %collective-permute-start.17 = (f32[128,256]{1,0:T(8,128)S(1)}, f32[128,256]{1,0:T(8,128)S(1)}, u32[]{:S(2)}, u32[]{:S(2)}) collective-permute-start(f32[128,256]{1,0:T(8,128)S(1)} %collective-permute-done.16.refs_3_), channel_id=1, source_target_pairs={{0,4},{1,5},{2,6},{3,7},{4,0},{5,1},{6,2},{7,3},{8,12},{9,13},{10,... | collective-permute-start | bytes 393224 | tf_op jit(solution)/shard_map/ppermute | solution.py:292

commit v6 on v5

--- a/solution.py
+++ b/solution.py
@@ -9,7 +9,7 @@
 
 inflation = 4.0
 HIGHEST = lax.Precision.HIGHEST
-UPDATE = lax.Precision.HIGH
+THREE_PASS = lax.Precision.HIGH
 VMEM = pl.BlockSpec(memory_space=pltpu.VMEM)
 SMEM = pl.BlockSpec(memory_space=pltpu.SMEM)
 
@@ -368,7 +368,7 @@
     members = scaled.shape[1]
     spread = scaled - jnp.sum(scaled, axis=1, keepdims=True) * (1.0 / members)
     misfit = noise_ref[...] - scale * scaled
-    return product(spread, jnp.concatenate([spread, misfit], axis=1), 0, 0)
+    return product(spread, jnp.concatenate([spread, misfit], axis=1), 0, 0, THREE_PASS)
 
 
 def partial_products(scale, *refs):
@@ -401,7 +401,7 @@
     for n in range(sems.shape[0]):
         part = pl.ds(n * chunk, chunk)
         held_ref[part] = log_ref[part] + product(
-            log_ref[part], weights_ref[...], precision=UPDATE
+            log_ref[part], weights_ref[...], precision=THREE_PASS
         )
         copies.append(pltpu.make_async_copy(held_ref.at[part], updated_hbm.at[part], sems.at[n]))
         copies[-1].start()

time: 51.8 us -> 51.2 us (0.988)
  Pallas kernels: 18 us -> 17.1 us
    pallas_call x8, Pallas kernels: 18 us -> 17.1 us  [call(): pl.pallas_call(kernel, out_shape=outs, in_specs=specs, out_specs=jax.tree...]
  transfers between devices with their start and end apart: 18 -> 18, of which waited for: 9 -> 10; matrix products, arithmetic and copies ran while one was open for 3% -> 3% of each run, Pallas kernels for 7% -> 6%
where the time goes in v6:
time: 51.2 us; the launch traced here: 50.9 us
  starting transfers between devices  19.1 us (37%)
  Pallas kernels  17.1 us (33%)
  waiting for transfers between devices  11.3 us (22%)
  other arithmetic  1.56 us (3%)
  between operations  0.93 us (2%)
  local copies, waits for them, and re-layouts  0.82 us (2%)
    pallas_call x8, Pallas kernels, call(): pl.pallas_call(kernel, out_shape=outs, in_specs=specs, out_specs=jax.tree...  17.1 us
    ppermute x8, starting transfers between devices, exchange(): lax.ppermute(face, ('gx', 'gy'), route)  9.6 us
    ppermute x10, starting transfers between devices, send(): return lax.ppermute(block, ('gx', 'gy'), route)  9.52 us
    ppermute x10, waiting for transfers between devices, send(): return lax.ppermute(block, ('gx', 'gy'), route)  6.37 us
    ppermute x8, waiting for transfers between devices, exchange(): lax.ppermute(face, ('gx', 'gy'), route)  4.97 us
  transfers between devices with their start and end apart: 18, of which 10 were waited for; matrix products, arithmetic and copies ran while one was open for 3% of the time, Pallas kernels for 6%

profile of v6, /device:TPU:0, one launch (start us, length us, event | category | flops | bytes accessed | tf_op | source)
XLA Modules:
  0.0 50.9 jit_solution(7707297065674182909)
XLA Ops:
  0.6 2.5 %prepare.1 = (f32[64,16,256]{2,1,0:T(8,128)S(1)}, f32[64,16,256]{2,1,0:T(8,128)S(1)}, f32[16,128]{1,0:T(8,128)S(1)}, f32[2,8,16,256]{3,2,1,0:T(8,128)}, f32[2,8,...) custom-call(f32[64,16,256]{2,1,0:T(8,128)} %bitcast.8, f32[64,16,256]{2,1,0:T(8,128)} %bitcast.9, ...), custom_call_target="tpu_custom_call" | custom-call | bytes 2101280 | tf_op jit(solution)/shard_map/prepare/pallas_call | solution.py:28
  3.1 0.5 collective-permute-start
  3.6 2.6 %collective-permute-start.1 = (f32[2,8,16,256]{3,2,1,0:T(8,128)}, f32[2,8,16,256]{3,2,1,0:T(8,128)S(1)}, u32[]{:S(2)}, u32[]{:S(2)}) collective-permute-start(f32[2,8,16,256]{3,2,1,0:T(8,128)} %get-tuple-element.25), channel_id=1, source_target_pairs={{0,1},{1,2},{2,3},{3,7},{4,0},{5,4},{6,5},{7,6},{8,9},{9,10},{10,1... | collective-permute-start | bytes 786440 | tf_op jit(solution)/shard_map/ppermute | solution.py:61
  6.2 2.3 %collective-permute-start.3 = (f32[2,8,16,256]{3,2,1,0:T(8,128)S(1)}, f32[2,8,16,256]{3,2,1,0:T(8,128)S(1)}, u32[]{:S(2)}, u32[]{:S(2)}) collective-permute-start(f32[2,8,16,256]{3,2,1,0:T(8,128)S(1)} %get-tuple-element.27), channel_id=1, source_target_pairs={{4,0},{5,1},{6,2},{7,3},{8,4},{9,5},{10,6},{11,7},{12,8},{13,9},{1... | collective-permute-start | bytes 786440 | tf_op jit(solution)/shard_map/ppermute | solution.py:61
  8.6 0.7 %multiply_bitcast_fusion = s32[32]{0:T(128)S(1)} fusion(s32[32,32]{1,0:T(8,128)} %constant.73.clone, s32[]{:T(128)S(6)} %select_n.42), kind=kLoop, calls=%fused_computation.11 | loop fusion | flops 32 | bytes 260 | tf_op jit(solution)/shard_map/mul | solution.py:538
  9.3 0.1 multiply_remainder_fusion
  9.4 0.7 %copy-done = f32[16]{0:T(128)S(1)} copy-done((f32[16]{0:T(128)S(1)}, f32[16]{0:T(128)}, u32[]{:S(2)}) %copy-start) | copy-done | bytes 88
  10.1 1.3 %middle_inside.1 = (f32[64,16,256]{2,1,0:T(8,128)S(1)}, f32[64,16,256]{2,1,0:T(8,128)S(1)}) custom-call(f32[16]{0:T(128)S(1)} %copy-done, f32[64,16,256]{2,1,0:T(8,128)S(1)} %get-tuple-element.20.t_ref, f32[64,16,256]{2,1,0:T(8,128)S(1)} %get-tuple-element.21.log_ref, f32[16,128]{1,0:T(8,128)S(1)} %get-tuple-element.22.columns_ref), custom_call_target="tpu_custom_call" | custom-call | flops 10000000 | bytes 2105408 | tf_op jit(solution)/shard_map/middle_inside/pallas_call | solution.py:28
  11.5 1.1 %collective-permute-done.1.rest_1_.rest_5_ = f32[2,8,16,256]{3,2,1,0:T(8,128)S(1)} collective-permute-done((f32[2,8,16,256]{3,2,1,0:T(8,128)}, f32[2,8,16,256]{3,2,1,0:T(8,128)S(1)}, u32[]{:S(2)}, u32[]{:S(2)}) %collective-permute-start.1) | collective-permute-done | bytes 262176 | tf_op jit(solution)/shard_map/ppermute | solution.py:61
  12.5 2.2 %collective-permute-done.2.rest_2_.rest_6_ = f32[2,8,16,256]{3,2,1,0:T(8,128)S(1)} collective-permute-done((f32[2,8,16,256]{3,2,1,0:T(8,128)}, f32[2,8,16,256]{3,2,1,0:T(8,128)S(1)}, u32[]{:S(2)}, u32[]{:S(2)}) %collective-permute-start.2) | collective-permute-done | bytes 262176 | tf_op jit(solution)/shard_map/ppermute | solution.py:61
  14.7 1.0 %middle_border.1 = (f32[64,16,256]{2,1,0:T(8,128)S(1)}, f32[8,16,256]{2,1,0:T(8,128)S(1)}, f32[8,16,256]{2,1,0:T(8,128)S(1)}, f32[8,16,256]{2,1,0:T(8,128)S(1)}, f32[8,16,256]{2,1,0:T(8,128)S(1)}) custom-call(f32[16]{0:T(128)S(1)} %copy-done, f32[64,16,256]{2,1,0:T(8,128)S(1)} %get-tuple-element.20.t_ref, ...), custom_call_target="tpu_custom_call", output_to_operand_aliasing={{0}: (7, {})} | custom-call | flops 10000000 | bytes 4194368 | tf_op jit(solution)/shard_map/middle_border/pallas_call | solution.py:28
  15.8 1.6 %collective-permute-start.5 = (f32[8,16,256]{2,1,0:T(8,128)S(1)}, f32[8,16,256]{2,1,0:T(8,128)S(1)}, u32[]{:S(2)}, u32[]{:S(2)}) collective-permute-start(f32[8,16,256]{2,1,0:T(8,128)S(1)} %get-tuple-element.31), channel_id=1, source_target_pairs={{0,1},{1,2},{2,3},{3,7},{4,0},{5,4},{6,5},{7,6},{8,9},{9,10},{10,1... | collective-permute-start | bytes 393224 | tf_op jit(solution)/shard_map/ppermute | solution.py:61
  17.4 2.5 %collective-permute-start.7 = (f32[8,16,256]{2,1,0:T(8,128)S(1)}, f32[8,16,256]{2,1,0:T(8,128)S(1)}, u32[]{:S(2)}, u32[]{:S(2)}) collective-permute-start(f32[8,16,256]{2,1,0:T(8,128)S(1)} %get-tuple-element.33), channel_id=1, source_target_pairs={{4,0},{5,1},{6,2},{7,3},{8,4},{9,5},{10,6},{11,7},{12,8},{13,9},{1... | collective-permute-start | bytes 393224 | tf_op jit(solution)/shard_map/ppermute | solution.py:61
  19.9 1.1 %final_inside.1.rest_8_ = f32[64,16,256]{2,1,0:T(8,128)S(1)} custom-call(f32[16]{0:T(128)S(1)} %copy-done, f32[64,16,256]{2,1,0:T(8,128)S(1)} %get-tuple-element.29.u_ref, f32[64,16,256]{2,1,0:T(8,128)S(1)} %get-tuple-element.23.h_ref), custom_call_target="tpu_custom_call" | custom-call | flops 10000000 | bytes 2097216 | tf_op jit(solution)/shard_map/final_inside/pallas_call | solution.py:28
  21.1 1.7 %collective-permute-done.6.rest_2_ = f32[8,16,256]{2,1,0:T(8,128)S(1)} collective-permute-done((f32[8,16,256]{2,1,0:T(8,128)S(1)}, f32[8,16,256]{2,1,0:T(8,128)S(1)}, u32[]{:S(2)}, u32[]{:S(2)}) %collective-permute-start.6) | collective-permute-done | bytes 131104 | tf_op jit(solution)/shard_map/ppermute | solution.py:61
  22.8 1.2 %observe.1 = (f32[64,16,256]{2,1,0:T(8,128)S(1)}, f32[32,256]{1,0:T(8,128)S(1)}) custom-call(f32[16]{0:T(128)S(1)} %copy-done, s32[32]{0:T(128)S(1)} %copy-done.1, f32[32]{0:T(128)S(1)} %copy-done.2, f32[32]{0:T(128)S(1)} %multiply_divide_fusion.factor_ref, f32[64,16,256]{2,1,0:T(8,128)S(1)} %get-tuple-element.29.u_ref, ...), custom_call_target="tpu_custom_call", output_to_operand_aliasing={{0}: (14, {})} | custom-call | flops 10000000 | bytes 4719040 | tf_op jit(solution)/shard_map/observe/pallas_call | solution.py:28
  24.0 2.0 %collective-permute-start.10 = (f32[32,256]{1,0:T(8,128)S(1)}, f32[32,256]{1,0:T(8,128)S(1)}, u32[]{:S(2)}, u32[]{:S(2)}) collective-permute-start(f32[32,256]{1,0:T(8,128)S(1)} %get-tuple-element.34.refs_0_), channel_id=1, source_target_pairs={{0,3},{1,2},{2,5},{3,4},{4,7},{5,6},{6,1},{7,0},{8,11},{9,10},{10,... | collective-permute-start | bytes 98312 | tf_op jit(solution)/shard_map/ppermute | solution.py:292
  26.0 1.2 %collective-permute-start.8 = (f32[32,256]{1,0:T(8,128)S(1)}, f32[32,256]{1,0:T(8,128)S(1)}, u32[]{:S(2)}, u32[]{:S(2)}) collective-permute-start(f32[32,256]{1,0:T(8,128)S(1)} %get-tuple-element.34.refs_0_), channel_id=1, source_target_pairs={{0,1},{1,3},{2,0},{3,2},{4,5},{5,7},{6,4},{7,6},{8,9},{9,11},{10,8... | collective-permute-start | bytes 98312 | tf_op jit(solution)/shard_map/ppermute | solution.py:292
  27.2 1.7 %collective-permute-start.9 = (f32[32,256]{1,0:T(8,128)S(1)}, f32[32,256]{1,0:T(8,128)S(1)}, u32[]{:S(2)}, u32[]{:S(2)}) collective-permute-start(f32[32,256]{1,0:T(8,128)S(1)} %get-tuple-element.34.refs_0_), channel_id=1, source_target_pairs={{1,0},{3,1},{0,2},{2,3},{5,4},{7,5},{4,6},{6,7},{9,8},{11,9},{8,10... | collective-permute-start | bytes 98312 | tf_op jit(solution)/shard_map/ppermute | solution.py:292
  28.9 0.4 collective-permute-done.10.refs_3_
  29.3 1.5 %collective-permute-done.8.refs_1_ = f32[32,256]{1,0:T(8,128)S(1)} collective-permute-done((f32[32,256]{1,0:T(8,128)S(1)}, f32[32,256]{1,0:T(8,128)S(1)}, u32[]{:S(2)}, u32[]{:S(2)}) %collective-permute-start.8) | collective-permute-done | bytes 32800 | tf_op jit(solution)/shard_map/ppermute | solution.py:292
  30.8 0.5 collective-permute-done.9.refs_2_
  31.3 2.1 %collective-permute-start.12 = (f32[128,256]{1,0:T(8,128)S(1)}, f32[128,256]{1,0:T(8,128)S(1)}, u32[]{:S(2)}, u32[]{:S(2)}) collective-permute-start(f32[128,256]{1,0:T(8,128)S(1)} %pack.1.refs_0_), channel_id=1, source_target_pairs={{0,8},{1,9},{2,10},{3,11},{4,12},{5,13},{6,14},{7,15},{8,24},{9,25... | collective-permute-start | bytes 393224 | tf_op jit(solution)/shard_map/ppermute | solution.py:292
  33.4 2.3 %collective-permute-start.16 = (f32[128,256]{1,0:T(8,128)S(1)}, f32[128,256]{1,0:T(8,128)S(1)}, u32[]{:S(2)}, u32[]{:S(2)}) collective-permute-start(f32[128,256]{1,0:T(8,128)S(1)} %pack.1.refs_0_), channel_id=1, source_target_pairs={{0,24},{1,25},{2,26},{3,27},{4,28},{5,29},{6,30},{7,31},{8,16},{9,... | collective-permute-start | bytes 393224 | tf_op jit(solution)/shard_map/ppermute | solution.py:292
  35.7 0.7 %fusion.4 = f32[1024,256]{1,0:T(8,128)S(1)} fusion(s32[1024]{0:T(1024)S(1)} %get-tuple-element.41, s32[1024]{0:T(1024)S(1)} %get-tuple-element.40, s32[256]{0:T(256)S(1)} %and_select_fusion), kind=kLoop, calls=%fused_computation.6 | loop fusion | flops 4980736 | bytes 1057792 | tf_op jit(solution)/shard_map/mul | solution.py:540
  36.5 0.7 %collective-permute-done.12.refs_1_ = f32[128,256]{1,0:T(8,128)S(1)} collective-permute-done((f32[128,256]{1,0:T(8,128)S(1)}, f32[128,256]{1,0:T(8,128)S(1)}, u32[]{:S(2)}, u32[]{:S(2)}) %collective-permute-start.12) | collective-permute-done | bytes 131104 | tf_op jit(solution)/shard_map/ppermute | solution.py:292
  37.3 2.5 %collective-permute-done.14.refs_2_ = f32[128,256]{1,0:T(8,128)S(1)} collective-permute-done((f32[128,256]{1,0:T(8,128)S(1)}, f32[128,256]{1,0:T(8,128)S(1)}, u32[]{:S(2)}, u32[]{:S(2)}) %collective-permute-start.14) | collective-permute-done | bytes 131104 | tf_op jit(solution)/shard_map/ppermute | solution.py:292
  39.8 0.3 collective-permute-done.16.refs_3_
  40.1 0.2 collective-permute-start.17
  40.4 0.7 %partial_products.1.refs_5_ = f32[256,512]{1,0:T(8,128)S(1)} custom-call(f32[128,256]{1,0:T(8,128)S(1)} %pack.1.refs_0_, f32[128,256]{1,0:T(8,128)S(1)} %collective-permute-done.12.refs_1_, f32[128,256]{1,0:T(8,128)S(1)} %collective-permute-done.14.refs_2_, f32[128,256]{1,0:T(8,128)S(1)} %collective-permute-done.16.refs_3_, ...), custom_call_target="tpu_custom_call" | custom-call | flops 100000000 | bytes 1048576 | tf_op jit(solution)/shard_map/partial_products/pallas_call | solution.py:28
  41.1 0.3 collective-permute-done.17.refs_3_
  41.5 9.3 %smooth.1 = (f32[1024,256]{1,0:T(8,128)}, f32[64,16,256]{2,1,0:T(8,128)}) custom-call(f32[128,256]{1,0:T(8,128)S(1)} %collective-permute-done.11.refs_0_, f32[128,256]{1,0:T(8,128)S(1)} %collective-permute-done.13.refs_1_, f32[128,256]{1,0:T(8,128)S(1)} %collective-permute-done.15.refs_2_, f32[128,256]{1,0:T(8,128)S(1)} %collective-permute-done.17.refs_3_, ...), custom_call_target="tpu_custom_call" | custom-call | flops 1000000000 | bytes 3670016 | tf_op jit(solution)/shard_map/smooth/pallas_call | solution.py:28
  (30 shorter events, 0.5 us)
Async XLA Ops:
  3.1 8.3 %collective-permute-start = (f32[2,8,16,256]{3,2,1,0:T(8,128)}, f32[2,8,16,256]{3,2,1,0:T(8,128)S(1)}, u32[]{:S(2)}, u32[]{:S(2)}) collective-permute-start(f32[2,8,16,256]{3,2,1,0:T(8,128)} %get-tuple-element.24), channel_id=1, source_target_pairs={{0,4},{1,5},{2,6},{3,7},{4,8},{5,9},{6,10},{7,11},{8,12},{9,13},{1... | collective-permute-start | bytes 786440 | tf_op jit(solution)/shard_map/ppermute | solution.py:61
  3.6 8.9 %collective-permute-start.1 = (f32[2,8,16,256]{3,2,1,0:T(8,128)}, f32[2,8,16,256]{3,2,1,0:T(8,128)S(1)}, u32[]{:S(2)}, u32[]{:S(2)}) collective-permute-start(f32[2,8,16,256]{3,2,1,0:T(8,128)} %get-tuple-element.25), channel_id=1, source_target_pairs={{0,1},{1,2},{2,3},{3,7},{4,0},{5,4},{6,5},{7,6},{8,9},{9,10},{10,1... | collective-permute-start | bytes 786440 | tf_op jit(solution)/shard_map/ppermute | solution.py:61
  6.2 8.4 %collective-permute-start.2 = (f32[2,8,16,256]{3,2,1,0:T(8,128)}, f32[2,8,16,256]{3,2,1,0:T(8,128)S(1)}, u32[]{:S(2)}, u32[]{:S(2)}) collective-permute-start(f32[2,8,16,256]{3,2,1,0:T(8,128)} %get-tuple-element.26), channel_id=1, source_target_pairs={{1,0},{2,1},{3,2},{7,3},{0,4},{4,5},{5,6},{6,7},{9,8},{10,9},{11,1... | collective-permute-start | bytes 786440 | tf_op jit(solution)/shard_map/ppermute | solution.py:61
  6.2 8.4 %collective-permute-start.3 = (f32[2,8,16,256]{3,2,1,0:T(8,128)S(1)}, f32[2,8,16,256]{3,2,1,0:T(8,128)S(1)}, u32[]{:S(2)}, u32[]{:S(2)}) collective-permute-start(f32[2,8,16,256]{3,2,1,0:T(8,128)S(1)} %get-tuple-element.27), channel_id=1, source_target_pairs={{4,0},{5,1},{6,2},{7,3},{8,4},{9,5},{10,6},{11,7},{12,8},{13,9},{1... | collective-permute-start | bytes 786440 | tf_op jit(solution)/shard_map/ppermute | solution.py:61
  9.4 0.7 %copy-start = (f32[16]{0:T(128)S(1)}, f32[16]{0:T(128)}, u32[]{:S(2)}) copy-start(f32[16]{0:T(128)} %courant_ref.7) | copy-start | bytes 196
  15.7 5.3 %collective-permute-start.4 = (f32[8,16,256]{2,1,0:T(8,128)S(1)}, f32[8,16,256]{2,1,0:T(8,128)S(1)}, u32[]{:S(2)}, u32[]{:S(2)}) collective-permute-start(f32[8,16,256]{2,1,0:T(8,128)S(1)} %get-tuple-element.30), channel_id=1, source_target_pairs={{0,4},{1,5},{2,6},{3,7},{4,8},{5,9},{6,10},{7,11},{8,12},{9,13},{1... | collective-permute-start | bytes 393224 | tf_op jit(solution)/shard_map/ppermute | solution.py:61
  15.8 5.3 %collective-permute-start.5 = (f32[8,16,256]{2,1,0:T(8,128)S(1)}, f32[8,16,256]{2,1,0:T(8,128)S(1)}, u32[]{:S(2)}, u32[]{:S(2)}) collective-permute-start(f32[8,16,256]{2,1,0:T(8,128)S(1)} %get-tuple-element.31), channel_id=1, source_target_pairs={{0,1},{1,2},{2,3},{3,7},{4,0},{5,4},{6,5},{7,6},{8,9},{9,10},{10,1... | collective-permute-start | bytes 393224 | tf_op jit(solution)/shard_map/ppermute | solution.py:61
  17.4 2.5 %copy-start.4 = (f32[32]{0:T(128)S(1)}, f32[32]{0:T(128)}, u32[]{:S(2)}) copy-start(f32[32]{0:T(128)} %param.17) | copy-start | bytes 388
  17.4 5.4 %collective-permute-start.6 = (f32[8,16,256]{2,1,0:T(8,128)S(1)}, f32[8,16,256]{2,1,0:T(8,128)S(1)}, u32[]{:S(2)}, u32[]{:S(2)}) collective-permute-start(f32[8,16,256]{2,1,0:T(8,128)S(1)} %get-tuple-element.32), channel_id=1, source_target_pairs={{1,0},{2,1},{3,2},{7,3},{0,4},{4,5},{5,6},{6,7},{9,8},{10,9},{11,1... | collective-permute-start | bytes 393224 | tf_op jit(solution)/shard_map/ppermute | solution.py:61
  17.4 5.4 %collective-permute-start.7 = (f32[8,16,256]{2,1,0:T(8,128)S(1)}, f32[8,16,256]{2,1,0:T(8,128)S(1)}, u32[]{:S(2)}, u32[]{:S(2)}) collective-permute-start(f32[8,16,256]{2,1,0:T(8,128)S(1)} %get-tuple-element.33), channel_id=1, source_target_pairs={{4,0},{5,1},{6,2},{7,3},{8,4},{9,5},{10,6},{11,7},{12,8},{13,9},{1... | collective-permute-start | bytes 393224 | tf_op jit(solution)/shard_map/ppermute | solution.py:61
  19.9 2.9 %copy-start.1 = (s32[32]{0:T(128)S(1)}, s32[32]{0:T(128)}, u32[]{:S(2)}) copy-start(s32[32]{0:T(128)} %cells_ref.1) | copy-start | bytes 388
  19.9 2.9 %copy-start.2 = (f32[32]{0:T(128)S(1)}, f32[32]{0:T(128)}, u32[]{:S(2)}) copy-start(f32[32]{0:T(128)} %reading_ref.1) | copy-start | bytes 388
  24.0 4.9 %copy-start.3 = (s32[256]{0:T(256)S(1)}, s32[256]{0:T(256)}, u32[]{:S(2)}) copy-start(s32[256]{0:T(256)} %param.18) | copy-start | bytes 3076
  24.0 5.3 %collective-permute-start.10 = (f32[32,256]{1,0:T(8,128)S(1)}, f32[32,256]{1,0:T(8,128)S(1)}, u32[]{:S(2)}, u32[]{:S(2)}) collective-permute-start(f32[32,256]{1,0:T(8,128)S(1)} %get-tuple-element.34.refs_0_), channel_id=1, source_target_pairs={{0,3},{1,2},{2,5},{3,4},{4,7},{5,6},{6,1},{7,0},{8,11},{9,10},{10,... | collective-permute-start | bytes 98312 | tf_op jit(solution)/shard_map/ppermute | solution.py:292
  26.0 4.9 %collective-permute-start.8 = (f32[32,256]{1,0:T(8,128)S(1)}, f32[32,256]{1,0:T(8,128)S(1)}, u32[]{:S(2)}, u32[]{:S(2)}) collective-permute-start(f32[32,256]{1,0:T(8,128)S(1)} %get-tuple-element.34.refs_0_), channel_id=1, source_target_pairs={{0,1},{1,3},{2,0},{3,2},{4,5},{5,7},{6,4},{7,6},{8,9},{9,11},{10,8... | collective-permute-start | bytes 98312 | tf_op jit(solution)/shard_map/ppermute | solution.py:292
  27.2 4.1 %collective-permute-start.9 = (f32[32,256]{1,0:T(8,128)S(1)}, f32[32,256]{1,0:T(8,128)S(1)}, u32[]{:S(2)}, u32[]{:S(2)}) collective-permute-start(f32[32,256]{1,0:T(8,128)S(1)} %get-tuple-element.34.refs_0_), channel_id=1, source_target_pairs={{1,0},{3,1},{0,2},{2,3},{5,4},{7,5},{4,6},{6,7},{9,8},{11,9},{8,10... | collective-permute-start | bytes 98312 | tf_op jit(solution)/shard_map/ppermute | solution.py:292
  31.3 5.9 %collective-permute-start.12 = (f32[128,256]{1,0:T(8,128)S(1)}, f32[128,256]{1,0:T(8,128)S(1)}, u32[]{:S(2)}, u32[]{:S(2)}) collective-permute-start(f32[128,256]{1,0:T(8,128)S(1)} %pack.1.refs_0_), channel_id=1, source_target_pairs={{0,8},{1,9},{2,10},{3,11},{4,12},{5,13},{6,14},{7,15},{8,24},{9,25... | collective-permute-start | bytes 393224 | tf_op jit(solution)/shard_map/ppermute | solution.py:292
  33.4 6.4 %collective-permute-start.14 = (f32[128,256]{1,0:T(8,128)S(1)}, f32[128,256]{1,0:T(8,128)S(1)}, u32[]{:S(2)}, u32[]{:S(2)}) collective-permute-start(f32[128,256]{1,0:T(8,128)S(1)} %pack.1.refs_0_), channel_id=1, source_target_pairs={{8,0},{9,1},{10,2},{11,3},{12,4},{13,5},{14,6},{15,7},{24,8},{25,9... | collective-permute-start | bytes 393224 | tf_op jit(solution)/shard_map/ppermute | solution.py:292
  33.4 6.7 %collective-permute-start.16 = (f32[128,256]{1,0:T(8,128)S(1)}, f32[128,256]{1,0:T(8,128)S(1)}, u32[]{:S(2)}, u32[]{:S(2)}) collective-permute-start(f32[128,256]{1,0:T(8,128)S(1)} %pack.1.refs_0_), channel_id=1, source_target_pairs={{0,24},{1,25},{2,26},{3,27},{4,28},{5,29},{6,30},{7,31},{8,16},{9,... | collective-permute-start | bytes 393224 | tf_op jit(solution)/shard_map/ppermute | solution.py:292
  36.4 4.6 %collective-permute-start.11 = (f32[128,256]{1,0:T(8,128)S(1)}, f32[128,256]{1,0:T(8,128)S(1)}, u32[]{:S(2)}, u32[]{:S(2)}) collective-permute-start(f32[128,256]{1,0:T(8,128)S(1)} %pack.1.refs_0_), channel_id=1, source_target_pairs={{0,4},{1,5},{2,6},{3,7},{4,0},{5,1},{6,2},{7,3},{8,12},{9,13},{10,... | collective-permute-start | bytes 393224 | tf_op jit(solution)/shard_map/ppermute | solution.py:292
  37.3 3.8 %collective-permute-start.13 = (f32[128,256]{1,0:T(8,128)S(1)}, f32[128,256]{1,0:T(8,128)S(1)}, u32[]{:S(2)}, u32[]{:S(2)}) collective-permute-start(f32[128,256]{1,0:T(8,128)S(1)} %collective-permute-done.12.refs_1_), channel_id=1, source_target_pairs={{0,4},{1,5},{2,6},{3,7},{4,0},{5,1},{6,2},{7,3},{8,12},{9,13},{10,... | collective-permute-start | bytes 393224 | tf_op jit(solution)/shard_map/ppermute | solution.py:292
  39.8 1.3 %collective-permute-start.15 = (f32[128,256]{1,0:T(8,128)S(1)}, f32[128,256]{1,0:T(8,128)S(1)}, u32[]{:S(2)}, u32[]{:S(2)}) collective-permute-start(f32[128,256]{1,0:T(8,128)S(1)} %collective-permute-done.14.refs_2_), channel_id=1, source_target_pairs={{0,4},{1,5},{2,6},{3,7},{4,0},{5,1},{6,2},{7,3},{8,12},{9,13},{10,... | collective-permute-start | bytes 393224 | tf_op jit(solution)/shard_map/ppermute | solution.py:292
  40.1 1.3 %collective-permute-start.17 = (f32[128,256]{1,0:T(8,128)S(1)}, f32[128,256]{1,0:T(8,128)S(1)}, u32[]{:S(2)}, u32[]{:S(2)}) collective-permute-start(f32[128,256]{1,0:T(8,128)S(1)} %collective-permute-done.16.refs_3_), channel_id=1, source_target_pairs={{0,4},{1,5},{2,6},{3,7},{4,0},{5,1},{6,2},{7,3},{8,12},{9,13},{10,... | collective-permute-start | bytes 393224 | tf_op jit(solution)/shard_map/ppermute | solution.py:292

commit v7 on v6

--- a/solution.py
+++ b/solution.py
@@ -102,10 +102,16 @@
     t_ref, log_ref, columns_ref, *face_refs, h_ref, turned, code_ref, rock_ref, sems = rest
     span_x, span_y = rows
     depth = t_ref.shape[1]
+    half = log_ref.shape[0] // 2
+    low, high = pl.ds(0, half), pl.ds(half, half)
+    pairs = (
+        (code_hbm, code_ref), (rock_hbm, rock_ref), (log_hbm.at[low], log_ref.at[low]),
+        (log_hbm.at[high], log_ref.at[high]), (t_hbm, t_ref),
+    )
     copies = [
         pltpu.make_async_copy(source, target, sems.at[n])
         for n, (source, target) in enumerate(
-            ((code_hbm, code_ref), (rock_hbm, rock_ref), (log_hbm, log_ref), (t_hbm, t_ref))
+            pairs
         )
     ]
     for copy in copies:
@@ -120,8 +126,11 @@
             base = jnp.where(code == level, 0.5 * rock_ref[level], base)
         turned[x * span_y : (x + 1) * span_y, :depth] = base
     columns_ref[...] = jnp.transpose(turned[...])[:depth]
+    cells = border(rows, True)
     copies[2].wait()
-    conductivity(rows, border(rows, True), log_ref, columns_ref, h_ref)
+    conductivity(rows, [c for c in cells if c[0] * span_y < half], log_ref, columns_ref, h_ref)
+    copies[3].wait()
+    conductivity(rows, [c for c in cells if c[0] * span_y >= half], log_ref, columns_ref, h_ref)
 
     def put(field):
         def store(n, k, layer):
@@ -130,7 +139,7 @@
         return store
 
     store_faces(h_ref, rows, put(1))
-    copies[3].wait()
+    copies[4].wait()
     store_faces(t_ref, rows, put(0))
 
 
@@ -498,7 +507,7 @@
             pltpu.VMEM((columns, 128), jnp.float32),
             pltpu.VMEM(rock_class_code.shape, jnp.int32),
             pltpu.SMEM(levels, jnp.float32),
-            pltpu.SemaphoreType.DMA((4,)),
+            pltpu.SemaphoreType.DMA((5,)),
         ],
     )
     got = exchange(sent)

time: 51.2 us -> 51.2 us (level)
  no operation moved by 1% of the time
where the time goes in v7:
time: 51.2 us; the launch traced here: 50.9 us
  starting transfers between devices  19.1 us (37%)
  Pallas kernels  17.1 us (33%)
  waiting for transfers between devices  11.3 us (22%)
  other arithmetic  1.56 us (3%)
  between operations  0.93 us (2%)
  local copies, waits for them, and re-layouts  0.82 us (2%)
    pallas_call x8, Pallas kernels, call(): pl.pallas_call(kernel, out_shape=outs, in_specs=specs, out_specs=jax.tree...  17.1 us
    ppermute x8, starting transfers between devices, exchange(): lax.ppermute(face, ('gx', 'gy'), route)  9.6 us
    ppermute x10, starting transfers between devices, send(): return lax.ppermute(block, ('gx', 'gy'), route)  9.52 us
    ppermute x10, waiting for transfers between devices, send(): return lax.ppermute(block, ('gx', 'gy'), route)  6.37 us
    ppermute x8, waiting for transfers between devices, exchange(): lax.ppermute(face, ('gx', 'gy'), route)  4.97 us
  transfers between devices with their start and end apart: 18, of which 10 were waited for; matrix products, arithmetic and copies ran while one was open for 3% of the time, Pallas kernels for 6%

profile of v7, /device:TPU:0, one launch (start us, length us, event | category | flops | bytes accessed | tf_op | source)
XLA Modules:
  0.0 50.9 jit_solution(10108613799419729788)
XLA Ops:
  0.6 2.5 %prepare.1 = (f32[64,16,256]{2,1,0:T(8,128)S(1)}, f32[64,16,256]{2,1,0:T(8,128)S(1)}, f32[16,128]{1,0:T(8,128)S(1)}, f32[2,8,16,256]{3,2,1,0:T(8,128)}, f32[2,8,...) custom-call(f32[64,16,256]{2,1,0:T(8,128)} %bitcast.8, f32[64,16,256]{2,1,0:T(8,128)} %bitcast.9, ...), custom_call_target="tpu_custom_call" | custom-call | bytes 2101280 | tf_op jit(solution)/shard_map/prepare/pallas_call | solution.py:28
  3.1 0.5 collective-permute-start
  3.6 2.6 %collective-permute-start.1 = (f32[2,8,16,256]{3,2,1,0:T(8,128)}, f32[2,8,16,256]{3,2,1,0:T(8,128)S(1)}, u32[]{:S(2)}, u32[]{:S(2)}) collective-permute-start(f32[2,8,16,256]{3,2,1,0:T(8,128)} %get-tuple-element.25), channel_id=1, source_target_pairs={{0,1},{1,2},{2,3},{3,7},{4,0},{5,4},{6,5},{7,6},{8,9},{9,10},{10,1... | collective-permute-start | bytes 786440 | tf_op jit(solution)/shard_map/ppermute | solution.py:61
  6.3 2.3 %collective-permute-start.3 = (f32[2,8,16,256]{3,2,1,0:T(8,128)S(1)}, f32[2,8,16,256]{3,2,1,0:T(8,128)S(1)}, u32[]{:S(2)}, u32[]{:S(2)}) collective-permute-start(f32[2,8,16,256]{3,2,1,0:T(8,128)S(1)} %get-tuple-element.27), channel_id=1, source_target_pairs={{4,0},{5,1},{6,2},{7,3},{8,4},{9,5},{10,6},{11,7},{12,8},{13,9},{1... | collective-permute-start | bytes 786440 | tf_op jit(solution)/shard_map/ppermute | solution.py:61
  8.6 0.7 %multiply_bitcast_fusion = s32[32]{0:T(128)S(1)} fusion(s32[32,32]{1,0:T(8,128)} %constant.73.clone, s32[]{:T(128)S(6)} %select_n.42), kind=kLoop, calls=%fused_computation.11 | loop fusion | flops 32 | bytes 260 | tf_op jit(solution)/shard_map/mul | solution.py:547
  9.3 0.1 multiply_remainder_fusion
  9.4 0.7 %copy-done = f32[16]{0:T(128)S(1)} copy-done((f32[16]{0:T(128)S(1)}, f32[16]{0:T(128)}, u32[]{:S(2)}) %copy-start) | copy-done | bytes 88
  10.1 1.3 %middle_inside.1 = (f32[64,16,256]{2,1,0:T(8,128)S(1)}, f32[64,16,256]{2,1,0:T(8,128)S(1)}) custom-call(f32[16]{0:T(128)S(1)} %copy-done, f32[64,16,256]{2,1,0:T(8,128)S(1)} %get-tuple-element.20.t_ref, f32[64,16,256]{2,1,0:T(8,128)S(1)} %get-tuple-element.21.log_ref, f32[16,128]{1,0:T(8,128)S(1)} %get-tuple-element.22.columns_ref), custom_call_target="tpu_custom_call" | custom-call | flops 10000000 | bytes 2105408 | tf_op jit(solution)/shard_map/middle_inside/pallas_call | solution.py:28
  11.5 1.1 %collective-permute-done.1.rest_1_.rest_5_ = f32[2,8,16,256]{3,2,1,0:T(8,128)S(1)} collective-permute-done((f32[2,8,16,256]{3,2,1,0:T(8,128)}, f32[2,8,16,256]{3,2,1,0:T(8,128)S(1)}, u32[]{:S(2)}, u32[]{:S(2)}) %collective-permute-start.1) | collective-permute-done | bytes 262176 | tf_op jit(solution)/shard_map/ppermute | solution.py:61
  12.5 2.2 %collective-permute-done.2.rest_2_.rest_6_ = f32[2,8,16,256]{3,2,1,0:T(8,128)S(1)} collective-permute-done((f32[2,8,16,256]{3,2,1,0:T(8,128)}, f32[2,8,16,256]{3,2,1,0:T(8,128)S(1)}, u32[]{:S(2)}, u32[]{:S(2)}) %collective-permute-start.2) | collective-permute-done | bytes 262176 | tf_op jit(solution)/shard_map/ppermute | solution.py:61
  14.7 1.0 %middle_border.1 = (f32[64,16,256]{2,1,0:T(8,128)S(1)}, f32[8,16,256]{2,1,0:T(8,128)S(1)}, f32[8,16,256]{2,1,0:T(8,128)S(1)}, f32[8,16,256]{2,1,0:T(8,128)S(1)}, f32[8,16,256]{2,1,0:T(8,128)S(1)}) custom-call(f32[16]{0:T(128)S(1)} %copy-done, f32[64,16,256]{2,1,0:T(8,128)S(1)} %get-tuple-element.20.t_ref, ...), custom_call_target="tpu_custom_call", output_to_operand_aliasing={{0}: (7, {})} | custom-call | flops 10000000 | bytes 4194368 | tf_op jit(solution)/shard_map/middle_border/pallas_call | solution.py:28
  15.8 1.6 %collective-permute-start.5 = (f32[8,16,256]{2,1,0:T(8,128)S(1)}, f32[8,16,256]{2,1,0:T(8,128)S(1)}, u32[]{:S(2)}, u32[]{:S(2)}) collective-permute-start(f32[8,16,256]{2,1,0:T(8,128)S(1)} %get-tuple-element.31), channel_id=1, source_target_pairs={{0,1},{1,2},{2,3},{3,7},{4,0},{5,4},{6,5},{7,6},{8,9},{9,10},{10,1... | collective-permute-start | bytes 393224 | tf_op jit(solution)/shard_map/ppermute | solution.py:61
  17.4 2.5 %collective-permute-start.7 = (f32[8,16,256]{2,1,0:T(8,128)S(1)}, f32[8,16,256]{2,1,0:T(8,128)S(1)}, u32[]{:S(2)}, u32[]{:S(2)}) collective-permute-start(f32[8,16,256]{2,1,0:T(8,128)S(1)} %get-tuple-element.33), channel_id=1, source_target_pairs={{4,0},{5,1},{6,2},{7,3},{8,4},{9,5},{10,6},{11,7},{12,8},{13,9},{1... | collective-permute-start | bytes 393224 | tf_op jit(solution)/shard_map/ppermute | solution.py:61
  19.9 1.1 %final_inside.1.rest_8_ = f32[64,16,256]{2,1,0:T(8,128)S(1)} custom-call(f32[16]{0:T(128)S(1)} %copy-done, f32[64,16,256]{2,1,0:T(8,128)S(1)} %get-tuple-element.29.u_ref, f32[64,16,256]{2,1,0:T(8,128)S(1)} %get-tuple-element.23.h_ref), custom_call_target="tpu_custom_call" | custom-call | flops 10000000 | bytes 2097216 | tf_op jit(solution)/shard_map/final_inside/pallas_call | solution.py:28
  21.1 1.7 %collective-permute-done.6.rest_2_ = f32[8,16,256]{2,1,0:T(8,128)S(1)} collective-permute-done((f32[8,16,256]{2,1,0:T(8,128)S(1)}, f32[8,16,256]{2,1,0:T(8,128)S(1)}, u32[]{:S(2)}, u32[]{:S(2)}) %collective-permute-start.6) | collective-permute-done | bytes 131104 | tf_op jit(solution)/shard_map/ppermute | solution.py:61
  22.8 1.2 %observe.1 = (f32[64,16,256]{2,1,0:T(8,128)S(1)}, f32[32,256]{1,0:T(8,128)S(1)}) custom-call(f32[16]{0:T(128)S(1)} %copy-done, s32[32]{0:T(128)S(1)} %copy-done.1, f32[32]{0:T(128)S(1)} %copy-done.2, f32[32]{0:T(128)S(1)} %multiply_divide_fusion.factor_ref, f32[64,16,256]{2,1,0:T(8,128)S(1)} %get-tuple-element.29.u_ref, ...), custom_call_target="tpu_custom_call", output_to_operand_aliasing={{0}: (14, {})} | custom-call | flops 10000000 | bytes 4719040 | tf_op jit(solution)/shard_map/observe/pallas_call | solution.py:28
  24.0 2.0 %collective-permute-start.10 = (f32[32,256]{1,0:T(8,128)S(1)}, f32[32,256]{1,0:T(8,128)S(1)}, u32[]{:S(2)}, u32[]{:S(2)}) collective-permute-start(f32[32,256]{1,0:T(8,128)S(1)} %get-tuple-element.34.refs_0_), channel_id=1, source_target_pairs={{0,3},{1,2},{2,5},{3,4},{4,7},{5,6},{6,1},{7,0},{8,11},{9,10},{10,... | collective-permute-start | bytes 98312 | tf_op jit(solution)/shard_map/ppermute | solution.py:301
  26.0 1.2 %collective-permute-start.8 = (f32[32,256]{1,0:T(8,128)S(1)}, f32[32,256]{1,0:T(8,128)S(1)}, u32[]{:S(2)}, u32[]{:S(2)}) collective-permute-start(f32[32,256]{1,0:T(8,128)S(1)} %get-tuple-element.34.refs_0_), channel_id=1, source_target_pairs={{0,1},{1,3},{2,0},{3,2},{4,5},{5,7},{6,4},{7,6},{8,9},{9,11},{10,8... | collective-permute-start | bytes 98312 | tf_op jit(solution)/shard_map/ppermute | solution.py:301
  27.2 1.7 %collective-permute-start.9 = (f32[32,256]{1,0:T(8,128)S(1)}, f32[32,256]{1,0:T(8,128)S(1)}, u32[]{:S(2)}, u32[]{:S(2)}) collective-permute-start(f32[32,256]{1,0:T(8,128)S(1)} %get-tuple-element.34.refs_0_), channel_id=1, source_target_pairs={{1,0},{3,1},{0,2},{2,3},{5,4},{7,5},{4,6},{6,7},{9,8},{11,9},{8,10... | collective-permute-start | bytes 98312 | tf_op jit(solution)/shard_map/ppermute | solution.py:301
  28.9 0.4 collective-permute-done.10.refs_3_
  29.3 1.5 %collective-permute-done.8.refs_1_ = f32[32,256]{1,0:T(8,128)S(1)} collective-permute-done((f32[32,256]{1,0:T(8,128)S(1)}, f32[32,256]{1,0:T(8,128)S(1)}, u32[]{:S(2)}, u32[]{:S(2)}) %collective-permute-start.8) | collective-permute-done | bytes 32800 | tf_op jit(solution)/shard_map/ppermute | solution.py:301
  30.8 0.5 collective-permute-done.9.refs_2_
  31.3 2.1 %collective-permute-start.12 = (f32[128,256]{1,0:T(8,128)S(1)}, f32[128,256]{1,0:T(8,128)S(1)}, u32[]{:S(2)}, u32[]{:S(2)}) collective-permute-start(f32[128,256]{1,0:T(8,128)S(1)} %pack.1.refs_0_), channel_id=1, source_target_pairs={{0,8},{1,9},{2,10},{3,11},{4,12},{5,13},{6,14},{7,15},{8,24},{9,25... | collective-permute-start | bytes 393224 | tf_op jit(solution)/shard_map/ppermute | solution.py:301
  33.4 2.3 %collective-permute-start.16 = (f32[128,256]{1,0:T(8,128)S(1)}, f32[128,256]{1,0:T(8,128)S(1)}, u32[]{:S(2)}, u32[]{:S(2)}) collective-permute-start(f32[128,256]{1,0:T(8,128)S(1)} %pack.1.refs_0_), channel_id=1, source_target_pairs={{0,24},{1,25},{2,26},{3,27},{4,28},{5,29},{6,30},{7,31},{8,16},{9,... | collective-permute-start | bytes 393224 | tf_op jit(solution)/shard_map/ppermute | solution.py:301
  35.7 0.7 %fusion.4 = f32[1024,256]{1,0:T(8,128)S(1)} fusion(s32[1024]{0:T(1024)S(1)} %get-tuple-element.41, s32[1024]{0:T(1024)S(1)} %get-tuple-element.40, s32[256]{0:T(256)S(1)} %and_select_fusion), kind=kLoop, calls=%fused_computation.6 | loop fusion | flops 4980736 | bytes 1057792 | tf_op jit(solution)/shard_map/mul | solution.py:549
  36.5 0.7 %collective-permute-done.12.refs_1_ = f32[128,256]{1,0:T(8,128)S(1)} collective-permute-done((f32[128,256]{1,0:T(8,128)S(1)}, f32[128,256]{1,0:T(8,128)S(1)}, u32[]{:S(2)}, u32[]{:S(2)}) %collective-permute-start.12) | collective-permute-done | bytes 131104 | tf_op jit(solution)/shard_map/ppermute | solution.py:301
  37.3 2.5 %collective-permute-done.14.refs_2_ = f32[128,256]{1,0:T(8,128)S(1)} collective-permute-done((f32[128,256]{1,0:T(8,128)S(1)}, f32[128,256]{1,0:T(8,128)S(1)}, u32[]{:S(2)}, u32[]{:S(2)}) %collective-permute-start.14) | collective-permute-done | bytes 131104 | tf_op jit(solution)/shard_map/ppermute | solution.py:301
  39.8 0.3 collective-permute-done.16.refs_3_
  40.1 0.2 collective-permute-start.17
  40.4 0.7 %partial_products.1.refs_5_ = f32[256,512]{1,0:T(8,128)S(1)} custom-call(f32[128,256]{1,0:T(8,128)S(1)} %pack.1.refs_0_, f32[128,256]{1,0:T(8,128)S(1)} %collective-permute-done.12.refs_1_, f32[128,256]{1,0:T(8,128)S(1)} %collective-permute-done.14.refs_2_, f32[128,256]{1,0:T(8,128)S(1)} %collective-permute-done.16.refs_3_, ...), custom_call_target="tpu_custom_call" | custom-call | flops 100000000 | bytes 1048576 | tf_op jit(solution)/shard_map/partial_products/pallas_call | solution.py:28
  41.1 0.3 collective-permute-done.17.refs_3_
  41.5 9.3 %smooth.1 = (f32[1024,256]{1,0:T(8,128)}, f32[64,16,256]{2,1,0:T(8,128)}) custom-call(f32[128,256]{1,0:T(8,128)S(1)} %collective-permute-done.11.refs_0_, f32[128,256]{1,0:T(8,128)S(1)} %collective-permute-done.13.refs_1_, f32[128,256]{1,0:T(8,128)S(1)} %collective-permute-done.15.refs_2_, f32[128,256]{1,0:T(8,128)S(1)} %collective-permute-done.17.refs_3_, ...), custom_call_target="tpu_custom_call" | custom-call | flops 1000000000 | bytes 3670016 | tf_op jit(solution)/shard_map/smooth/pallas_call | solution.py:28
  (30 shorter events, 0.5 us)
Async XLA Ops:
  3.1 8.3 %collective-permute-start = (f32[2,8,16,256]{3,2,1,0:T(8,128)}, f32[2,8,16,256]{3,2,1,0:T(8,128)S(1)}, u32[]{:S(2)}, u32[]{:S(2)}) collective-permute-start(f32[2,8,16,256]{3,2,1,0:T(8,128)} %get-tuple-element.24), channel_id=1, source_target_pairs={{0,4},{1,5},{2,6},{3,7},{4,8},{5,9},{6,10},{7,11},{8,12},{9,13},{1... | collective-permute-start | bytes 786440 | tf_op jit(solution)/shard_map/ppermute | solution.py:61
  3.6 8.9 %collective-permute-start.1 = (f32[2,8,16,256]{3,2,1,0:T(8,128)}, f32[2,8,16,256]{3,2,1,0:T(8,128)S(1)}, u32[]{:S(2)}, u32[]{:S(2)}) collective-permute-start(f32[2,8,16,256]{3,2,1,0:T(8,128)} %get-tuple-element.25), channel_id=1, source_target_pairs={{0,1},{1,2},{2,3},{3,7},{4,0},{5,4},{6,5},{7,6},{8,9},{9,10},{10,1... | collective-permute-start | bytes 786440 | tf_op jit(solution)/shard_map/ppermute | solution.py:61
  6.2 8.4 %collective-permute-start.2 = (f32[2,8,16,256]{3,2,1,0:T(8,128)}, f32[2,8,16,256]{3,2,1,0:T(8,128)S(1)}, u32[]{:S(2)}, u32[]{:S(2)}) collective-permute-start(f32[2,8,16,256]{3,2,1,0:T(8,128)} %get-tuple-element.26), channel_id=1, source_target_pairs={{1,0},{2,1},{3,2},{7,3},{0,4},{4,5},{5,6},{6,7},{9,8},{10,9},{11,1... | collective-permute-start | bytes 786440 | tf_op jit(solution)/shard_map/ppermute | solution.py:61
  6.3 8.4 %collective-permute-start.3 = (f32[2,8,16,256]{3,2,1,0:T(8,128)S(1)}, f32[2,8,16,256]{3,2,1,0:T(8,128)S(1)}, u32[]{:S(2)}, u32[]{:S(2)}) collective-permute-start(f32[2,8,16,256]{3,2,1,0:T(8,128)S(1)} %get-tuple-element.27), channel_id=1, source_target_pairs={{4,0},{5,1},{6,2},{7,3},{8,4},{9,5},{10,6},{11,7},{12,8},{13,9},{1... | collective-permute-start | bytes 786440 | tf_op jit(solution)/shard_map/ppermute | solution.py:61
  9.4 0.7 %copy-start = (f32[16]{0:T(128)S(1)}, f32[16]{0:T(128)}, u32[]{:S(2)}) copy-start(f32[16]{0:T(128)} %courant_ref.7) | copy-start | bytes 196
  15.7 5.3 %collective-permute-start.4 = (f32[8,16,256]{2,1,0:T(8,128)S(1)}, f32[8,16,256]{2,1,0:T(8,128)S(1)}, u32[]{:S(2)}, u32[]{:S(2)}) collective-permute-start(f32[8,16,256]{2,1,0:T(8,128)S(1)} %get-tuple-element.30), channel_id=1, source_target_pairs={{0,4},{1,5},{2,6},{3,7},{4,8},{5,9},{6,10},{7,11},{8,12},{9,13},{1... | collective-permute-start | bytes 393224 | tf_op jit(solution)/shard_map/ppermute | solution.py:61
  15.8 5.3 %collective-permute-start.5 = (f32[8,16,256]{2,1,0:T(8,128)S(1)}, f32[8,16,256]{2,1,0:T(8,128)S(1)}, u32[]{:S(2)}, u32[]{:S(2)}) collective-permute-start(f32[8,16,256]{2,1,0:T(8,128)S(1)} %get-tuple-element.31), channel_id=1, source_target_pairs={{0,1},{1,2},{2,3},{3,7},{4,0},{5,4},{6,5},{7,6},{8,9},{9,10},{10,1... | collective-permute-start | bytes 393224 | tf_op jit(solution)/shard_map/ppermute | solution.py:61
  17.4 2.5 %copy-start.4 = (f32[32]{0:T(128)S(1)}, f32[32]{0:T(128)}, u32[]{:S(2)}) copy-start(f32[32]{0:T(128)} %param.17) | copy-start | bytes 388
  17.4 5.4 %collective-permute-start.6 = (f32[8,16,256]{2,1,0:T(8,128)S(1)}, f32[8,16,256]{2,1,0:T(8,128)S(1)}, u32[]{:S(2)}, u32[]{:S(2)}) collective-permute-start(f32[8,16,256]{2,1,0:T(8,128)S(1)} %get-tuple-element.32), channel_id=1, source_target_pairs={{1,0},{2,1},{3,2},{7,3},{0,4},{4,5},{5,6},{6,7},{9,8},{10,9},{11,1... | collective-permute-start | bytes 393224 | tf_op jit(solution)/shard_map/ppermute | solution.py:61
  17.4 5.4 %collective-permute-start.7 = (f32[8,16,256]{2,1,0:T(8,128)S(1)}, f32[8,16,256]{2,1,0:T(8,128)S(1)}, u32[]{:S(2)}, u32[]{:S(2)}) collective-permute-start(f32[8,16,256]{2,1,0:T(8,128)S(1)} %get-tuple-element.33), channel_id=1, source_target_pairs={{4,0},{5,1},{6,2},{7,3},{8,4},{9,5},{10,6},{11,7},{12,8},{13,9},{1... | collective-permute-start | bytes 393224 | tf_op jit(solution)/shard_map/ppermute | solution.py:61
  19.9 2.9 %copy-start.1 = (s32[32]{0:T(128)S(1)}, s32[32]{0:T(128)}, u32[]{:S(2)}) copy-start(s32[32]{0:T(128)} %cells_ref.1) | copy-start | bytes 388
  19.9 2.9 %copy-start.2 = (f32[32]{0:T(128)S(1)}, f32[32]{0:T(128)}, u32[]{:S(2)}) copy-start(f32[32]{0:T(128)} %reading_ref.1) | copy-start | bytes 388
  24.0 4.9 %copy-start.3 = (s32[256]{0:T(256)S(1)}, s32[256]{0:T(256)}, u32[]{:S(2)}) copy-start(s32[256]{0:T(256)} %param.18) | copy-start | bytes 3076
  24.0 5.3 %collective-permute-start.10 = (f32[32,256]{1,0:T(8,128)S(1)}, f32[32,256]{1,0:T(8,128)S(1)}, u32[]{:S(2)}, u32[]{:S(2)}) collective-permute-start(f32[32,256]{1,0:T(8,128)S(1)} %get-tuple-element.34.refs_0_), channel_id=1, source_target_pairs={{0,3},{1,2},{2,5},{3,4},{4,7},{5,6},{6,1},{7,0},{8,11},{9,10},{10,... | collective-permute-start | bytes 98312 | tf_op jit(solution)/shard_map/ppermute | solution.py:301
  26.0 4.9 %collective-permute-start.8 = (f32[32,256]{1,0:T(8,128)S(1)}, f32[32,256]{1,0:T(8,128)S(1)}, u32[]{:S(2)}, u32[]{:S(2)}) collective-permute-start(f32[32,256]{1,0:T(8,128)S(1)} %get-tuple-element.34.refs_0_), channel_id=1, source_target_pairs={{0,1},{1,3},{2,0},{3,2},{4,5},{5,7},{6,4},{7,6},{8,9},{9,11},{10,8... | collective-permute-start | bytes 98312 | tf_op jit(solution)/shard_map/ppermute | solution.py:301
  27.2 4.1 %collective-permute-start.9 = (f32[32,256]{1,0:T(8,128)S(1)}, f32[32,256]{1,0:T(8,128)S(1)}, u32[]{:S(2)}, u32[]{:S(2)}) collective-permute-start(f32[32,256]{1,0:T(8,128)S(1)} %get-tuple-element.34.refs_0_), channel_id=1, source_target_pairs={{1,0},{3,1},{0,2},{2,3},{5,4},{7,5},{4,6},{6,7},{9,8},{11,9},{8,10... | collective-permute-start | bytes 98312 | tf_op jit(solution)/shard_map/ppermute | solution.py:301
  31.3 5.9 %collective-permute-start.12 = (f32[128,256]{1,0:T(8,128)S(1)}, f32[128,256]{1,0:T(8,128)S(1)}, u32[]{:S(2)}, u32[]{:S(2)}) collective-permute-start(f32[128,256]{1,0:T(8,128)S(1)} %pack.1.refs_0_), channel_id=1, source_target_pairs={{0,8},{1,9},{2,10},{3,11},{4,12},{5,13},{6,14},{7,15},{8,24},{9,25... | collective-permute-start | bytes 393224 | tf_op jit(solution)/shard_map/ppermute | solution.py:301
  33.4 6.4 %collective-permute-start.14 = (f32[128,256]{1,0:T(8,128)S(1)}, f32[128,256]{1,0:T(8,128)S(1)}, u32[]{:S(2)}, u32[]{:S(2)}) collective-permute-start(f32[128,256]{1,0:T(8,128)S(1)} %pack.1.refs_0_), channel_id=1, source_target_pairs={{8,0},{9,1},{10,2},{11,3},{12,4},{13,5},{14,6},{15,7},{24,8},{25,9... | collective-permute-start | bytes 393224 | tf_op jit(solution)/shard_map/ppermute | solution.py:301
  33.4 6.7 %collective-permute-start.16 = (f32[128,256]{1,0:T(8,128)S(1)}, f32[128,256]{1,0:T(8,128)S(1)}, u32[]{:S(2)}, u32[]{:S(2)}) collective-permute-start(f32[128,256]{1,0:T(8,128)S(1)} %pack.1.refs_0_), channel_id=1, source_target_pairs={{0,24},{1,25},{2,26},{3,27},{4,28},{5,29},{6,30},{7,31},{8,16},{9,... | collective-permute-start | bytes 393224 | tf_op jit(solution)/shard_map/ppermute | solution.py:301
  36.5 4.6 %collective-permute-start.11 = (f32[128,256]{1,0:T(8,128)S(1)}, f32[128,256]{1,0:T(8,128)S(1)}, u32[]{:S(2)}, u32[]{:S(2)}) collective-permute-start(f32[128,256]{1,0:T(8,128)S(1)} %pack.1.refs_0_), channel_id=1, source_target_pairs={{0,4},{1,5},{2,6},{3,7},{4,0},{5,1},{6,2},{7,3},{8,12},{9,13},{10,... | collective-permute-start | bytes 393224 | tf_op jit(solution)/shard_map/ppermute | solution.py:301
  37.3 3.8 %collective-permute-start.13 = (f32[128,256]{1,0:T(8,128)S(1)}, f32[128,256]{1,0:T(8,128)S(1)}, u32[]{:S(2)}, u32[]{:S(2)}) collective-permute-start(f32[128,256]{1,0:T(8,128)S(1)} %collective-permute-done.12.refs_1_), channel_id=1, source_target_pairs={{0,4},{1,5},{2,6},{3,7},{4,0},{5,1},{6,2},{7,3},{8,12},{9,13},{10,... | collective-permute-start | bytes 393224 | tf_op jit(solution)/shard_map/ppermute | solution.py:301
  39.8 1.3 %collective-permute-start.15 = (f32[128,256]{1,0:T(8,128)S(1)}, f32[128,256]{1,0:T(8,128)S(1)}, u32[]{:S(2)}, u32[]{:S(2)}) collective-permute-start(f32[128,256]{1,0:T(8,128)S(1)} %collective-permute-done.14.refs_2_), channel_id=1, source_target_pairs={{0,4},{1,5},{2,6},{3,7},{4,0},{5,1},{6,2},{7,3},{8,12},{9,13},{10,... | collective-permute-start | bytes 393224 | tf_op jit(solution)/shard_map/ppermute | solution.py:301
  40.1 1.3 %collective-permute-start.17 = (f32[128,256]{1,0:T(8,128)S(1)}, f32[128,256]{1,0:T(8,128)S(1)}, u32[]{:S(2)}, u32[]{:S(2)}) collective-permute-start(f32[128,256]{1,0:T(8,128)S(1)} %collective-permute-done.16.refs_3_), channel_id=1, source_target_pairs={{0,4},{1,5},{2,6},{3,7},{4,0},{5,1},{6,2},{7,3},{8,12},{9,13},{10,... | collective-permute-start | bytes 393224 | tf_op jit(solution)/shard_map/ppermute | solution.py:301

commit v8 on v7

--- a/solution.py
+++ b/solution.py
@@ -377,12 +377,18 @@
     members = scaled.shape[1]
     spread = scaled - jnp.sum(scaled, axis=1, keepdims=True) * (1.0 / members)
     misfit = noise_ref[...] - scale * scaled
-    return product(spread, jnp.concatenate([spread, misfit], axis=1), 0, 0, THREE_PASS)
+    half = members // 2
+    right = jnp.concatenate([spread, misfit], axis=1)
+    upper = product(spread[:, :half], right, 0, 0, THREE_PASS)
+    lower = product(spread[:, half:], right[:, half:], 0, 0, THREE_PASS)
+    return upper, lower
 
 
 def partial_products(scale, *refs):
     *piece_refs, noise_ref, sums_ref = refs
-    sums_ref[...] = products(scale, piece_refs, noise_ref)
+    half = sums_ref.shape[0] // 2
+    sums_ref[half:, :half] = jnp.zeros((half, half), jnp.float32)
+    sums_ref[:half], sums_ref[half:, half:] = products(scale, piece_refs, noise_ref)
 
 
 def update(scale, sums_ref, log_ref, updated_hbm, weights_ref, held_ref, sems):
@@ -423,7 +429,10 @@
     sums_ref, weights_ref, held_ref, sems, final_sem = refs[-5:]
     keep = pltpu.make_async_copy(inner_ref, final_hbm, final_sem)
     keep.start()
-    sums_ref[...] = near_ref[...] + products(scale, piece_refs, noise_ref)
+    half = sums_ref.shape[0] // 2
+    upper, lower = products(scale, piece_refs, noise_ref)
+    sums_ref[:half] = near_ref[:half] + upper
+    sums_ref[half:, half:] = near_ref[half:, half:] + lower
     update(scale, sums_ref, log_ref, updated_hbm, weights_ref, held_ref, sems)
     keep.wait()
 

time: 51.2 us -> 51.3 us (level)
  no operation moved by 1% of the time
where the time goes in v8:
time: 51.3 us; the launch traced here: 51 us
  starting transfers between devices  19.1 us (37%)
  Pallas kernels  17.3 us (34%)
  waiting for transfers between devices  11.3 us (22%)
  other arithmetic  1.56 us (3%)
  between operations  0.94 us (2%)
  local copies, waits for them, and re-layouts  0.82 us (2%)
    pallas_call x8, Pallas kernels, call(): pl.pallas_call(kernel, out_shape=outs, in_specs=specs, out_specs=jax.tree...  17.3 us
    ppermute x8, starting transfers between devices, exchange(): lax.ppermute(face, ('gx', 'gy'), route)  9.6 us
    ppermute x10, starting transfers between devices, send(): return lax.ppermute(block, ('gx', 'gy'), route)  9.52 us
    ppermute x10, waiting for transfers between devices, send(): return lax.ppermute(block, ('gx', 'gy'), route)  6.3 us
    ppermute x8, waiting for transfers between devices, exchange(): lax.ppermute(face, ('gx', 'gy'), route)  4.97 us
  transfers between devices with their start and end apart: 18, of which 10 were waited for; matrix products, arithmetic and copies ran while one was open for 3% of the time, Pallas kernels for 6%

profile of v8, /device:TPU:0, one launch (start us, length us, event | category | flops | bytes accessed | tf_op | source)
XLA Modules:
  0.0 51.0 jit_solution(17513241876229637220)
XLA Ops:
  0.6 2.5 %prepare.1 = (f32[64,16,256]{2,1,0:T(8,128)S(1)}, f32[64,16,256]{2,1,0:T(8,128)S(1)}, f32[16,128]{1,0:T(8,128)S(1)}, f32[2,8,16,256]{3,2,1,0:T(8,128)}, f32[2,8,...) custom-call(f32[64,16,256]{2,1,0:T(8,128)} %bitcast.8, f32[64,16,256]{2,1,0:T(8,128)} %bitcast.9, ...), custom_call_target="tpu_custom_call" | custom-call | bytes 2101280 | tf_op jit(solution)/shard_map/prepare/pallas_call | solution.py:28
  3.1 0.5 collective-permute-start
  3.6 2.6 %collective-permute-start.1 = (f32[2,8,16,256]{3,2,1,0:T(8,128)}, f32[2,8,16,256]{3,2,1,0:T(8,128)S(1)}, u32[]{:S(2)}, u32[]{:S(2)}) collective-permute-start(f32[2,8,16,256]{3,2,1,0:T(8,128)} %get-tuple-element.25), channel_id=1, source_target_pairs={{0,1},{1,2},{2,3},{3,7},{4,0},{5,4},{6,5},{7,6},{8,9},{9,10},{10,1... | collective-permute-start | bytes 786440 | tf_op jit(solution)/shard_map/ppermute | solution.py:61
  6.3 2.3 %collective-permute-start.3 = (f32[2,8,16,256]{3,2,1,0:T(8,128)S(1)}, f32[2,8,16,256]{3,2,1,0:T(8,128)S(1)}, u32[]{:S(2)}, u32[]{:S(2)}) collective-permute-start(f32[2,8,16,256]{3,2,1,0:T(8,128)S(1)} %get-tuple-element.27), channel_id=1, source_target_pairs={{4,0},{5,1},{6,2},{7,3},{8,4},{9,5},{10,6},{11,7},{12,8},{13,9},{1... | collective-permute-start | bytes 786440 | tf_op jit(solution)/shard_map/ppermute | solution.py:61
  8.6 0.7 %multiply_bitcast_fusion = s32[32]{0:T(128)S(1)} fusion(s32[32,32]{1,0:T(8,128)} %constant.73.clone, s32[]{:T(128)S(6)} %select_n.42), kind=kLoop, calls=%fused_computation.11 | loop fusion | flops 32 | bytes 260 | tf_op jit(solution)/shard_map/mul | solution.py:556
  9.3 0.1 multiply_remainder_fusion
  9.4 0.7 %copy-done = f32[16]{0:T(128)S(1)} copy-done((f32[16]{0:T(128)S(1)}, f32[16]{0:T(128)}, u32[]{:S(2)}) %copy-start) | copy-done | bytes 88
  10.1 1.3 %middle_inside.1 = (f32[64,16,256]{2,1,0:T(8,128)S(1)}, f32[64,16,256]{2,1,0:T(8,128)S(1)}) custom-call(f32[16]{0:T(128)S(1)} %copy-done, f32[64,16,256]{2,1,0:T(8,128)S(1)} %get-tuple-element.20.t_ref, f32[64,16,256]{2,1,0:T(8,128)S(1)} %get-tuple-element.21.log_ref, f32[16,128]{1,0:T(8,128)S(1)} %get-tuple-element.22.columns_ref), custom_call_target="tpu_custom_call" | custom-call | flops 10000000 | bytes 2105408 | tf_op jit(solution)/shard_map/middle_inside/pallas_call | solution.py:28
  11.5 1.1 %collective-permute-done.1.rest_1_.rest_5_ = f32[2,8,16,256]{3,2,1,0:T(8,128)S(1)} collective-permute-done((f32[2,8,16,256]{3,2,1,0:T(8,128)}, f32[2,8,16,256]{3,2,1,0:T(8,128)S(1)}, u32[]{:S(2)}, u32[]{:S(2)}) %collective-permute-start.1) | collective-permute-done | bytes 262176 | tf_op jit(solution)/shard_map/ppermute | solution.py:61
  12.5 2.2 %collective-permute-done.2.rest_2_.rest_6_ = f32[2,8,16,256]{3,2,1,0:T(8,128)S(1)} collective-permute-done((f32[2,8,16,256]{3,2,1,0:T(8,128)}, f32[2,8,16,256]{3,2,1,0:T(8,128)S(1)}, u32[]{:S(2)}, u32[]{:S(2)}) %collective-permute-start.2) | collective-permute-done | bytes 262176 | tf_op jit(solution)/shard_map/ppermute | solution.py:61
  14.7 1.0 %middle_border.1 = (f32[64,16,256]{2,1,0:T(8,128)S(1)}, f32[8,16,256]{2,1,0:T(8,128)S(1)}, f32[8,16,256]{2,1,0:T(8,128)S(1)}, f32[8,16,256]{2,1,0:T(8,128)S(1)}, f32[8,16,256]{2,1,0:T(8,128)S(1)}) custom-call(f32[16]{0:T(128)S(1)} %copy-done, f32[64,16,256]{2,1,0:T(8,128)S(1)} %get-tuple-element.20.t_ref, ...), custom_call_target="tpu_custom_call", output_to_operand_aliasing={{0}: (7, {})} | custom-call | flops 10000000 | bytes 4194368 | tf_op jit(solution)/shard_map/middle_border/pallas_call | solution.py:28
  15.8 1.6 %collective-permute-start.5 = (f32[8,16,256]{2,1,0:T(8,128)S(1)}, f32[8,16,256]{2,1,0:T(8,128)S(1)}, u32[]{:S(2)}, u32[]{:S(2)}) collective-permute-start(f32[8,16,256]{2,1,0:T(8,128)S(1)} %get-tuple-element.31), channel_id=1, source_target_pairs={{0,1},{1,2},{2,3},{3,7},{4,0},{5,4},{6,5},{7,6},{8,9},{9,10},{10,1... | collective-permute-start | bytes 393224 | tf_op jit(solution)/shard_map/ppermute | solution.py:61
  17.4 2.5 %collective-permute-start.7 = (f32[8,16,256]{2,1,0:T(8,128)S(1)}, f32[8,16,256]{2,1,0:T(8,128)S(1)}, u32[]{:S(2)}, u32[]{:S(2)}) collective-permute-start(f32[8,16,256]{2,1,0:T(8,128)S(1)} %get-tuple-element.33), channel_id=1, source_target_pairs={{4,0},{5,1},{6,2},{7,3},{8,4},{9,5},{10,6},{11,7},{12,8},{13,9},{1... | collective-permute-start | bytes 393224 | tf_op jit(solution)/shard_map/ppermute | solution.py:61
  19.9 1.1 %final_inside.1.rest_8_ = f32[64,16,256]{2,1,0:T(8,128)S(1)} custom-call(f32[16]{0:T(128)S(1)} %copy-done, f32[64,16,256]{2,1,0:T(8,128)S(1)} %get-tuple-element.29.u_ref, f32[64,16,256]{2,1,0:T(8,128)S(1)} %get-tuple-element.23.h_ref), custom_call_target="tpu_custom_call" | custom-call | flops 10000000 | bytes 2097216 | tf_op jit(solution)/shard_map/final_inside/pallas_call | solution.py:28
  21.1 1.7 %collective-permute-done.6.rest_2_ = f32[8,16,256]{2,1,0:T(8,128)S(1)} collective-permute-done((f32[8,16,256]{2,1,0:T(8,128)S(1)}, f32[8,16,256]{2,1,0:T(8,128)S(1)}, u32[]{:S(2)}, u32[]{:S(2)}) %collective-permute-start.6) | collective-permute-done | bytes 131104 | tf_op jit(solution)/shard_map/ppermute | solution.py:61
  22.8 1.2 %observe.1 = (f32[64,16,256]{2,1,0:T(8,128)S(1)}, f32[32,256]{1,0:T(8,128)S(1)}) custom-call(f32[16]{0:T(128)S(1)} %copy-done, s32[32]{0:T(128)S(1)} %copy-done.1, f32[32]{0:T(128)S(1)} %copy-done.2, f32[32]{0:T(128)S(1)} %multiply_divide_fusion.factor_ref, f32[64,16,256]{2,1,0:T(8,128)S(1)} %get-tuple-element.29.u_ref, ...), custom_call_target="tpu_custom_call", output_to_operand_aliasing={{0}: (14, {})} | custom-call | flops 10000000 | bytes 4719040 | tf_op jit(solution)/shard_map/observe/pallas_call | solution.py:28
  24.0 2.0 %collective-permute-start.10 = (f32[32,256]{1,0:T(8,128)S(1)}, f32[32,256]{1,0:T(8,128)S(1)}, u32[]{:S(2)}, u32[]{:S(2)}) collective-permute-start(f32[32,256]{1,0:T(8,128)S(1)} %get-tuple-element.34.refs_0_), channel_id=1, source_target_pairs={{0,3},{1,2},{2,5},{3,4},{4,7},{5,6},{6,1},{7,0},{8,11},{9,10},{10,... | collective-permute-start | bytes 98312 | tf_op jit(solution)/shard_map/ppermute | solution.py:301
  26.0 1.2 %collective-permute-start.8 = (f32[32,256]{1,0:T(8,128)S(1)}, f32[32,256]{1,0:T(8,128)S(1)}, u32[]{:S(2)}, u32[]{:S(2)}) collective-permute-start(f32[32,256]{1,0:T(8,128)S(1)} %get-tuple-element.34.refs_0_), channel_id=1, source_target_pairs={{0,1},{1,3},{2,0},{3,2},{4,5},{5,7},{6,4},{7,6},{8,9},{9,11},{10,8... | collective-permute-start | bytes 98312 | tf_op jit(solution)/shard_map/ppermute | solution.py:301
  27.2 1.7 %collective-permute-start.9 = (f32[32,256]{1,0:T(8,128)S(1)}, f32[32,256]{1,0:T(8,128)S(1)}, u32[]{:S(2)}, u32[]{:S(2)}) collective-permute-start(f32[32,256]{1,0:T(8,128)S(1)} %get-tuple-element.34.refs_0_), channel_id=1, source_target_pairs={{1,0},{3,1},{0,2},{2,3},{5,4},{7,5},{4,6},{6,7},{9,8},{11,9},{8,10... | collective-permute-start | bytes 98312 | tf_op jit(solution)/shard_map/ppermute | solution.py:301
  28.9 0.4 collective-permute-done.10.refs_3_
  29.3 1.5 %collective-permute-done.8.refs_1_ = f32[32,256]{1,0:T(8,128)S(1)} collective-permute-done((f32[32,256]{1,0:T(8,128)S(1)}, f32[32,256]{1,0:T(8,128)S(1)}, u32[]{:S(2)}, u32[]{:S(2)}) %collective-permute-start.8) | collective-permute-done | bytes 32800 | tf_op jit(solution)/shard_map/ppermute | solution.py:301
  30.8 0.5 collective-permute-done.9.refs_2_
  31.3 2.1 %collective-permute-start.12 = (f32[128,256]{1,0:T(8,128)S(1)}, f32[128,256]{1,0:T(8,128)S(1)}, u32[]{:S(2)}, u32[]{:S(2)}) collective-permute-start(f32[128,256]{1,0:T(8,128)S(1)} %pack.1.refs_0_), channel_id=1, source_target_pairs={{0,8},{1,9},{2,10},{3,11},{4,12},{5,13},{6,14},{7,15},{8,24},{9,25... | collective-permute-start | bytes 393224 | tf_op jit(solution)/shard_map/ppermute | solution.py:301
  33.4 2.3 %collective-permute-start.16 = (f32[128,256]{1,0:T(8,128)S(1)}, f32[128,256]{1,0:T(8,128)S(1)}, u32[]{:S(2)}, u32[]{:S(2)}) collective-permute-start(f32[128,256]{1,0:T(8,128)S(1)} %pack.1.refs_0_), channel_id=1, source_target_pairs={{0,24},{1,25},{2,26},{3,27},{4,28},{5,29},{6,30},{7,31},{8,16},{9,... | collective-permute-start | bytes 393224 | tf_op jit(solution)/shard_map/ppermute | solution.py:301
  35.7 0.7 %fusion.4 = f32[1024,256]{1,0:T(8,128)S(1)} fusion(s32[1024]{0:T(1024)S(1)} %get-tuple-element.41, s32[1024]{0:T(1024)S(1)} %get-tuple-element.40, s32[256]{0:T(256)S(1)} %and_select_fusion), kind=kLoop, calls=%fused_computation.6 | loop fusion | flops 4980736 | bytes 1057792 | tf_op jit(solution)/shard_map/mul | solution.py:558
  36.5 0.7 %collective-permute-done.12.refs_1_ = f32[128,256]{1,0:T(8,128)S(1)} collective-permute-done((f32[128,256]{1,0:T(8,128)S(1)}, f32[128,256]{1,0:T(8,128)S(1)}, u32[]{:S(2)}, u32[]{:S(2)}) %collective-permute-start.12) | collective-permute-done | bytes 131104 | tf_op jit(solution)/shard_map/ppermute | solution.py:301
  37.3 2.5 %collective-permute-done.14.refs_2_ = f32[128,256]{1,0:T(8,128)S(1)} collective-permute-done((f32[128,256]{1,0:T(8,128)S(1)}, f32[128,256]{1,0:T(8,128)S(1)}, u32[]{:S(2)}, u32[]{:S(2)}) %collective-permute-start.14) | collective-permute-done | bytes 131104 | tf_op jit(solution)/shard_map/ppermute | solution.py:301
  39.8 0.3 collective-permute-done.16.refs_3_
  40.1 0.2 collective-permute-start.17
  40.4 0.8 %partial_products.1.refs_5_ = f32[256,512]{1,0:T(8,128)S(1)} custom-call(f32[128,256]{1,0:T(8,128)S(1)} %pack.1.refs_0_, f32[128,256]{1,0:T(8,128)S(1)} %collective-permute-done.12.refs_1_, f32[128,256]{1,0:T(8,128)S(1)} %collective-permute-done.14.refs_2_, f32[128,256]{1,0:T(8,128)S(1)} %collective-permute-done.16.refs_3_, ...), custom_call_target="tpu_custom_call" | custom-call | flops 100000000 | bytes 1048576 | tf_op jit(solution)/shard_map/partial_products/pallas_call | solution.py:28
  41.2 0.3 collective-permute-done.17.refs_3_
  41.5 9.4 %smooth.1 = (f32[1024,256]{1,0:T(8,128)}, f32[64,16,256]{2,1,0:T(8,128)}) custom-call(f32[128,256]{1,0:T(8,128)S(1)} %collective-permute-done.11.refs_0_, f32[128,256]{1,0:T(8,128)S(1)} %collective-permute-done.13.refs_1_, f32[128,256]{1,0:T(8,128)S(1)} %collective-permute-done.15.refs_2_, f32[128,256]{1,0:T(8,128)S(1)} %collective-permute-done.17.refs_3_, ...), custom_call_target="tpu_custom_call" | custom-call | flops 1000000000 | bytes 3670016 | tf_op jit(solution)/shard_map/smooth/pallas_call | solution.py:28
  (30 shorter events, 0.4 us)
Async XLA Ops:
  3.1 8.3 %collective-permute-start = (f32[2,8,16,256]{3,2,1,0:T(8,128)}, f32[2,8,16,256]{3,2,1,0:T(8,128)S(1)}, u32[]{:S(2)}, u32[]{:S(2)}) collective-permute-start(f32[2,8,16,256]{3,2,1,0:T(8,128)} %get-tuple-element.24), channel_id=1, source_target_pairs={{0,4},{1,5},{2,6},{3,7},{4,8},{5,9},{6,10},{7,11},{8,12},{9,13},{1... | collective-permute-start | bytes 786440 | tf_op jit(solution)/shard_map/ppermute | solution.py:61
  3.6 8.9 %collective-permute-start.1 = (f32[2,8,16,256]{3,2,1,0:T(8,128)}, f32[2,8,16,256]{3,2,1,0:T(8,128)S(1)}, u32[]{:S(2)}, u32[]{:S(2)}) collective-permute-start(f32[2,8,16,256]{3,2,1,0:T(8,128)} %get-tuple-element.25), channel_id=1, source_target_pairs={{0,1},{1,2},{2,3},{3,7},{4,0},{5,4},{6,5},{7,6},{8,9},{9,10},{10,1... | collective-permute-start | bytes 786440 | tf_op jit(solution)/shard_map/ppermute | solution.py:61
  6.2 8.4 %collective-permute-start.2 = (f32[2,8,16,256]{3,2,1,0:T(8,128)}, f32[2,8,16,256]{3,2,1,0:T(8,128)S(1)}, u32[]{:S(2)}, u32[]{:S(2)}) collective-permute-start(f32[2,8,16,256]{3,2,1,0:T(8,128)} %get-tuple-element.26), channel_id=1, source_target_pairs={{1,0},{2,1},{3,2},{7,3},{0,4},{4,5},{5,6},{6,7},{9,8},{10,9},{11,1... | collective-permute-start | bytes 786440 | tf_op jit(solution)/shard_map/ppermute | solution.py:61
  6.3 8.4 %collective-permute-start.3 = (f32[2,8,16,256]{3,2,1,0:T(8,128)S(1)}, f32[2,8,16,256]{3,2,1,0:T(8,128)S(1)}, u32[]{:S(2)}, u32[]{:S(2)}) collective-permute-start(f32[2,8,16,256]{3,2,1,0:T(8,128)S(1)} %get-tuple-element.27), channel_id=1, source_target_pairs={{4,0},{5,1},{6,2},{7,3},{8,4},{9,5},{10,6},{11,7},{12,8},{13,9},{1... | collective-permute-start | bytes 786440 | tf_op jit(solution)/shard_map/ppermute | solution.py:61
  9.4 0.7 %copy-start = (f32[16]{0:T(128)S(1)}, f32[16]{0:T(128)}, u32[]{:S(2)}) copy-start(f32[16]{0:T(128)} %courant_ref.7) | copy-start | bytes 196
  15.7 5.3 %collective-permute-start.4 = (f32[8,16,256]{2,1,0:T(8,128)S(1)}, f32[8,16,256]{2,1,0:T(8,128)S(1)}, u32[]{:S(2)}, u32[]{:S(2)}) collective-permute-start(f32[8,16,256]{2,1,0:T(8,128)S(1)} %get-tuple-element.30), channel_id=1, source_target_pairs={{0,4},{1,5},{2,6},{3,7},{4,8},{5,9},{6,10},{7,11},{8,12},{9,13},{1... | collective-permute-start | bytes 393224 | tf_op jit(solution)/shard_map/ppermute | solution.py:61
  15.8 5.3 %collective-permute-start.5 = (f32[8,16,256]{2,1,0:T(8,128)S(1)}, f32[8,16,256]{2,1,0:T(8,128)S(1)}, u32[]{:S(2)}, u32[]{:S(2)}) collective-permute-start(f32[8,16,256]{2,1,0:T(8,128)S(1)} %get-tuple-element.31), channel_id=1, source_target_pairs={{0,1},{1,2},{2,3},{3,7},{4,0},{5,4},{6,5},{7,6},{8,9},{9,10},{10,1... | collective-permute-start | bytes 393224 | tf_op jit(solution)/shard_map/ppermute | solution.py:61
  17.4 2.5 %copy-start.4 = (f32[32]{0:T(128)S(1)}, f32[32]{0:T(128)}, u32[]{:S(2)}) copy-start(f32[32]{0:T(128)} %param.17) | copy-start | bytes 388
  17.4 5.4 %collective-permute-start.6 = (f32[8,16,256]{2,1,0:T(8,128)S(1)}, f32[8,16,256]{2,1,0:T(8,128)S(1)}, u32[]{:S(2)}, u32[]{:S(2)}) collective-permute-start(f32[8,16,256]{2,1,0:T(8,128)S(1)} %get-tuple-element.32), channel_id=1, source_target_pairs={{1,0},{2,1},{3,2},{7,3},{0,4},{4,5},{5,6},{6,7},{9,8},{10,9},{11,1... | collective-permute-start | bytes 393224 | tf_op jit(solution)/shard_map/ppermute | solution.py:61
  17.4 5.4 %collective-permute-start.7 = (f32[8,16,256]{2,1,0:T(8,128)S(1)}, f32[8,16,256]{2,1,0:T(8,128)S(1)}, u32[]{:S(2)}, u32[]{:S(2)}) collective-permute-start(f32[8,16,256]{2,1,0:T(8,128)S(1)} %get-tuple-element.33), channel_id=1, source_target_pairs={{4,0},{5,1},{6,2},{7,3},{8,4},{9,5},{10,6},{11,7},{12,8},{13,9},{1... | collective-permute-start | bytes 393224 | tf_op jit(solution)/shard_map/ppermute | solution.py:61
  19.9 2.9 %copy-start.1 = (s32[32]{0:T(128)S(1)}, s32[32]{0:T(128)}, u32[]{:S(2)}) copy-start(s32[32]{0:T(128)} %cells_ref.1) | copy-start | bytes 388
  19.9 2.9 %copy-start.2 = (f32[32]{0:T(128)S(1)}, f32[32]{0:T(128)}, u32[]{:S(2)}) copy-start(f32[32]{0:T(128)} %reading_ref.1) | copy-start | bytes 388
  24.0 4.9 %copy-start.3 = (s32[256]{0:T(256)S(1)}, s32[256]{0:T(256)}, u32[]{:S(2)}) copy-start(s32[256]{0:T(256)} %param.18) | copy-start | bytes 3076
  24.0 5.3 %collective-permute-start.10 = (f32[32,256]{1,0:T(8,128)S(1)}, f32[32,256]{1,0:T(8,128)S(1)}, u32[]{:S(2)}, u32[]{:S(2)}) collective-permute-start(f32[32,256]{1,0:T(8,128)S(1)} %get-tuple-element.34.refs_0_), channel_id=1, source_target_pairs={{0,3},{1,2},{2,5},{3,4},{4,7},{5,6},{6,1},{7,0},{8,11},{9,10},{10,... | collective-permute-start | bytes 98312 | tf_op jit(solution)/shard_map/ppermute | solution.py:301
  26.0 4.9 %collective-permute-start.8 = (f32[32,256]{1,0:T(8,128)S(1)}, f32[32,256]{1,0:T(8,128)S(1)}, u32[]{:S(2)}, u32[]{:S(2)}) collective-permute-start(f32[32,256]{1,0:T(8,128)S(1)} %get-tuple-element.34.refs_0_), channel_id=1, source_target_pairs={{0,1},{1,3},{2,0},{3,2},{4,5},{5,7},{6,4},{7,6},{8,9},{9,11},{10,8... | collective-permute-start | bytes 98312 | tf_op jit(solution)/shard_map/ppermute | solution.py:301
  27.2 4.1 %collective-permute-start.9 = (f32[32,256]{1,0:T(8,128)S(1)}, f32[32,256]{1,0:T(8,128)S(1)}, u32[]{:S(2)}, u32[]{:S(2)}) collective-permute-start(f32[32,256]{1,0:T(8,128)S(1)} %get-tuple-element.34.refs_0_), channel_id=1, source_target_pairs={{1,0},{3,1},{0,2},{2,3},{5,4},{7,5},{4,6},{6,7},{9,8},{11,9},{8,10... | collective-permute-start | bytes 98312 | tf_op jit(solution)/shard_map/ppermute | solution.py:301
  31.3 5.9 %collective-permute-start.12 = (f32[128,256]{1,0:T(8,128)S(1)}, f32[128,256]{1,0:T(8,128)S(1)}, u32[]{:S(2)}, u32[]{:S(2)}) collective-permute-start(f32[128,256]{1,0:T(8,128)S(1)} %pack.1.refs_0_), channel_id=1, source_target_pairs={{0,8},{1,9},{2,10},{3,11},{4,12},{5,13},{6,14},{7,15},{8,24},{9,25... | collective-permute-start | bytes 393224 | tf_op jit(solution)/shard_map/ppermute | solution.py:301
  33.4 6.4 %collective-permute-start.14 = (f32[128,256]{1,0:T(8,128)S(1)}, f32[128,256]{1,0:T(8,128)S(1)}, u32[]{:S(2)}, u32[]{:S(2)}) collective-permute-start(f32[128,256]{1,0:T(8,128)S(1)} %pack.1.refs_0_), channel_id=1, source_target_pairs={{8,0},{9,1},{10,2},{11,3},{12,4},{13,5},{14,6},{15,7},{24,8},{25,9... | collective-permute-start | bytes 393224 | tf_op jit(solution)/shard_map/ppermute | solution.py:301
  33.4 6.7 %collective-permute-start.16 = (f32[128,256]{1,0:T(8,128)S(1)}, f32[128,256]{1,0:T(8,128)S(1)}, u32[]{:S(2)}, u32[]{:S(2)}) collective-permute-start(f32[128,256]{1,0:T(8,128)S(1)} %pack.1.refs_0_), channel_id=1, source_target_pairs={{0,24},{1,25},{2,26},{3,27},{4,28},{5,29},{6,30},{7,31},{8,16},{9,... | collective-permute-start | bytes 393224 | tf_op jit(solution)/shard_map/ppermute | solution.py:301
  36.5 4.7 %collective-permute-start.11 = (f32[128,256]{1,0:T(8,128)S(1)}, f32[128,256]{1,0:T(8,128)S(1)}, u32[]{:S(2)}, u32[]{:S(2)}) collective-permute-start(f32[128,256]{1,0:T(8,128)S(1)} %pack.1.refs_0_), channel_id=1, source_target_pairs={{0,4},{1,5},{2,6},{3,7},{4,0},{5,1},{6,2},{7,3},{8,12},{9,13},{10,... | collective-permute-start | bytes 393224 | tf_op jit(solution)/shard_map/ppermute | solution.py:301
  37.3 3.9 %collective-permute-start.13 = (f32[128,256]{1,0:T(8,128)S(1)}, f32[128,256]{1,0:T(8,128)S(1)}, u32[]{:S(2)}, u32[]{:S(2)}) collective-permute-start(f32[128,256]{1,0:T(8,128)S(1)} %collective-permute-done.12.refs_1_), channel_id=1, source_target_pairs={{0,4},{1,5},{2,6},{3,7},{4,0},{5,1},{6,2},{7,3},{8,12},{9,13},{10,... | collective-permute-start | bytes 393224 | tf_op jit(solution)/shard_map/ppermute | solution.py:301
  39.8 1.4 %collective-permute-start.15 = (f32[128,256]{1,0:T(8,128)S(1)}, f32[128,256]{1,0:T(8,128)S(1)}, u32[]{:S(2)}, u32[]{:S(2)}) collective-permute-start(f32[128,256]{1,0:T(8,128)S(1)} %collective-permute-done.14.refs_2_), channel_id=1, source_target_pairs={{0,4},{1,5},{2,6},{3,7},{4,0},{5,1},{6,2},{7,3},{8,12},{9,13},{10,... | collective-permute-start | bytes 393224 | tf_op jit(solution)/shard_map/ppermute | solution.py:301
  40.1 1.3 %collective-permute-start.17 = (f32[128,256]{1,0:T(8,128)S(1)}, f32[128,256]{1,0:T(8,128)S(1)}, u32[]{:S(2)}, u32[]{:S(2)}) collective-permute-start(f32[128,256]{1,0:T(8,128)S(1)} %collective-permute-done.16.refs_3_), channel_id=1, source_target_pairs={{0,4},{1,5},{2,6},{3,7},{4,0},{5,1},{6,2},{7,3},{8,12},{9,13},{10,... | collective-permute-start | bytes 393224 | tf_op jit(solution)/shard_map/ppermute | solution.py:301
